TPU v7x, 32 devices: a whole 2x2x4 slice. The times are simulated.
32 devices in a mesh: groups: 2 (over x), pairs: 8 (over z, y), mp: 2 (over core).
Axes of the slice: x: 2, y: 2, z: 4, core: 2. Of those that a mesh axis runs over, the one named last changes fastest.
Arguments:
- tokens: bfloat16 [64, 196, 768], P(('groups', 'pairs'), None, 'mp'), parts along dimension 0, may hold values from -6 to 6
- gain_query: float32 [768], replicated, may hold values from 0.25 to 1.75
- gain_context: float32 [768], replicated, may hold values from 0.25 to 1.75
- query_weight: bfloat16 [768, 768], replicated, may hold values from -1 to 1
- key_weight: bfloat16 [768, 768], replicated, may hold values from -8 to 8
- value_weight: bfloat16 [768, 768], replicated, may hold values from -0.21875 to 0.21875
- out_weight: bfloat16 [768, 768], replicated, may hold values from -0.21875 to 0.21875
- gain_head: float32 [768], replicated, may hold values from 0.25 to 1.75
- hidden_weight: bfloat16 [768, 1024], replicated, may hold values from -0.21875 to 0.21875
- hidden_bias: float32 [1024], replicated, may hold values from -3 to 3
- point_weight: bfloat16 [4, 1024], replicated, may hold values from -0.1875 to 0.1875
- view_owner: int32 [192, 1], P('groups'), parts along dimension 0, may hold values from 0 to 7; in each aligned block of 12 rows (0 to 11, 12 to 23, ...) at most 2 rows name the same one
- view_local: int32 [192], P('groups'), parts along dimension 0, may hold values from 0 to 3
- pair_count: int32 [16], P('groups'), parts along dimension 0, may hold values from 1 to 6, 24 in all
Outputs:
- joined: float32 [64, 4, 196], P(('groups', 'pairs', 'mp')), parts along dimension 0
There are 2 independent parts, one for each index of `groups`. A program takes and returns all parts, laid end to end along the dimension named above; an argument that names none is the same for every part. Nothing has to cross between parts.
Inputs may be any that keep to these rules, and one draw needn't show every extreme that they name: `view_owner`: among the 12 views of one worker no owner appears more than 2 times, and in every draw some owner appears exactly 2 times. `pair_count`: some worker has exactly 6 pairs in every draw; the counts sum to 24.
All inputs are finite; a program needn't handle non-finite values.
Results may differ from a plain program's by a relative error of at most 0.012.
The roundings to bfloat16 on the way count: a program that leaves them out, or rounds other values in their place, can miss the bound.
Values may be sent and summed in bfloat16 or wider, within the bound.
No kernel may reach another device: no remote copies, remote signals or barrier semaphores. Data moves between devices by JAX's collectives and lax.ppermute only.
A program may use at most 128 MiB of HBM per device.

v0:
```python
import math

import jax
import jax.numpy as jnp
from jax import lax
from jax.sharding import PartitionSpec as P

HEADS = 12


EPS = 1e-06


def norm_rows(rows_in, gain_vec):
    rows_in = rows_in.astype(jnp.float32)
    average = jnp.mean(rows_in, axis=-1, keepdims=True)
    centered = rows_in - average
    variance = jnp.mean(centered * centered, axis=-1, keepdims=True)
    return (centered * lax.rsqrt(variance + EPS) * gain_vec).astype(jnp.bfloat16)


def project(rows_in, weight):
    return jnp.einsum("vtd,de->vte", rows_in, weight, preferred_element_type=jnp.float32)


def attention(queries, key_rows, value_rows, head_count):
    view_count, token_count, feature_width = queries.shape
    head_size = feature_width // head_count
    split_shape = (view_count, token_count, head_count, head_size)
    scores = jnp.einsum(
        "vqhd,vkhd->vhqk",
        queries.reshape(split_shape),
        key_rows.reshape(split_shape),
        preferred_element_type=jnp.float32,
    ) / math.sqrt(head_size)
    row_max = jnp.max(scores, axis=-1, keepdims=True)
    exponent = jnp.exp(scores - row_max)
    attn_probs = (exponent / jnp.sum(exponent, axis=-1, keepdims=True)).astype(jnp.bfloat16)
    blended = jnp.einsum(
        "vhqk,vkhd->vqhd",
        attn_probs,
        value_rows.reshape(split_shape),
        preferred_element_type=jnp.float32,
    )
    return blended.astype(jnp.bfloat16).reshape(view_count, token_count, feature_width)


def point_terms(head_out):
    confidence = 1.0 + jnp.exp(head_out[:, 3:4])
    return jnp.concatenate([head_out[:, :3] * confidence, confidence], axis=1)


def per_device(
    tokens,
    gain_query,
    gain_context,
    query_weight,
    key_weight,
    value_weight,
    out_weight,
    gain_head,
    hidden_weight,
    hidden_bias,
    point_weight,
    view_owner,
    view_local,
    pair_count,
):
    worker_count = lax.axis_size("pairs")
    worker_index = lax.axis_index("pairs")
    core_index = lax.axis_index("mp")
    core_count = lax.axis_size("mp")
    image_count = tokens.shape[0]
    token_count = tokens.shape[1]
    full_width = query_weight.shape[0]
    hidden_width = hidden_weight.shape[1]
    request_count = view_local.shape[0] // worker_count
    slot_count = request_count // 2
    owners = view_owner[:, 0].reshape(worker_count, request_count)
    local_rows = view_local.reshape(worker_count, request_count)
    global_rows = owners * image_count + local_rows
    my_images = global_rows[worker_index]
    shard_rows = lax.all_gather(tokens, "pairs", axis=0, tiled=True)
    row_ids = jnp.arange(shard_rows.shape[0])
    onehot = (my_images[:, None] == row_ids[None, :]).astype(jnp.bfloat16)
    half_views = jnp.einsum(
        "vi,itd->vtd", onehot, shard_rows, preferred_element_type=jnp.float32
    ).astype(jnp.bfloat16)
    full_views = lax.all_gather(half_views, "mp", axis=2, tiled=True)
    pair_total = pair_count[worker_index]
    part_width = full_width // core_count
    hidden_part = hidden_width // core_count
    context_views = full_views.reshape(slot_count, 2, token_count, full_width)[:, ::-1].reshape(
        request_count, token_count, full_width
    )
    query_in = norm_rows(full_views, gain_query)
    context_in = norm_rows(context_views, gain_context)
    query_part = lax.dynamic_slice_in_dim(query_weight, core_index * part_width, part_width, 1)
    key_part = lax.dynamic_slice_in_dim(key_weight, core_index * part_width, part_width, 1)
    value_part = lax.dynamic_slice_in_dim(value_weight, core_index * part_width, part_width, 1)
    query_proj = project(query_in, query_part).astype(jnp.bfloat16)
    key_proj = project(context_in, key_part).astype(jnp.bfloat16)
    value_proj = project(context_in, value_part).astype(jnp.bfloat16)
    attended_part = attention(query_proj, key_proj, value_proj, HEADS // core_count)
    attended = lax.all_gather(attended_part, "mp", axis=2, tiled=True)
    updated = full_views.astype(jnp.float32) + project(attended, out_weight)
    head_in = norm_rows(updated, gain_head)
    first_part = lax.dynamic_slice_in_dim(hidden_weight, core_index * hidden_part, hidden_part, 1)
    bias_part = lax.dynamic_slice_in_dim(hidden_bias, core_index * hidden_part, hidden_part, 0)
    second_part = lax.dynamic_slice_in_dim(point_weight, core_index * hidden_part, hidden_part, 1)
    hidden = jax.nn.gelu(project(head_in, first_part) + bias_part).astype(jnp.bfloat16)
    head_part = jnp.einsum("vth,ch->vct", hidden, second_part, preferred_element_type=jnp.float32)
    head_out = lax.psum(head_part, "mp")
    view_ids = jnp.arange(request_count)
    live_mask = jnp.logical_and(view_ids % 2 == core_index, view_ids // 2 < pair_total).astype(
        jnp.float32
    )
    contrib = point_terms(head_out) * live_mask[:, None, None]
    image_rows = my_images[view_ids]
    row_ids = jnp.arange(image_count // core_count * lax.axis_size(("pairs", "mp")))
    onehot = (image_rows[:, None] == row_ids[None, :]).astype(jnp.float32)
    return lax.psum_scatter(
        jnp.einsum("vr,vct->rct", onehot, contrib, precision=lax.Precision.HIGHEST),
        ("pairs", "mp"),
        scatter_dimension=0,
        tiled=True,
    )


def solution(mesh):
    return jax.shard_map(
        per_device,
        mesh=mesh,
        in_specs=(
            P(("groups", "pairs"), None, "mp"),
            P(),
            P(),
            P(),
            P(),
            P(),
            P(),
            P(),
            P(),
            P(),
            P(),
            P("groups", None),
            P("groups"),
            P("groups"),
        ),
        out_specs=P(("groups", "pairs", "mp"), None, None),
        check_vma=False,
    )
```

profile of v0, /device:TPU:0, one launch (start us, length us, event | category | flops | bytes accessed | tf_op | source)
XLA Modules:
  0.0 322.9 jit_solution(13960240500838489043)
XLA Ops:
  6.5 2.1 copy.39
  8.7 0.7 multiply_reduce_fusion.3
  9.5 0.7 reshape.108
  10.2 84.3 %all-gather.4.cloned.1.call-done = bf16[32,196,384]{2,1,0:T(8,128)(2,1)} async-done(((bf16[4,196,384]{2,1,0:T(8,128)(2,1)}), bf16[32,196,384]{2,1,0:T(8,128)(2,1)}) %all-gather.4.cloned.1.call-update) | async-done | bytes 4816912 | tf_op jit(solution)/shard_map/all_gather | solution.py:83
  94.6 4.7 %fusion.31 = bf16[12,196,384]{2,0,1:T(8,128)(2,1)} fusion(bf16[32,196,384]{2,1,0:T(8,128)(2,1)} %all-gather.4.cloned.1.call-done, s32[12]{0:T(128)S(1)} %fusion.77), kind=kOutput, calls=%fused_computation.41 | convolution fusion | flops 58706304 | bytes 6623280 | tf_op jit(solution)/shard_map/vi,itd->vtd/dot_general | solution.py:86
  99.3 12.7 %all-gather.6.cloned.1.call-done = bf16[12,196,768]{2,0,1:T(8,128)(2,1)} async-done(((bf16[12,196,384]{2,0,1:T(8,128)(2,1)}), bf16[12,196,768]{2,0,1:T(8,128)(2,1)}) %all-gather.6.cloned.1.call-update) | async-done | bytes 3612688 | tf_op jit(solution)/shard_map/all_gather | solution.py:89
  112.1 3.5 %copy.41 = bf16[12,196,768]{2,1,0:T(8,128)(2,1)S(1)} copy(bf16[12,196,768]{2,0,1:T(8,128)(2,1)} %all-gather.6.cloned.1.call-done) | data formatting | bytes 7225344 | tf_op jit(solution)/shard_map/all_gather | solution.py:89
  116.2 1.2 copy-done.1
  117.4 1.4 multiply_reduce_fusion.2
  118.8 3.2 convert_reduce_fusion
  122.0 4.1 %fusion.6 = f32[12,196]{0,1:T(8,128)S(1)} fusion(bf16[12,196,768]{2,0,1:T(8,128)(2,1)} %all-gather.6.cloned.1.call-done, f32[12,196]{0,1:T(8,128)S(1)} %broadcast_multiply_fusion.1), kind=kLoop, calls=%fused_computation.11 | loop fusion | flops 7222992 | bytes 3631488 | tf_op jit(solution)/shard_map/reduce_sum | solution.py:18
  126.8 2.8 fusion.11
  129.6 3.3 %convolution_convert_fusion = bf16[12,196,384]{2,1,0:T(8,128)(2,1)S(1)} fusion(bf16[12,196,768]{2,1,0:T(8,128)(2,1)S(1)} %fusion.11, bf16[768,768]{1,0:T(8,128)(2,1)} %param.18, s32[]{:T(128)S(6)} %select_n.37), kind=kOutput, calls=%fused_computation.44 | convolution fusion | flops 1388169216 | bytes 6008836 | tf_op jit(solution)/shard_map/vtd,de->vte/dot_general | solution.py:23
  133.0 3.4 %convolution_convert_fusion.1 = bf16[12,196,384]{2,1,0:T(8,128)(2,1)} fusion(bf16[12,196,768]{2,1,0:T(8,128)(2,1)S(1)} %fusion.11, bf16[768,768]{1,0:T(8,128)(2,1)S(1)} %copy-done.6, s32[]{:T(128)S(6)} %select_n.37), kind=kOutput, calls=%fused_computation.45 | convolution fusion | flops 1388169216 | bytes 6082564 | tf_op jit(solution)/shard_map/vtd,de->vte/dot_general | solution.py:23
  136.4 4.0 %copy.42 = bf16[12,196,384]{1,2,0:T(8,128)(2,1)} copy(bf16[12,196,384]{2,1,0:T(8,128)(2,1)} %convolution_convert_fusion.1) | data formatting | bytes 3612672 | tf_op jit(solution)/shard_map/convert_element_type | solution.py:103
  140.4 2.5 copy.45
  142.9 4.3 %fusion.8 = bf16[12,196,768]{2,0,1:T(8,128)(2,1)S(1)} fusion(bf16[12,196,768]{2,0,1:T(8,128)(2,1)} %all-gather.6.cloned.1.call-done, f32[768]{0:T(1024)S(1)} %copy-done.3, f32[12,196]{0,1:T(8,128)} %add_rsqrt_fusion.1, f32[12,196]{0,1:T(8,128)S(1)} %broadcast_multiply_fusion.1), kind=kLoop, calls=%fused_computation.13 | loop fusion | flops 9031680 | bytes 7247232 | tf_op jit(solution)/shard_map/convert_element_type | solution.py:19
  147.2 2.9 fusion.35
  150.2 2.5 copy.44
  152.7 13.0 %fusion.83 = (f32[12,6,196]{2,1,0:T(8,128)S(1)}, f32[12,6,196,196]{2,3,1,0:T(8,128)}) fusion(bf16[12,196,6,64]{1,3,2,0:T(8,128)(2,1)} %bitcast.64, bf16[12,196,6,64]{1,3,2,0:T(8,128)(2,1)} %bitcast.63), kind=kOutput, calls=%fused_computation.98 | convolution fusion | flops 362339904 | bytes 14732928 | tf_op jit(solution)/shard_map/sub | solution.py:37
  165.6 8.9 %fusion.34 = bf16[12,6,64,196]{3,2,1,0:T(8,128)(2,1)} fusion(bf16[12,196,6,64]{1,3,2,0:T(8,128)(2,1)} %bitcast.62, f32[12,6,196,196]{2,3,1,0:T(8,128)} %get-tuple-element.6, f32[12,6,196]{2,1,0:T(8,128)S(1)} %get-tuple-element.5), kind=kOutput, calls=%fused_computation.42 | convolution fusion | flops 360476928 | bytes 14732928 | tf_op jit(solution)/shard_map/vhqk,vkhd->vqhd/dot_general | solution.py:39
  174.6 4.2 %copy.47 = bf16[12,196,384]{2,1,0:T(8,128)(2,1)} copy(bf16[12,196,384]{1,2,0:T(8,128)(2,1)} %bitcast.65) | data formatting | bytes 3612672 | tf_op jit(solution)/shard_map/reshape | solution.py:45
  180.9 12.1 %all-gather.8.cloned.1.call-done = bf16[12,196,768]{2,1,0:T(8,128)(2,1)} async-done(((bf16[12,196,384]{2,1,0:T(8,128)(2,1)}), bf16[12,196,768]{2,1,0:T(8,128)(2,1)}) %all-gather.8.cloned.1.call-update) | async-done | bytes 3612688 | tf_op jit(solution)/shard_map/all_gather | solution.py:105
  193.0 5.2 %fusion.44 = f32[12,196,768]{2,1,0:T(8,128)S(1)} fusion(bf16[12,196,768]{2,1,0:T(8,128)(2,1)} %all-gather.8.cloned.1.call-done, bf16[768,768]{1,0:T(8,128)(2,1)S(1)} %copy-done.8), kind=kOutput, calls=%fused_computation.47 | convolution fusion | flops 2774532096 | bytes 12017664 | tf_op jit(solution)/shard_map/vtd,de->vte/dot_general | solution.py:23
  198.2 4.7 %fusion.24 = f32[12,196]{0,1:T(8,128)S(1)} fusion(f32[12,196,768]{2,1,0:T(8,128)S(1)} %fusion.44, bf16[12,196,768]{2,0,1:T(8,128)(2,1)} %all-gather.6.cloned.1.call-done), kind=kLoop, calls=%fused_computation.34 | loop fusion | flops 5416656 | bytes 10847424 | tf_op jit(solution)/shard_map/reduce_sum | solution.py:16
  202.9 7.0 %multiply_reduce_fusion.1 = f32[12,196]{0,1:T(8,128)S(1)} fusion(f32[12,196]{0,1:T(8,128)S(1)} %broadcast_multiply_fusion, f32[12,196,768]{2,1,0:T(8,128)S(1)} %fusion.44, bf16[12,196,768]{2,0,1:T(8,128)(2,1)} %all-gather.6.cloned.1.call-done), kind=kLoop, calls=%fused_computation.15 | loop fusion | flops 9029328 | bytes 10856832 | tf_op jit(solution)/shard_map/reduce_sum | solution.py:18
  210.0 5.1 %multiply_convert_fusion = bf16[12,196,768]{2,0,1:T(8,128)(2,1)} fusion(f32[768]{0:T(1024)S(1)} %copy-done.4, f32[12,196]{0,1:T(8,128)S(1)} %add_rsqrt_fusion, f32[12,196]{0,1:T(8,128)S(1)} %broadcast_multiply_fusion, f32[12,196,768]{2,1,0:T(8,128)S(1)} %fusion.44, bf16[12,196,768]{2,0,1:T(8,128)(2,1)S(1)} %bitcast.58), kind=kLoop, calls=%fused_computation.14 | loop fusion | flops 10838016 | bytes 14472576 | tf_op jit(solution)/shard_map/convert_element_type | solution.py:19
  215.2 6.7 %fusion.46 = f32[12,4,196]{2,1,0:T(4,128)S(1)} fusion(f32[512]{0:T(512)S(1)} %dynamic_slice.30, bf16[12,196,768]{2,0,1:T(8,128)(2,1)} %multiply_convert_fusion, bf16[768,1024]{1,0:T(8,128)(2,1)S(1)} %copy-done, s32[]{:T(128)S(6)} %select_n.36, bf16[4,1024]{1,0:T(4,128)(2,1)S(1)} %copy-done.9), kind=kOutput, calls=%fused_computation.49 | convolution fusion | flops 1871364096 | bytes 4443904 | tf_op jit(solution)/shard_map/vth,ch->vct/dot_general | solution.py:112
  221.8 3.6 %psum.7 = f32[12,4,196]{2,1,0:T(4,128)S(1)} all-reduce(f32[12,4,196]{2,1,0:T(4,128)S(1)} %fusion.46), channel_id=1, replica_groups=mesh['groups'=2,'pairs'=8,'mp'=2] {'mp'}, use_global_device_ids=true, to_apply=%region_8.0 | all-reduce | flops 9408 | bytes 75264 | tf_op jit(solution)/shard_map/psum | solution.py:113
  225.9 0.7 copy.51
  227.9 87.1 %all-reduce.3.cloned.1.call-done = f32[32,4,196]{2,1,0:T(4,128)} async-done(((f32[32,4,196]{2,1,0:T(4,128)}), f32[32,4,196]{2,1,0:T(4,128)}) %all-reduce.3.cloned.1.call-update) | async-done | bytes 100368
  315.0 1.3 constant_dynamic-slice_fusion.1
  (60 shorter events, 4.7 us)
Async XLA Ops:
  6.5 208.6 %copy-start = (bf16[768,1024]{1,0:T(8,128)(2,1)S(1)}, bf16[768,1024]{1,0:T(8,128)(2,1)}, u32[]{:S(2)}) copy-start(bf16[768,1024]{1,0:T(8,128)(2,1)} %param.22) | copy-start | bytes 4718596
  6.5 88.0 %all-gather.4.cloned.1.call-start = ((), (), s32[]{:S(2)}) async-start(), calls=%async_computation | async-start | bytes 5529600 | tf_op jit(solution)/shard_map/all_gather | solution.py:83
  8.7 103.4 %all-gather.6.cloned.1.call-start = ((), (), s32[]{:S(2)}) async-start(), calls=%async_computation.1 | async-start | bytes 7225344 | tf_op jit(solution)/shard_map/all_gather | solution.py:89
  99.3 93.7 %all-gather.8.cloned.1.call-start = ((), (), s32[]{:S(2)}) async-start(), calls=%async_computation.2 | async-start | bytes 5529600 | tf_op jit(solution)/shard_map/all_gather | solution.py:105
  115.6 1.8 copy-start.1
  118.8 8.1 %copy-start.2 = (f32[768]{0:T(1024)S(1)}, f32[768]{0:T(1024)}, u32[]{:S(2)}) copy-start(f32[768]{0:T(1024)} %param.16) | copy-start | bytes 9220
  129.6 3.4 %copy-start.6 = (bf16[768,768]{1,0:T(8,128)(2,1)S(1)}, bf16[768,768]{1,0:T(8,128)(2,1)}, u32[]{:S(2)}) copy-start(bf16[768,768]{1,0:T(8,128)(2,1)} %param.19) | copy-start | bytes 3538948
  136.4 6.5 %copy-start.3 = (f32[768]{0:T(1024)S(1)}, f32[768]{0:T(1024)}, u32[]{:S(2)}) copy-start(f32[768]{0:T(1024)} %param.15) | copy-start | bytes 9220
  142.9 4.3 %copy-start.7 = (bf16[768,768]{1,0:T(8,128)(2,1)S(1)}, bf16[768,768]{1,0:T(8,128)(2,1)}, u32[]{:S(2)}) copy-start(bf16[768,768]{1,0:T(8,128)(2,1)} %param.17) | copy-start | bytes 3538948
  174.6 4.3 %copy-start.10 = (s32[8]{0:T(128)S(1)}, s32[8]{0:T(128)}, u32[]{:S(2)}) copy-start(s32[8]{0:T(128)} %param.27) | copy-start | bytes 100
  174.6 5.5 %copy-start.5 = (f32[1024]{0:T(1024)S(1)}, f32[1024]{0:T(1024)}, u32[]{:S(2)}) copy-start(f32[1024]{0:T(1024)} %param.23) | copy-start | bytes 12292
  174.6 18.4 %copy-start.8 = (bf16[768,768]{1,0:T(8,128)(2,1)S(1)}, bf16[768,768]{1,0:T(8,128)(2,1)}, u32[]{:S(2)}) copy-start(bf16[768,768]{1,0:T(8,128)(2,1)} %param.20) | copy-start | bytes 3538948
  178.8 136.2 %all-reduce.3.cloned.1.call-start = ((), (), s32[]{:S(2)}) async-start(), calls=%async_computation.3 | async-start | bytes 262144
  198.2 11.8 %slice-start = ((s8[4816896]{0:T(1024)(128)(4,1)}), s8[622592]{0:T(1024)(128)(4,1)S(1)}, s32[]{:S(2)}) async-start(s8[4816896]{0:T(1024)(128)(4,1)} %bitcast.57), calls=%async_computation.4 | async-start | bytes 1245184
  202.9 7.1 %slice-start.1 = ((s8[4816896]{0:T(1024)(128)(4,1)}), s8[4194304]{0:T(1024)(128)(4,1)S(1)}, s32[]{:S(2)}) async-start(s8[4816896]{0:T(1024)(128)(4,1)} %bitcast.57), calls=%async_computation.5 | async-start | bytes 8388608
  202.9 7.1 %copy-start.4 = (f32[768]{0:T(1024)S(1)}, f32[768]{0:T(1024)}, u32[]{:S(2)}) copy-start(f32[768]{0:T(1024)} %param.21) | copy-start | bytes 9220
  210.0 5.2 %copy-start.9 = (bf16[4,1024]{1,0:T(4,128)(2,1)S(1)}, bf16[4,1024]{1,0:T(4,128)(2,1)}, u32[]{:S(2)}) copy-start(bf16[4,1024]{1,0:T(4,128)(2,1)} %param.24) | copy-start | bytes 24580
  215.2 11.5 %copy-start.11 = (u32[32]{0:T(128)S(1)}, u32[32]{0:T(128)}, u32[]{:S(2)}) copy-start(u32[32]{0:T(128)} %constant.82) | copy-start | bytes 388
Sparse Core Ops, SparseCore 0:
  9.5 84.9 all-gather.3
  99.4 12.6 all-gather.5
  178.9 13.9 all-gather.7
  226.8 88.2 all-reduce.2
where the time goes:
time: 325 us; the launch traced here: 323 us
  waiting for transfers between devices  196 us (60%)
  matrix products  48.5 us (15%)
  other arithmetic  35.4 us (11%)
  local copies, waits for them, and re-layouts  24.9 us (8%)
  between operations  14.1 us (4%)
  blocking collectives  3.56 us (1%)
    unnamed x5, waiting for transfers between devices  87.2 us
    all_gather x1, waiting for transfers between devices, per_device(): shard_rows = lax.all_gather(tokens, 'pairs', axis=0, tiled=True)  84.3 us
    dot_general x4, matrix products, project(): jnp.einsum('vtd,de->vte', rows_in, weight, preferred_element_type=jnp.flo...  14.9 us
    sub x1, matrix products, attention(): exponent = jnp.exp(scores - row_max)  13 us
    all_gather x1, waiting for transfers between devices, per_device(): full_views = lax.all_gather(half_views, 'mp', axis=2, tiled=True)  12.7 us
    reduce_sum x3, other arithmetic, norm_rows(): variance = jnp.mean(centered * centered, axis=-1, keepdims=True)  12.5 us
    convert_element_type x3, other arithmetic, norm_rows(): (centered * lax.rsqrt(variance + EPS) * gain_vec).astype(jnp.bfloat16)  12.2 us
    all_gather x1, waiting for transfers between devices, per_device(): attended = lax.all_gather(attended_part, 'mp', axis=2, tiled=True)  12.1 us
  transfers between devices with their start and end apart: 4, of which 4 were waited for; matrix products, arithmetic and copies ran while one was open for 1% of the time, Pallas kernels for 0%

commit v1 on v0

v1 whole, which is shorter than its diff:
```python
import functools

import jax
import jax.numpy as jnp
from jax import lax
from jax.experimental import pallas as pl
from jax.experimental.pallas import tpu as pltpu
from jax.sharding import PartitionSpec as P

HEADS = 12
EPS = 1e-06
F32 = jnp.float32
BF16 = jnp.bfloat16


def ring_place(index, count):
    if count > 8:
        return index
    half = index // 2
    return jnp.where(index % 2 == 0, half, count - 1 - half)


def ring_order(count):
    if count > 8:
        return list(range(count))
    return list(range(0, count, 2)) + list(range(count - 1, 0, -2))


def ring_gather(shard, count):
    order = ring_order(count)
    ahead = [(order[i], order[(i + 1) % count]) for i in range(count)]
    back = [(b, a) for a, b in ahead]
    middle = count // 2
    half = shard.shape[0] // 2
    parts = [None] * (count + 1)
    parts[0] = shard
    going, coming = shard, shard
    for step in range(1, middle):
        going = lax.ppermute(going, "pairs", ahead)
        coming = lax.ppermute(coming, "pairs", back)
        parts[count - step] = going
        parts[step] = coming
    parts[middle] = lax.ppermute(going[:half], "pairs", ahead)
    parts[count] = lax.ppermute(coming[half:], "pairs", back)
    return parts


def plan(owners, locals_, counts, worker, core, image_count, worker_count):
    requests = locals_.shape[0] // worker_count
    share = requests // 4
    first = jnp.array([0, 1, 2, 3, 4, 5, 3, 2], jnp.int32)
    second = jnp.array([4, 5, 3, 2, 0, 1, 2, 3], jnp.int32)
    place = jnp.where(core == 0, first, second)
    pair = worker * share + place // 2
    workers = jnp.arange(worker_count, dtype=jnp.int32)
    upto = jnp.sum(
        jnp.where(workers[None, :] <= workers[:, None], counts[None, :], 0), axis=1
    )
    past = upto[None, :] <= pair[:, None]
    holder = jnp.sum(past.astype(jnp.int32), axis=1)
    slot = pair - jnp.sum(jnp.where(past, counts[None, :], 0), axis=1)
    view = holder * requests + slot * 2 + place % 2
    all_images = owners * image_count + locals_
    ids = jnp.arange(all_images.shape[0], dtype=jnp.int32)
    image = jnp.sum(jnp.where(view[:, None] == ids[None, :], all_images[None, :], 0), axis=1)
    owner, row = image // image_count, image % image_count
    gap = (ring_place(owner, worker_count) - ring_place(worker, worker_count)) % worker_count
    middle, half = worker_count // 2, image_count // 2
    late = jnp.logical_and(gap == middle, row >= half)
    part = jnp.where(late, worker_count, gap)
    row = jnp.where(late, row - half, row)
    head = jnp.broadcast_to(jnp.asarray(core, jnp.int32), (8,))
    return jnp.stack([part, row, image, head])


def fetch(table, column, parts, target, sem, wait):
    if wait:
        pltpu.make_async_copy(parts[0].at[0], target, sem).wait()
        return
    part, row = table[0, column], table[1, column]
    for k, source in enumerate(parts):

        @pl.when(part == k)
        def _():
            pltpu.make_async_copy(source.at[row], target, sem).start()


def pick_kernel(count, table, *refs):
    parts, out, sems = refs[:count], refs[count], refs[count + 1]
    for wait in (False, True):
        for j in range(4):
            fetch(table, 4 + j, parts, out.at[j], sems.at[j], wait)


def norm_last(rows, gain):
    average = jnp.mean(rows, axis=-1, keepdims=True)
    centered = rows - average
    variance = jnp.mean(centered * centered, axis=-1, keepdims=True)
    return centered * lax.rsqrt(variance + EPS) * gain


def decode_kernel(count, tokens, table, *refs):
    parts = refs[:count]
    (other, gain_q, gain_c, gain_h, bias_h, wp) = refs[count : count + 6]
    weights = refs[count + 6 : count + 11]
    out = refs[count + 11]
    (mine, theirs, xq, xc, res, q, k, v, att, hid) = refs[count + 12 : count + 22]
    held = refs[count + 22 : count + 27]
    sems, wsems, osem = refs[count + 27 :]
    wq, wk, wv, wo, wh = held
    rows, half = mine.shape[1], mine.shape[2]
    views, padded, width = q.shape
    core = table[3, 0]

    for j in range(4):
        fetch(table, j, parts, mine.at[j], sems.at[j], False)
    incoming = pltpu.make_async_copy(other, theirs, osem)
    incoming.start()
    copies = [
        pltpu.make_async_copy(weights[i], held[i], wsems.at[i]) for i in range(len(weights))
    ]
    for copy in copies:
        copy.start()

    out[...] = jnp.zeros_like(out)
    tail = jnp.zeros((views, padded - rows, width), BF16)
    xq[:, rows:, :] = tail
    xc[:, rows:, :] = tail
    res[:, rows:, :] = tail
    for j in range(4):
        fetch(table, j, parts, mine.at[j], sems.at[j], True)
    incoming.wait()

    here = pl.ds(pl.multiple_of(core * half, half), half)
    there = pl.ds(pl.multiple_of((1 - core) * half, half), half)
    context_of = (1, 0, None, 2)
    for j in range(4):
        raw_a, raw_b = mine[j], theirs[j]
        a, b = raw_a.astype(F32), raw_b.astype(F32)
        average = (
            jnp.sum(a, axis=-1, keepdims=True) + jnp.sum(b, axis=-1, keepdims=True)
        ) / width
        a, b = a - average, b - average
        variance = (
            jnp.sum(a * a, axis=-1, keepdims=True) + jnp.sum(b * b, axis=-1, keepdims=True)
        ) / width
        scale = lax.rsqrt(variance + EPS)
        a, b = a * scale, b * scale
        if j < views:
            xq[j, :rows, here] = (a * gain_q[:, here]).astype(BF16)
            xq[j, :rows, there] = (b * gain_q[:, there]).astype(BF16)
            res[j, :rows, here] = raw_a
            res[j, :rows, there] = raw_b
        if context_of[j] is not None:
            xc[context_of[j], :rows, here] = (a * gain_c[:, here]).astype(BF16)
            xc[context_of[j], :rows, there] = (b * gain_c[:, there]).astype(BF16)

    total = views * padded
    head_size = width // HEADS
    queries = xq[...].reshape(total, width)
    contexts = xc[...].reshape(total, width)
    copies[0].wait()
    proj = jnp.dot(queries, wq[...], preferred_element_type=F32)
    q[...] = (proj.astype(BF16) * BF16(head_size**-0.5)).reshape(views, padded, width)
    copies[1].wait()
    proj = jnp.dot(contexts, wk[...], preferred_element_type=F32)
    k[...] = proj.astype(BF16).reshape(views, padded, width)
    copies[2].wait()
    proj = jnp.dot(contexts, wv[...], preferred_element_type=F32)
    v[...] = proj.astype(BF16).reshape(views, padded, width)

    block = 2 * head_size
    low = lax.broadcasted_iota(jnp.int32, (padded, block), 1) < head_size
    hide = jnp.where(lax.broadcasted_iota(jnp.int32, (1, padded), 1) < tokens, 0.0, -1e30)
    nothing = jnp.zeros((padded, block), BF16)

    def attend(i, carry):
        for b in range(width // block):
            cols = slice(b * block, (b + 1) * block)
            qb, kb, vb = q[i, :, cols], k[i, :, cols], v[i, :, cols]
            blended = []
            for keep in (0, 1):
                qh = jnp.where(low, qb, nothing) if keep == 0 else jnp.where(low, nothing, qb)
                scores = lax.dot_general(
                    qh, kb, (((1,), (1,)), ((), ())), preferred_element_type=F32
                )
                scores = scores + hide
                peak = jnp.max(scores, axis=-1, keepdims=True)
                expo = jnp.exp(scores - peak)
                inverse = 1.0 / jnp.sum(expo, axis=-1, keepdims=True)
                probs = (expo * inverse).astype(BF16)
                blended.append(jnp.dot(probs, vb, preferred_element_type=F32))
            att[i, :, cols] = jnp.where(low, blended[0], blended[1]).astype(BF16)
        return carry

    lax.fori_loop(0, views, attend, 0)

    copies[3].wait()
    updated = jnp.dot(att[...].reshape(total, width), wo[...], preferred_element_type=F32)
    updated = updated + res[...].reshape(total, width).astype(F32)
    head_in = norm_last(updated, gain_h[...]).astype(BF16)
    copies[4].wait()
    hidden = jnp.dot(head_in, wh[...], preferred_element_type=F32) + bias_h[...]
    hid[...] = jax.nn.gelu(hidden).astype(BF16).reshape(views, padded, hid.shape[2])
    for i in range(views):
        raw = lax.dot_general(
            wp[...], hid[i], (((1,), (1,)), ((), ())), preferred_element_type=F32
        )
        conf = 1.0 + jnp.exp(raw[3:4])
        last = lax.broadcasted_iota(jnp.int32, raw.shape, 0) == 3
        contrib = jnp.where(last, conf, raw * conf)
        image = table[2, i]
        out[image] = out[image] + contrib[:, :tokens]


def per_device(
    tokens,
    gain_query,
    gain_context,
    query_weight,
    key_weight,
    value_weight,
    out_weight,
    gain_head,
    hidden_weight,
    hidden_bias,
    point_weight,
    view_owner,
    view_local,
    pair_count,
):
    worker_count = lax.axis_size("pairs")
    core_count = lax.axis_size("mp")
    worker = lax.axis_index("pairs").astype(jnp.int32)
    core = lax.axis_index("mp").astype(jnp.int32)
    image_count, token_count, half = tokens.shape
    width, hidden_width = hidden_weight.shape
    rows = -(-token_count // 8) * 8
    padded = -(-token_count // 16) * 16
    views = 3

    shard = jnp.pad(tokens, ((0, 0), (0, rows - token_count), (0, 0)))
    parts = ring_gather(shard, worker_count)
    table = plan(
        view_owner[:, 0], view_local, pair_count, worker, core, image_count, worker_count
    )

    count = len(parts)
    anywhere = pl.BlockSpec(memory_space=pl.ANY)
    scalars = pl.BlockSpec(memory_space=pltpu.SMEM)
    vector = pl.BlockSpec(memory_space=pltpu.VMEM)
    send = pl.pallas_call(
        functools.partial(pick_kernel, count),
        out_shape=jax.ShapeDtypeStruct((4, rows, half), BF16),
        in_specs=[scalars] + [anywhere] * count,
        out_specs=anywhere,
        scratch_shapes=[pltpu.SemaphoreType.DMA((4,))],
        name="pick",
    )(table, *parts)
    other = lax.ppermute(send, "mp", [(0, 1), (1, 0)])

    flat = pl.pallas_call(
        functools.partial(decode_kernel, count, token_count),
        out_shape=jax.ShapeDtypeStruct((worker_count * image_count, 4, token_count), F32),
        in_specs=[scalars] + [anywhere] * (count + 1) + [vector] * 5 + [anywhere] * 5,
        out_specs=vector,
        scratch_shapes=[
            pltpu.VMEM((4, rows, half), BF16),
            pltpu.VMEM((4, rows, half), BF16),
            pltpu.VMEM((views, padded, width), BF16),
            pltpu.VMEM((views, padded, width), BF16),
            pltpu.VMEM((views, padded, width), BF16),
            pltpu.VMEM((views, padded, width), BF16),
            pltpu.VMEM((views, padded, width), BF16),
            pltpu.VMEM((views, padded, width), BF16),
            pltpu.VMEM((views, padded, width), BF16),
            pltpu.VMEM((views, padded, hidden_width), BF16),
            pltpu.VMEM((width, width), BF16),
            pltpu.VMEM((width, width), BF16),
            pltpu.VMEM((width, width), BF16),
            pltpu.VMEM((width, width), BF16),
            pltpu.VMEM((width, hidden_width), BF16),
            pltpu.SemaphoreType.DMA((4,)),
            pltpu.SemaphoreType.DMA((5,)),
            pltpu.SemaphoreType.DMA,
        ],
        compiler_params=pltpu.CompilerParams(vmem_limit_bytes=48 * 1024 * 1024),
        name="decode",
    )(
        table,
        *parts,
        other,
        gain_query.reshape(1, width),
        gain_context.reshape(1, width),
        gain_head.reshape(1, width),
        hidden_bias.reshape(1, hidden_width),
        point_weight,
        query_weight,
        key_weight,
        value_weight,
        out_weight,
        hidden_weight,
    )
    arrived = lax.all_to_all(flat, ("pairs", "mp"), 0, 0, tiled=True)
    mine = image_count // core_count
    return jnp.sum(arrived.reshape(worker_count * core_count, mine, 4, token_count), axis=0)


def solution(mesh):
    return jax.shard_map(
        per_device,
        mesh=mesh,
        in_specs=(
            P(("groups", "pairs"), None, "mp"),
            P(),
            P(),
            P(),
            P(),
            P(),
            P(),
            P(),
            P(),
            P(),
            P(),
            P("groups", None),
            P("groups"),
            P("groups"),
        ),
        out_specs=P(("groups", "pairs", "mp"), None, None),
        check_vma=False,
    )
```

time: 325 us -> 115 us (0.35)
  waiting for transfers between devices: 196 us -> 46.2 us
  matrix products: 48.5 us -> 0 us
  Pallas kernels: 0 us -> 35.7 us
  other arithmetic: 35.4 us -> 1.83 us
  local copies, waits for them, and re-layouts: 24.9 us -> 7.8 us
  between operations: 14.1 us -> 0.24 us
  blocking collectives: 3.56 us -> 13.1 us
  starting transfers between devices: 0.13 us -> 9.34 us
    all_gather x3 -> x0, waiting for transfers between devices: 109 us -> none  [the longest x1 84.3 us: per_device(): shard_rows = lax.all_gather(tokens, 'pairs', axis=0, tiled=True)]
    unnamed x5 -> x0, waiting for transfers between devices: 87.2 us -> none
    ppermute x0 -> x9, waiting for transfers between devices: none -> 46.2 us  [the longest x3 38.6 us: ring_gather(): going = lax.ppermute(going, 'pairs', ahead)]
    pallas_call x0 -> x2, Pallas kernels: none -> 35.7 us  [the longest x1 20.5 us: per_device(): pl.pallas_call(functools.partial(pick_kernel, count), out_shape=jax.Shape...]
    dot_general x8 -> x0, matrix products: 35.6 us -> none  [the longest x4 14.9 us: project(): jnp.einsum('vtd,de->vte', rows_in, weight, preferred_element_type=jnp.flo...]
    reduce_sum x6 -> x4, other arithmetic: 21 us -> 1.12 us  [the longest x1 0.64 us: per_device(): jnp.sum(arrived.reshape(worker_count * core_count, mine, 4, token_count),...]
    all_to_all x0 -> x1, blocking collectives: none -> 13.1 us  [per_device(): arrived = lax.all_to_all(flat, ('pairs', 'mp'), 0, 0, tiled=True)]
    sub x1 -> x0, matrix products: 13 us -> none  [attention(): exponent = jnp.exp(scores - row_max)]
  transfers between devices with their start and end apart: 4 -> 9, of which waited for: 4 -> 6; matrix products, arithmetic and copies ran while one was open for 1% -> 1% of each run, Pallas kernels for 0% -> 0%
where the time goes in v1:
time: 115 us; the launch traced here: 114 us
  waiting for transfers between devices  46.2 us (40%)
  Pallas kernels  35.7 us (31%)
  blocking collectives  13.1 us (11%)
  starting transfers between devices  9.34 us (8%)
  local copies, waits for them, and re-layouts  7.8 us (7%)
  other arithmetic  1.83 us (2%)
    ppermute x3, waiting for transfers between devices, ring_gather(): going = lax.ppermute(going, 'pairs', ahead)  38.6 us
    pallas_call x1, Pallas kernels, per_device(): pl.pallas_call(functools.partial(pick_kernel, count), out_shape=jax.Shape...  20.5 us
    pallas_call x1, Pallas kernels, per_device(): pl.pallas_call(functools.partial(decode_kernel, count, token_count), out_...  15.3 us
    all_to_all x1, blocking collectives, per_device(): arrived = lax.all_to_all(flat, ('pairs', 'mp'), 0, 0, tiled=True)  13.1 us
    unnamed x47, local copies, waits for them, and re-layouts  7.59 us
    ppermute x3, starting transfers between devices, ring_gather(): going = lax.ppermute(going, 'pairs', ahead)  6.35 us
    ppermute x1, waiting for transfers between devices, ring_gather(): parts[middle] = lax.ppermute(going[:half], 'pairs', ahead)  3.95 us
  transfers between devices with their start and end apart: 9, of which 6 were waited for; matrix products, arithmetic and copies ran while one was open for 1% of the time, Pallas kernels for 0%

profile of v1, /device:TPU:0, one launch (start us, length us, event | category | flops | bytes accessed | tf_op | source)
XLA Modules:
  0.0 114.3 jit_solution(6291991391994569584)
XLA Ops:
  0.0 1.2 %copy.18 = bf16[4,196,384]{2,1,0:T(8,128)(2,1)S(1)} copy(bf16[4,196,384]{2,0,1:T(4,128)(2,1)} %param.16) | data formatting | bytes 1204224 | tf_op args[0]
  1.2 0.1 pad.4.refs_0_
  1.3 3.1 %collective-permute-start.3 = (bf16[4,200,384]{2,1,0:T(8,128)(2,1)S(1)}, bf16[4,200,384]{2,1,0:T(8,128)(2,1)S(1)}, u32[]{:S(2)}, u32[]{:S(2)}) collective-permute-start(bf16[4,200,384]{2,1,0:T(8,128)(2,1)S(1)} %pad.4.refs_0_), channel_id=1, source_target_pairs={{0,4},{4,8},{8,12},{12,14},{14,10},{10,6},{6,2},{2,0},{1,5},{5,9},... | collective-permute-start | bytes 1843208 | tf_op jit(solution)/shard_map/ppermute | solution.py:39
  4.4 0.0 collective-permute-start
  4.4 13.8 %collective-permute-done.3.refs_7_ = bf16[4,200,384]{2,1,0:T(8,128)(2,1)S(1)} collective-permute-done((bf16[4,200,384]{2,1,0:T(8,128)(2,1)S(1)}, bf16[4,200,384]{2,1,0:T(8,128)(2,1)S(1)}, u32[]{:S(2)}, u32[]{:S(2)}) %collective-permute-start.3) | collective-permute-done | bytes 614432 | tf_op jit(solution)/shard_map/ppermute | solution.py:39
  18.2 1.8 %collective-permute-start.4 = (bf16[4,200,384]{2,1,0:T(8,128)(2,1)S(1)}, bf16[4,200,384]{2,1,0:T(8,128)(2,1)}, u32[]{:S(2)}, u32[]{:S(2)}) collective-permute-start(bf16[4,200,384]{2,1,0:T(8,128)(2,1)S(1)} %collective-permute-done.3.refs_7_), channel_id=1, source_target_pairs={{0,4},{4,8},{8,12},{12,14},{14,10},{10,6},{6,2},{2,0},{1,5},{5,9},... | collective-permute-start | bytes 1843208 | tf_op jit(solution)/shard_map/ppermute | solution.py:39
  20.0 0.2 collective-permute-start.1
  20.2 0.1 select_reduce_fusion.1
  20.4 13.0 %collective-permute-done.4.refs_6_ = bf16[4,200,384]{2,1,0:T(8,128)(2,1)} collective-permute-done((bf16[4,200,384]{2,1,0:T(8,128)(2,1)S(1)}, bf16[4,200,384]{2,1,0:T(8,128)(2,1)}, u32[]{:S(2)}, u32[]{:S(2)}) %collective-permute-start.4) | collective-permute-done | bytes 614432 | tf_op jit(solution)/shard_map/ppermute | solution.py:39
  33.3 1.5 %collective-permute-start.5 = (bf16[4,200,384]{2,1,0:T(8,128)(2,1)}, bf16[4,200,384]{2,1,0:T(8,128)(2,1)S(1)}, u32[]{:S(2)}, u32[]{:S(2)}) collective-permute-start(bf16[4,200,384]{2,1,0:T(8,128)(2,1)} %collective-permute-done.4.refs_6_), channel_id=1, source_target_pairs={{0,4},{4,8},{8,12},{12,14},{14,10},{10,6},{6,2},{2,0},{1,5},{5,9},... | collective-permute-start | bytes 1843208 | tf_op jit(solution)/shard_map/ppermute | solution.py:39
  34.8 0.5 collective-permute-start.2
  35.3 0.2 fusion
  35.6 0.2 select_reduce_fusion
  35.8 11.9 %collective-permute-done.5.refs_5_ = bf16[4,200,384]{2,1,0:T(8,128)(2,1)S(1)} collective-permute-done((bf16[4,200,384]{2,1,0:T(8,128)(2,1)}, bf16[4,200,384]{2,1,0:T(8,128)(2,1)S(1)}, u32[]{:S(2)}, u32[]{:S(2)}) %collective-permute-start.5) | collective-permute-done | bytes 614432 | tf_op jit(solution)/shard_map/ppermute | solution.py:39
  47.7 1.3 %collective-permute-start.6 = (bf16[2,200,384]{2,1,0:T(8,128)(2,1)S(1)}, bf16[2,200,384]{2,1,0:T(8,128)(2,1)S(1)}, u32[]{:S(2)}, u32[]{:S(2)}) collective-permute-start(bf16[2,200,384]{2,1,0:T(8,128)(2,1)S(1)} %slice.8), channel_id=1, source_target_pairs={{0,4},{4,8},{8,12},{12,14},{14,10},{10,6},{6,2},{2,0},{1,5},{5,9},... | collective-permute-start | bytes 921608 | tf_op jit(solution)/shard_map/ppermute | solution.py:43
  49.1 0.8 collective-permute-start.7
  49.9 0.1 pad.8.clone
  50.0 0.7 add_add_fusion.table
  50.6 3.9 %collective-permute-done.6.refs_4_ = bf16[2,200,384]{2,1,0:T(8,128)(2,1)S(1)} collective-permute-done((bf16[2,200,384]{2,1,0:T(8,128)(2,1)S(1)}, bf16[2,200,384]{2,1,0:T(8,128)(2,1)S(1)}, u32[]{:S(2)}, u32[]{:S(2)}) %collective-permute-start.6) | collective-permute-done | bytes 307232 | tf_op jit(solution)/shard_map/ppermute | solution.py:43
  54.6 1.5 %collective-permute-done.7.refs_8_ = bf16[2,200,384]{2,1,0:T(8,128)(2,1)} collective-permute-done((bf16[2,200,384]{2,1,0:T(8,128)(2,1)S(1)}, bf16[2,200,384]{2,1,0:T(8,128)(2,1)}, u32[]{:S(2)}, u32[]{:S(2)}) %collective-permute-start.7) | collective-permute-done | bytes 307232 | tf_op jit(solution)/shard_map/ppermute | solution.py:44
  56.1 20.5 %pick.1 = bf16[4,200,384]{2,1,0:T(8,128)(2,1)} custom-call(s32[4,8]{1,0:T(4,128)} %add_add_fusion.table, bf16[4,200,384]{2,1,0:T(8,128)(2,1)} %copy-done, bf16[4,200,384]{2,1,0:T(8,128)(2,1)} %copy-done.8, bf16[4,200,384]{2,1,0:T(8,128)(2,1)} %collective-permute-done.1.refs_2_, bf16[4,200,384]{2,1,0:T(8,128)(2,1)} %copy-done.4, ...), custom_call_target="tpu_custom_call" | custom-call | tf_op jit(solution)/shard_map/pick/pallas_call | solution.py:252
  76.6 0.1 collective-permute-start.8
  76.7 2.2 %collective-permute-done.8.refs_9_ = bf16[4,200,384]{2,1,0:T(8,128)(2,1)S(1)} collective-permute-done((bf16[4,200,384]{2,1,0:T(8,128)(2,1)}, bf16[4,200,384]{2,1,0:T(8,128)(2,1)S(1)}, u32[]{:S(2)}, u32[]{:S(2)}) %collective-permute-start.8) | collective-permute-done | bytes 614432 | tf_op jit(solution)/shard_map/ppermute | solution.py:260
  78.9 1.1 copy-done.1
  80.0 1.1 copy-done.3
  81.1 1.1 copy-done.5
  82.1 1.1 copy-done.7
  83.2 1.1 copy-done.9
  84.3 1.0 copy-done.11
  85.2 15.3 %decode.1 = f32[32,4,196]{2,1,0:T(4,128)S(1)} custom-call(s32[4,8]{1,0:T(4,128)S(1)} %copy-done.12, bf16[4,200,384]{2,1,0:T(8,128)(2,1)S(1)} %copy-done.1, bf16[4,200,384]{2,1,0:T(8,128)(2,1)S(1)} %copy-done.9, bf16[4,200,384]{2,1,0:T(8,128)(2,1)} %collective-permute-done.1.refs_2_, bf16[4,200,384]{2,1,0:T(8,128)(2,1)S(1)} %copy-done.5, ...), custom_call_target="tpu_custom_call" | custom-call | tf_op jit(solution)/shard_map/decode/pallas_call | solution.py:262
  100.5 13.1 %all_to_all.5 = f32[32,4,196]{2,1,0:T(4,128)S(1)} all-to-all(f32[32,4,196]{2,1,0:T(4,128)S(1)} %decode.1), channel_id=1, replica_groups=mesh['groups'=2,'pairs'=8,'mp'=2] {'pairs','mp'}, dimensions={0} | all-to-all | bytes 200704 | tf_op jit(solution)/shard_map/all_to_all | solution.py:304
  113.6 0.6 reduce_sum.52
  (52 shorter events, 0.2 us)
Async XLA Ops:
  0.0 20.3 %copy-start.18 = (s32[8]{0:T(128)S(1)}, s32[8]{0:T(128)}, u32[]{:S(2)}) copy-start(s32[8]{0:T(128)} %constant.111.clone) | copy-start | bytes 100
  0.0 20.3 %copy-start.19 = (s32[8]{0:T(128)S(1)}, s32[8]{0:T(128)}, u32[]{:S(2)}) copy-start(s32[8]{0:T(128)} %constant.112.clone) | copy-start | bytes 100
  0.0 20.2 %copy-start.20 = (s32[8]{0:T(128)S(1)}, s32[8]{0:T(128)}, u32[]{:S(2)}) copy-start(s32[8]{0:T(128)} %param.29) | copy-start | bytes 100
  0.0 35.5 %copy-start.22 = (s32[96,1]{0,1:T(1,128)S(1)}, s32[96,1]{0,1:T(1,128)}, u32[]{:S(2)}) copy-start(s32[96,1]{0,1:T(1,128)} %param.27) | copy-start | bytes 1156
  0.0 35.5 %copy-start.21 = (s32[96]{0:T(128)S(1)}, s32[96]{0:T(128)}, u32[]{:S(2)}) copy-start(s32[96]{0:T(128)} %param.28) | copy-start | bytes 1156
  1.3 54.8 %copy-start = (bf16[4,200,384]{2,1,0:T(8,128)(2,1)}, bf16[4,200,384]{2,1,0:T(8,128)(2,1)S(1)}, u32[]{:S(2)}) copy-start(bf16[4,200,384]{2,1,0:T(8,128)(2,1)S(1)} %pad.4.refs_0_) | copy-start | bytes 1843204
  1.3 16.9 %collective-permute-start.3 = (bf16[4,200,384]{2,1,0:T(8,128)(2,1)S(1)}, bf16[4,200,384]{2,1,0:T(8,128)(2,1)S(1)}, u32[]{:S(2)}, u32[]{:S(2)}) collective-permute-start(bf16[4,200,384]{2,1,0:T(8,128)(2,1)S(1)} %pad.4.refs_0_), channel_id=1, source_target_pairs={{0,4},{4,8},{8,12},{12,14},{14,10},{10,6},{6,2},{2,0},{1,5},{5,9},... | collective-permute-start | bytes 1843208 | tf_op jit(solution)/shard_map/ppermute | solution.py:39
  4.4 15.6 %collective-permute-start = (bf16[4,200,384]{2,1,0:T(8,128)(2,1)S(1)}, bf16[4,200,384]{2,1,0:T(8,128)(2,1)S(1)}, u32[]{:S(2)}, u32[]{:S(2)}) collective-permute-start(bf16[4,200,384]{2,1,0:T(8,128)(2,1)S(1)} %pad.4.refs_0_), channel_id=1, source_target_pairs={{4,0},{8,4},{12,8},{14,12},{10,14},{6,10},{2,6},{0,2},{5,1},{9,5},... | collective-permute-start | bytes 1843208 | tf_op jit(solution)/shard_map/ppermute | solution.py:40
  18.2 37.9 %copy-start.6 = (bf16[4,200,384]{2,1,0:T(8,128)(2,1)}, bf16[4,200,384]{2,1,0:T(8,128)(2,1)S(1)}, u32[]{:S(2)}) copy-start(bf16[4,200,384]{2,1,0:T(8,128)(2,1)S(1)} %collective-permute-done.3.refs_7_) | copy-start | bytes 1843204
  18.2 15.1 %collective-permute-start.4 = (bf16[4,200,384]{2,1,0:T(8,128)(2,1)S(1)}, bf16[4,200,384]{2,1,0:T(8,128)(2,1)}, u32[]{:S(2)}, u32[]{:S(2)}) collective-permute-start(bf16[4,200,384]{2,1,0:T(8,128)(2,1)S(1)} %collective-permute-done.3.refs_7_), channel_id=1, source_target_pairs={{0,4},{4,8},{8,12},{12,14},{14,10},{10,6},{6,2},{2,0},{1,5},{5,9},... | collective-permute-start | bytes 1843208 | tf_op jit(solution)/shard_map/ppermute | solution.py:39
  20.0 36.1 %copy-start.8 = (bf16[4,200,384]{2,1,0:T(8,128)(2,1)}, bf16[4,200,384]{2,1,0:T(8,128)(2,1)S(1)}, u32[]{:S(2)}) copy-start(bf16[4,200,384]{2,1,0:T(8,128)(2,1)S(1)} %collective-permute-done.refs_1_) | copy-start | bytes 1843204
  20.0 14.8 %collective-permute-start.1 = (bf16[4,200,384]{2,1,0:T(8,128)(2,1)S(1)}, bf16[4,200,384]{2,1,0:T(8,128)(2,1)}, u32[]{:S(2)}, u32[]{:S(2)}) collective-permute-start(bf16[4,200,384]{2,1,0:T(8,128)(2,1)S(1)} %collective-permute-done.refs_1_), channel_id=1, source_target_pairs={{4,0},{8,4},{12,8},{14,12},{10,14},{6,10},{2,6},{0,2},{5,1},{9,5},... | collective-permute-start | bytes 1843208 | tf_op jit(solution)/shard_map/ppermute | solution.py:40
  33.3 14.3 %collective-permute-start.5 = (bf16[4,200,384]{2,1,0:T(8,128)(2,1)}, bf16[4,200,384]{2,1,0:T(8,128)(2,1)S(1)}, u32[]{:S(2)}, u32[]{:S(2)}) collective-permute-start(bf16[4,200,384]{2,1,0:T(8,128)(2,1)} %collective-permute-done.4.refs_6_), channel_id=1, source_target_pairs={{0,4},{4,8},{8,12},{12,14},{14,10},{10,6},{6,2},{2,0},{1,5},{5,9},... | collective-permute-start | bytes 1843208 | tf_op jit(solution)/shard_map/ppermute | solution.py:39
  34.8 14.2 %collective-permute-start.2 = (bf16[4,200,384]{2,1,0:T(8,128)(2,1)}, bf16[4,200,384]{2,1,0:T(8,128)(2,1)S(1)}, u32[]{:S(2)}, u32[]{:S(2)}) collective-permute-start(bf16[4,200,384]{2,1,0:T(8,128)(2,1)} %collective-permute-done.1.refs_2_), channel_id=1, source_target_pairs={{4,0},{8,4},{12,8},{14,12},{10,14},{6,10},{2,6},{0,2},{5,1},{9,5},... | collective-permute-start | bytes 1843208 | tf_op jit(solution)/shard_map/ppermute | solution.py:40
  47.6 8.4 %copy-start.2 = (bf16[4,200,384]{2,1,0:T(8,128)(2,1)}, bf16[4,200,384]{2,1,0:T(8,128)(2,1)S(1)}, u32[]{:S(2)}) copy-start(bf16[4,200,384]{2,1,0:T(8,128)(2,1)S(1)} %collective-permute-done.5.refs_5_) | copy-start | bytes 1843204
  47.7 6.9 %collective-permute-start.6 = (bf16[2,200,384]{2,1,0:T(8,128)(2,1)S(1)}, bf16[2,200,384]{2,1,0:T(8,128)(2,1)S(1)}, u32[]{:S(2)}, u32[]{:S(2)}) collective-permute-start(bf16[2,200,384]{2,1,0:T(8,128)(2,1)S(1)} %slice.8), channel_id=1, source_target_pairs={{0,4},{4,8},{8,12},{12,14},{14,10},{10,6},{6,2},{2,0},{1,5},{5,9},... | collective-permute-start | bytes 921608 | tf_op jit(solution)/shard_map/ppermute | solution.py:43
  49.0 7.1 %copy-start.4 = (bf16[4,200,384]{2,1,0:T(8,128)(2,1)}, bf16[4,200,384]{2,1,0:T(8,128)(2,1)S(1)}, u32[]{:S(2)}) copy-start(bf16[4,200,384]{2,1,0:T(8,128)(2,1)S(1)} %collective-permute-done.2.refs_3_) | copy-start | bytes 1843204
  49.1 7.0 %collective-permute-start.7 = (bf16[2,200,384]{2,1,0:T(8,128)(2,1)S(1)}, bf16[2,200,384]{2,1,0:T(8,128)(2,1)}, u32[]{:S(2)}, u32[]{:S(2)}) collective-permute-start(bf16[2,200,384]{2,1,0:T(8,128)(2,1)S(1)} %slice.9), channel_id=1, source_target_pairs={{4,0},{8,4},{12,8},{14,12},{10,14},{6,10},{2,6},{0,2},{5,1},{9,5},... | collective-permute-start | bytes 921608 | tf_op jit(solution)/shard_map/ppermute | solution.py:44
  50.6 26.0 %copy-start.15 = (f32[768]{0:T(1024)S(1)}, f32[768]{0:T(1024)}, u32[]{:S(2)}) copy-start(f32[768]{0:T(1024)} %param.17) | copy-start | bytes 9220
  50.6 26.1 %copy-start.16 = (f32[768]{0:T(1024)S(1)}, f32[768]{0:T(1024)}, u32[]{:S(2)}) copy-start(f32[768]{0:T(1024)} %param.18) | copy-start | bytes 9220
  50.6 26.1 %copy-start.17 = (f32[768]{0:T(1024)S(1)}, f32[768]{0:T(1024)}, u32[]{:S(2)}) copy-start(f32[768]{0:T(1024)} %param.23) | copy-start | bytes 9220
  50.6 28.3 %copy-start.12 = (s32[4,8]{1,0:T(4,128)S(1)}, s32[4,8]{1,0:T(4,128)}, u32[]{:S(2)}) copy-start(s32[4,8]{1,0:T(4,128)} %add_add_fusion.table) | copy-start | bytes 388
  50.6 28.3 %copy-start.13 = (bf16[4,1024]{1,0:T(4,128)(2,1)S(1)}, bf16[4,1024]{1,0:T(4,128)(2,1)}, u32[]{:S(2)}) copy-start(bf16[4,1024]{1,0:T(4,128)(2,1)} %refs_14_.1) | copy-start | bytes 24580
  50.6 28.3 %copy-start.14 = (f32[1024]{0:T(1024)S(1)}, f32[1024]{0:T(1024)}, u32[]{:S(2)}) copy-start(f32[1024]{0:T(1024)} %param.25) | copy-start | bytes 12292
  54.6 1.5 %copy-start.10 = (bf16[2,200,384]{2,1,0:T(8,128)(2,1)}, bf16[2,200,384]{2,1,0:T(8,128)(2,1)S(1)}, u32[]{:S(2)}) copy-start(bf16[2,200,384]{2,1,0:T(8,128)(2,1)S(1)} %collective-permute-done.6.refs_4_) | copy-start | bytes 921604
  76.6 2.3 %collective-permute-start.8 = (bf16[4,200,384]{2,1,0:T(8,128)(2,1)}, bf16[4,200,384]{2,1,0:T(8,128)(2,1)S(1)}, u32[]{:S(2)}, u32[]{:S(2)}) collective-permute-start(bf16[4,200,384]{2,1,0:T(8,128)(2,1)} %pick.1), channel_id=1, source_target_pairs={{0,1},{1,0},{2,3},{3,2},{4,5},{5,4},{6,7},{7,6},{8,9},{9,8},{10,11... | collective-permute-start | bytes 1843208 | tf_op jit(solution)/shard_map/ppermute | solution.py:260
  78.9 1.1 copy-start.1
  80.0 1.1 copy-start.3
  81.1 1.1 copy-start.5
  82.1 1.1 copy-start.7
  83.2 1.1 copy-start.9
  84.3 1.0 copy-start.11

commit v2 on v1

--- a/solution.py
+++ b/solution.py
@@ -13,6 +13,14 @@
 BF16 = jnp.bfloat16
 
 
+def in_hbm(array):
+    return pltpu.with_memory_space_constraint(array, pltpu.HBM)
+
+
+def in_vmem(array):
+    return pltpu.with_memory_space_constraint(array, pltpu.VMEM)
+
+
 def ring_place(index, count):
     if count > 8:
         return index
@@ -26,31 +34,183 @@
     return list(range(0, count, 2)) + list(range(count - 1, 0, -2))
 
 
-def ring_gather(shard, count):
-    order = ring_order(count)
-    ahead = [(order[i], order[(i + 1) % count]) for i in range(count)]
-    back = [(b, a) for a, b in ahead]
-    middle = count // 2
-    half = shard.shape[0] // 2
-    parts = [None] * (count + 1)
-    parts[0] = shard
+def ring_steps(worker_count):
+    order = ring_order(worker_count)
+    ahead = [(order[i], order[(i + 1) % worker_count]) for i in range(worker_count)]
+    return ahead, [(b, a) for a, b in ahead]
+
+
+def ring_near(shard, worker_count, reach):
+    ahead, back = ring_steps(worker_count)
+    parts = {0: shard}
     going, coming = shard, shard
-    for step in range(1, middle):
+    for step in range(1, reach + 1):
         going = lax.ppermute(going, "pairs", ahead)
         coming = lax.ppermute(coming, "pairs", back)
-        parts[count - step] = going
+        parts[worker_count - step] = going
+        parts[step] = coming
+    return parts
+
+
+def ring_far(parts, worker_count, reach):
+    ahead, back = ring_steps(worker_count)
+    middle = worker_count // 2
+    parts = dict(parts)
+    going, coming = parts[worker_count - reach], parts[reach]
+    half = going.shape[0] // 2
+    for step in range(reach + 1, middle):
+        going = lax.ppermute(going, "pairs", ahead)
+        coming = lax.ppermute(coming, "pairs", back)
+        parts[worker_count - step] = going
         parts[step] = coming
     parts[middle] = lax.ppermute(going[:half], "pairs", ahead)
-    parts[count] = lax.ppermute(coming[half:], "pairs", back)
+    parts[worker_count] = lax.ppermute(coming[half:], "pairs", back)
     return parts
+
+
+FIRST = (0, 1, 2, 3, 4, 5, 3, 2)
+SECOND = (4, 5, 3, 2, 0, 1, 2, 3)
+
+
+def deal_kernel(
+    worker_count,
+    image_count,
+    reach,
+    owners,
+    locals_,
+    counts,
+    me,
+    table,
+    first,
+    fits,
+    holder,
+    spot,
+    load,
+    members,
+    parent,
+):
+    share = 3
+    requests = owners.shape[0] // worker_count
+    pairs = worker_count * share
+    everyone = 2**worker_count - 1
+
+    def list_worker(w, r):
+        def list_slot(s, r):
+            first[r] = w * requests + 2 * s
+            return r + 1
+
+        return lax.fori_loop(0, counts[w], list_slot, r)
+
+    lax.fori_loop(0, worker_count, list_worker, 0)
+
+    def near(view):
+        place = ring_place(owners[view], worker_count)
+        turned = (2 ** (2 * reach + 1) - 1) << lax.rem(place + worker_count - reach, worker_count)
+        return (turned | (turned >> worker_count)) & everyone
+
+    def set_pair(r, carry):
+        fits[r] = near(first[r]) & near(first[r] + 1)
+        holder[r] = -1
+        spot[r] = 0
+        return carry
+
+    lax.fori_loop(0, pairs, set_pair, 0)
+    for w in range(worker_count):
+        load[w] = 0
+
+    def put(pair, w, slot):
+        members[w * share + slot] = pair
+        holder[pair] = w
+        spot[pair] = slot
+
+    def match(r, missed):
+        for w in range(worker_count):
+            parent[w] = r
+
+        def searching(state):
+            seen, done, found = state
+            return jnp.logical_and(found < 0, (seen & ~done) != 0)
+
+        def search(state):
+            seen, done, found = state
+            todo = seen & ~done
+            w = jnp.int32(0)
+            for x in range(worker_count - 1, -1, -1):
+                w = jnp.where(((todo >> x) & 1) == 1, jnp.int32(x), w)
+            room = load[w] < share
+            fresh_all = jnp.int32(0)
+            for i in range(share):
+                q = jnp.where(room, r, members[w * share + i])
+                fresh = jnp.where(room, 0, fits[q] & ~(seen | fresh_all))
+                for x in range(worker_count):
+
+                    @pl.when(((fresh >> x) & 1) == 1)
+                    def _():
+                        parent[x] = q
+
+                fresh_all = fresh_all | fresh
+            return seen | fresh_all, done | (1 << w), jnp.where(room, w, found)
+
+        start = (fits[r], jnp.int32(0), jnp.int32(-1))
+        _, _, found = lax.while_loop(searching, search, start)
+
+        @pl.when(found >= 0)
+        def _():
+            def moving(state):
+                return state[0] >= 0
+
+            def move(state):
+                w, slot = state
+                pair = parent[w]
+                after = (holder[pair], spot[pair])
+                put(pair, w, slot)
+                return after
+
+            slot = load[found]
+            load[found] = slot + 1
+            lax.while_loop(moving, move, (found, slot))
+
+        return missed + jnp.where(found < 0, 1, 0)
+
+    for w in range(pairs):
+        members[w] = 0
+    missed = lax.fori_loop(0, pairs, match, jnp.int32(0))
+
+    @pl.when(missed > 0)
+    def _():
+        def place_pair(r, carry):
+            def try_worker(w, carry):
+                @pl.when(jnp.logical_and(holder[r] < 0, load[w] < share))
+                def _():
+                    put(r, w, load[w])
+                    load[w] = load[w] + 1
+
+                return carry
+
+            return lax.fori_loop(0, worker_count, try_worker, carry)
+
+        lax.fori_loop(0, pairs, place_pair, 0)
+
+    core = me[1]
+    here = ring_place(me[0], worker_count)
+    middle, half = worker_count // 2, image_count // 2
+    for column in range(8):
+        place = jnp.where(core == 0, FIRST[column], SECOND[column])
+        view = first[members[here * share + place // 2]] + lax.rem(place, 2)
+        owner, row = owners[view], locals_[view]
+        gap = lax.rem(ring_place(owner, worker_count) - here + worker_count, worker_count)
+        late = jnp.logical_and(gap == middle, row >= half)
+        table[0, column] = jnp.where(late, worker_count, gap)
+        table[1, column] = jnp.where(late, row - half, row)
+        table[2, column] = owner * image_count + row
+        table[3, column] = core
+        table[4, column] = jnp.where(missed == 0, 1, 0)
 
 
 def plan(owners, locals_, counts, worker, core, image_count, worker_count):
     requests = locals_.shape[0] // worker_count
     share = requests // 4
-    first = jnp.array([0, 1, 2, 3, 4, 5, 3, 2], jnp.int32)
-    second = jnp.array([4, 5, 3, 2, 0, 1, 2, 3], jnp.int32)
-    place = jnp.where(core == 0, first, second)
+    place = jnp.where(core == 0, jnp.array(FIRST, jnp.int32), jnp.array(SECOND, jnp.int32))
     pair = worker * share + place // 2
     workers = jnp.arange(worker_count, dtype=jnp.int32)
     upto = jnp.sum(
@@ -73,23 +233,43 @@
     return jnp.stack([part, row, image, head])
 
 
-def fetch(table, column, parts, target, sem, wait):
+def fetch(table, column, keys, parts, target, sem, wait):
     if wait:
         pltpu.make_async_copy(parts[0].at[0], target, sem).wait()
         return
     part, row = table[0, column], table[1, column]
-    for k, source in enumerate(parts):
-
-        @pl.when(part == k)
+    for key, source in zip(keys, parts, strict=True):
+
+        @pl.when(part == key)
         def _():
             pltpu.make_async_copy(source.at[row], target, sem).start()
 
 
-def pick_kernel(count, table, *refs):
-    parts, out, sems = refs[:count], refs[count], refs[count + 1]
+def pick_kernel(keys, table, *refs):
+    parts, (keep, send, sems) = refs[: len(keys)], refs[len(keys) :]
     for wait in (False, True):
         for j in range(4):
-            fetch(table, 4 + j, parts, out.at[j], sems.at[j], wait)
+            fetch(table, 4 + j, keys, parts, send.at[j], sems.at[4 + j], wait)
+            fetch(table, j, keys, parts, keep.at[j], sems.at[j], wait)
+
+
+def pick(table, parts):
+    keys = sorted(parts)
+    hold = in_vmem if len(keys) < 10 else in_hbm
+    space = pltpu.VMEM if len(keys) < 10 else pltpu.HBM
+    _, rows, half = parts[0].shape
+    picked = jax.ShapeDtypeStruct((4, rows, half), BF16)
+    vector = pl.BlockSpec(memory_space=pltpu.VMEM)
+    return pl.pallas_call(
+        functools.partial(pick_kernel, keys),
+        out_shape=(picked, picked),
+        in_specs=[pl.BlockSpec(memory_space=pltpu.SMEM)]
+        + [pl.BlockSpec(memory_space=space)] * len(keys),
+        out_specs=(vector, vector),
+        scratch_shapes=[pltpu.SemaphoreType.DMA((8,))],
+        compiler_params=pltpu.CompilerParams(vmem_limit_bytes=8 * 1024 * 1024),
+        name="pick",
+    )(table, *[hold(parts[key]) for key in keys])
 
 
 def norm_last(rows, gain):
@@ -99,23 +279,16 @@
     return centered * lax.rsqrt(variance + EPS) * gain
 
 
-def decode_kernel(count, tokens, table, *refs):
-    parts = refs[:count]
-    (other, gain_q, gain_c, gain_h, bias_h, wp) = refs[count : count + 6]
-    weights = refs[count + 6 : count + 11]
-    out = refs[count + 11]
-    (mine, theirs, xq, xc, res, q, k, v, att, hid) = refs[count + 12 : count + 22]
-    held = refs[count + 22 : count + 27]
-    sems, wsems, osem = refs[count + 27 :]
+def decode_kernel(tokens, table, *refs):
+    (mine, theirs, gain_q, gain_c, gain_h, bias_h, wp) = refs[:7]
+    weights, out = refs[7:12], refs[12]
+    (xq, xc, res, q, k, v, att, hid) = refs[13:21]
+    held, wsems = refs[21:26], refs[26]
     wq, wk, wv, wo, wh = held
     rows, half = mine.shape[1], mine.shape[2]
     views, padded, width = q.shape
     core = table[3, 0]
 
-    for j in range(4):
-        fetch(table, j, parts, mine.at[j], sems.at[j], False)
-    incoming = pltpu.make_async_copy(other, theirs, osem)
-    incoming.start()
     copies = [
         pltpu.make_async_copy(weights[i], held[i], wsems.at[i]) for i in range(len(weights))
     ]
@@ -127,9 +300,6 @@
     xq[:, rows:, :] = tail
     xc[:, rows:, :] = tail
     res[:, rows:, :] = tail
-    for j in range(4):
-        fetch(table, j, parts, mine.at[j], sems.at[j], True)
-    incoming.wait()
 
     here = pl.ds(pl.multiple_of(core * half, half), half)
     there = pl.ds(pl.multiple_of((1 - core) * half, half), half)
@@ -240,66 +410,64 @@
     views = 3
 
     shard = jnp.pad(tokens, ((0, 0), (0, rows - token_count), (0, 0)))
-    parts = ring_gather(shard, worker_count)
-    table = plan(
-        view_owner[:, 0], view_local, pair_count, worker, core, image_count, worker_count
-    )
-
-    count = len(parts)
-    anywhere = pl.BlockSpec(memory_space=pl.ANY)
+    anywhere = pl.BlockSpec(memory_space=pltpu.HBM)
     scalars = pl.BlockSpec(memory_space=pltpu.SMEM)
     vector = pl.BlockSpec(memory_space=pltpu.VMEM)
-    send = pl.pallas_call(
-        functools.partial(pick_kernel, count),
-        out_shape=jax.ShapeDtypeStruct((4, rows, half), BF16),
-        in_specs=[scalars] + [anywhere] * count,
-        out_specs=anywhere,
-        scratch_shapes=[pltpu.SemaphoreType.DMA((4,))],
-        name="pick",
-    )(table, *parts)
+    owners = view_owner[:, 0]
+    if worker_count == 8:
+        reach = 2
+        pairs = worker_count * views
+        table = pl.pallas_call(
+            functools.partial(deal_kernel, worker_count, image_count, reach),
+            out_shape=jax.ShapeDtypeStruct((5, 8), jnp.int32),
+            in_specs=[scalars] * 4,
+            out_specs=scalars,
+            scratch_shapes=[pltpu.SMEM((pairs,), jnp.int32)] * 4
+            + [pltpu.SMEM((worker_count,), jnp.int32), pltpu.SMEM((pairs,), jnp.int32)]
+            + [pltpu.SMEM((worker_count,), jnp.int32)],
+            compiler_params=pltpu.CompilerParams(vmem_limit_bytes=2 * 1024 * 1024),
+            name="deal",
+        )(owners, view_local, pair_count, jnp.stack([worker, core]))
+        parts = ring_near(shard, worker_count, reach)
+        keep, send = lax.cond(
+            table[4, 0] == 1,
+            lambda near: pick(table, near),
+            lambda near: pick(table, ring_far(near, worker_count, reach)),
+            parts,
+        )
+    else:
+        table = plan(owners, view_local, pair_count, worker, core, image_count, worker_count)
+        parts = ring_far({0: shard, worker_count: shard}, worker_count, 0)
+        keep, send = pick(table, parts)
     other = lax.ppermute(send, "mp", [(0, 1), (1, 0)])
 
+    wide = pltpu.VMEM((views, padded, width), BF16)
+    square = pltpu.VMEM((width, width), BF16)
     flat = pl.pallas_call(
-        functools.partial(decode_kernel, count, token_count),
+        functools.partial(decode_kernel, token_count),
         out_shape=jax.ShapeDtypeStruct((worker_count * image_count, 4, token_count), F32),
-        in_specs=[scalars] + [anywhere] * (count + 1) + [vector] * 5 + [anywhere] * 5,
+        in_specs=[scalars] + [vector] * 7 + [anywhere] * 5,
         out_specs=vector,
-        scratch_shapes=[
-            pltpu.VMEM((4, rows, half), BF16),
-            pltpu.VMEM((4, rows, half), BF16),
-            pltpu.VMEM((views, padded, width), BF16),
-            pltpu.VMEM((views, padded, width), BF16),
-            pltpu.VMEM((views, padded, width), BF16),
-            pltpu.VMEM((views, padded, width), BF16),
-            pltpu.VMEM((views, padded, width), BF16),
-            pltpu.VMEM((views, padded, width), BF16),
-            pltpu.VMEM((views, padded, width), BF16),
-            pltpu.VMEM((views, padded, hidden_width), BF16),
-            pltpu.VMEM((width, width), BF16),
-            pltpu.VMEM((width, width), BF16),
-            pltpu.VMEM((width, width), BF16),
-            pltpu.VMEM((width, width), BF16),
-            pltpu.VMEM((width, hidden_width), BF16),
-            pltpu.SemaphoreType.DMA((4,)),
-            pltpu.SemaphoreType.DMA((5,)),
-            pltpu.SemaphoreType.DMA,
-        ],
-        compiler_params=pltpu.CompilerParams(vmem_limit_bytes=48 * 1024 * 1024),
+        scratch_shapes=[wide] * 7
+        + [pltpu.VMEM((views, padded, hidden_width), BF16)]
+        + [square] * 4
+        + [pltpu.VMEM((width, hidden_width), BF16), pltpu.SemaphoreType.DMA((5,))],
+        compiler_params=pltpu.CompilerParams(vmem_limit_bytes=32 * 1024 * 1024),
         name="decode",
     )(
         table,
-        *parts,
+        keep,
         other,
         gain_query.reshape(1, width),
         gain_context.reshape(1, width),
         gain_head.reshape(1, width),
         hidden_bias.reshape(1, hidden_width),
         point_weight,
-        query_weight,
-        key_weight,
-        value_weight,
-        out_weight,
-        hidden_weight,
+        in_hbm(query_weight),
+        in_hbm(key_weight),
+        in_hbm(value_weight),
+        in_hbm(out_weight),
+        in_hbm(hidden_weight),
     )
     arrived = lax.all_to_all(flat, ("pairs", "mp"), 0, 0, tiled=True)
     mine = image_count // core_count

time: 115 us -> 69.4 us (0.60)
  waiting for transfers between devices: 46.2 us -> 22.7 us
  Pallas kernels: 35.7 us -> 25.2 us
  local copies, waits for them, and re-layouts: 7.8 us -> 1.81 us
  starting transfers between devices: 9.34 us -> 5.24 us
    ppermute x8 -> x4, waiting for transfers between devices: 44.1 us -> 20.6 us  [the longest x2 19.5 us: ring_near(): coming = lax.ppermute(coming, 'pairs', back)]
    pallas_call x2 -> x3, Pallas kernels: 35.7 us -> 25.2 us  [the longest x1 15.6 us: per_device(): pl.pallas_call(functools.partial(decode_kernel, token_count), out_shape=j...]
    unnamed x47 -> x17, local copies, waits for them, and re-layouts: 7.59 us -> 1.22 us
    ppermute x8 -> x4, starting transfers between devices: 9.27 us -> 5.17 us  [the longest x2 4.7 us: ring_near(): coming = lax.ppermute(coming, 'pairs', back)]
  transfers between devices with their start and end apart: 9 -> 5, of which waited for: 6 -> 4; matrix products, arithmetic and copies ran while one was open for 1% -> 1% of each run, Pallas kernels for 0% -> 9%
where the time goes in v2:
time: 69.4 us; the launch traced here: 69.2 us
  Pallas kernels  25.2 us (36%)
  waiting for transfers between devices  22.7 us (33%)
  blocking collectives  12.7 us (18%)
  starting transfers between devices  5.24 us (8%)
  local copies, waits for them, and re-layouts  1.81 us (3%)
  between operations  0.77 us (1%)
  other arithmetic  0.71 us (1%)
    ppermute x2, waiting for transfers between devices, ring_near(): coming = lax.ppermute(coming, 'pairs', back)  19.5 us
    pallas_call x1, Pallas kernels, per_device(): pl.pallas_call(functools.partial(decode_kernel, token_count), out_shape=j...  15.6 us
    all_to_all x1, blocking collectives, per_device(): arrived = lax.all_to_all(flat, ('pairs', 'mp'), 0, 0, tiled=True)  12.7 us
    pallas_call x1, Pallas kernels, per_device(): pl.pallas_call(functools.partial(deal_kernel, worker_count, image_count,...  6.07 us
    ppermute x2, starting transfers between devices, ring_near(): coming = lax.ppermute(coming, 'pairs', back)  4.7 us
    pallas_call x1, Pallas kernels, pick(): pl.pallas_call(functools.partial(pick_kernel, keys), out_shape=(picked, p...  3.52 us
    ppermute x1, waiting for transfers between devices, per_device(): other = lax.ppermute(send, 'mp', [(0, 1), (1, 0)])  2.17 us
  transfers between devices with their start and end apart: 5, of which 4 were waited for; matrix products, arithmetic and copies ran while one was open for 1% of the time, Pallas kernels for 9%

profile of v2, /device:TPU:0, one launch (start us, length us, event | category | flops | bytes accessed | tf_op | source)
XLA Modules:
  0.0 69.2 jit_solution(14927626364339006486)
XLA Ops:
  0.0 0.0 copy-start.2
  0.0 0.0 copy-start.3
  0.0 0.0 copy-start.4
  0.0 1.2 %copy.15 = bf16[4,196,384]{2,1,0:T(8,128)(2,1)S(1)} copy(bf16[4,196,384]{2,0,1:T(4,128)(2,1)} %param.16) | data formatting | bytes 1204224 | tf_op args[0]
  1.2 0.1 pad.4
  1.3 3.0 %collective-permute-start.4 = (bf16[4,200,384]{2,1,0:T(8,128)(2,1)S(1)}, bf16[4,200,384]{2,1,0:T(8,128)(2,1)S(1)}, u32[]{:S(2)}, u32[]{:S(2)}) collective-permute-start(bf16[4,200,384]{2,1,0:T(8,128)(2,1)S(1)} %pad.4), channel_id=1, source_target_pairs={{4,0},{8,4},{12,8},{14,12},{10,14},{6,10},{2,6},{0,2},{5,1},{9,5},... | collective-permute-start | bytes 1843208 | tf_op jit(solution)/shard_map/ppermute | solution.py:49
  4.3 0.1 collective-permute-start.6
  4.4 13.8 %collective-permute-done.4 = bf16[4,200,384]{2,1,0:T(8,128)(2,1)S(1)} collective-permute-done((bf16[4,200,384]{2,1,0:T(8,128)(2,1)S(1)}, bf16[4,200,384]{2,1,0:T(8,128)(2,1)S(1)}, u32[]{:S(2)}, u32[]{:S(2)}) %collective-permute-start.4) | collective-permute-done | bytes 614432 | tf_op jit(solution)/shard_map/ppermute | solution.py:49
  18.2 1.7 %collective-permute-start.5 = (bf16[4,200,384]{2,1,0:T(8,128)(2,1)S(1)}, bf16[4,200,384]{2,1,0:T(8,128)(2,1)S(1)}, u32[]{:S(2)}, u32[]{:S(2)}) collective-permute-start(bf16[4,200,384]{2,1,0:T(8,128)(2,1)S(1)} %collective-permute-done.4), channel_id=1, source_target_pairs={{4,0},{8,4},{12,8},{14,12},{10,14},{6,10},{2,6},{0,2},{5,1},{9,5},... | collective-permute-start | bytes 1843208 | tf_op jit(solution)/shard_map/ppermute | solution.py:49
  19.9 0.0 collective-permute-done.6
  19.9 0.3 collective-permute-start.7
  20.2 0.1 pad_add_fusion.me
  20.3 0.0 copy-done.2
  20.3 0.0 copy-done.3
  20.3 0.0 copy-done.4
  20.3 6.1 %deal.1.table = s32[5,8]{1,0:T(8,128)S(1)} custom-call(s32[96]{0:T(128)S(1)} %bitcast.7, s32[96]{0:T(128)S(1)} %copy-done.3, s32[8]{0:T(128)S(1)} %copy-done.4, s32[2]{0:T(128)S(1)} %pad_add_fusion.me), custom_call_target="tpu_custom_call" | custom-call | tf_op jit(solution)/shard_map/deal/pallas_call | solution.py:420
  26.4 0.5 slice.9
  27.6 5.7 %collective-permute-done.5 = bf16[4,200,384]{2,1,0:T(8,128)(2,1)S(1)} collective-permute-done((bf16[4,200,384]{2,1,0:T(8,128)(2,1)S(1)}, bf16[4,200,384]{2,1,0:T(8,128)(2,1)S(1)}, u32[]{:S(2)}, u32[]{:S(2)}) %collective-permute-start.5) | collective-permute-done | bytes 614432 | tf_op jit(solution)/shard_map/ppermute | solution.py:49
  33.2 1.1 %collective-permute-done.7 = bf16[4,200,384]{2,1,0:T(8,128)(2,1)S(1)} collective-permute-done((bf16[4,200,384]{2,1,0:T(8,128)(2,1)S(1)}, bf16[4,200,384]{2,1,0:T(8,128)(2,1)S(1)}, u32[]{:S(2)}, u32[]{:S(2)}) %collective-permute-start.7) | collective-permute-done | bytes 614432 | tf_op jit(solution)/shard_map/ppermute | solution.py:48
  34.3 0.0 copy-start.1
  34.4 3.5 %conditional.1 = ((bf16[4,200,384]{2,1,0:T(8,128)(2,1)}, bf16[4,200,384]{2,1,0:T(8,128)(2,1)})) conditional(s32[]{:T(128)} %bitcast.3, (bf16[4,200,384]{2,1,0:T(8,128)(2,1)S(1)}, bf16[4,200,384]{2,1,0:T(8,128)(2,1)S(1)}, s32[5,8]{1,0:T(8,128)S(1)}, bf16[4,200,384]{2,1,0:T(8,128)(2,1)S(1)}, bf16[4,200,384]{2,1,0:T(8,128)(2,1)S(1)}, ...), branch_computations={%region_0.1_spmd, %region_1.2_spmd} | conditional | bytes 8601768 | solution.py:432
  34.4 3.5 %pick.3 = (bf16[4,200,384]{2,1,0:T(8,128)(2,1)}, bf16[4,200,384]{2,1,0:T(8,128)(2,1)}) custom-call(s32[5,8]{1,0:T(8,128)S(1)} %get-tuple-element.35.table, bf16[4,200,384]{2,1,0:T(8,128)(2,1)S(1)} %get-tuple-element.36.refs_0_, bf16[4,200,384]{2,1,0:T(8,128)(2,1)S(1)} %get-tuple-element.37.refs_1_, bf16[4,200,384]{2,1,0:T(8,128)(2,1)S(1)} %get-tuple-element.38.refs_2_, ...), custom_call_target="tpu_custom_call" | custom-call | tf_op jit(solution)/shard_map/cond/branch_1_fun/pick/pallas_call | solution.py:263
  37.9 0.1 collective-permute-start.8
  38.0 0.0 copy-done.5
  38.0 0.0 copy-done.6
  38.0 0.0 copy-done.7
  38.0 2.2 %collective-permute-done.8.refs_1_ = bf16[4,200,384]{2,1,0:T(8,128)(2,1)S(1)} collective-permute-done((bf16[4,200,384]{2,1,0:T(8,128)(2,1)}, bf16[4,200,384]{2,1,0:T(8,128)(2,1)S(1)}, u32[]{:S(2)}, u32[]{:S(2)}) %collective-permute-start.8) | collective-permute-done | bytes 614432 | tf_op jit(solution)/shard_map/ppermute | solution.py:442
  40.2 0.0 copy-done
  40.2 0.0 copy-done.1
  40.2 15.6 %decode.1 = f32[32,4,196]{2,1,0:T(4,128)S(1)} custom-call(s32[5,8]{1,0:T(8,128)S(1)} %deal.1.table, bf16[4,200,384]{2,1,0:T(8,128)(2,1)} %get-tuple-element.43.refs_0_, bf16[4,200,384]{2,1,0:T(8,128)(2,1)S(1)} %collective-permute-done.8.refs_1_, f32[1,768]{1,0:T(1,128)S(1)} %reshape.19.refs_2_, f32[1,768]{1,0:T(1,128)S(1)} %reshape.20.refs_3_, ...), custom_call_target="tpu_custom_call" | custom-call | tf_op jit(solution)/shard_map/decode/pallas_call | solution.py:446
  55.8 12.7 %all_to_all.5 = f32[32,4,196]{2,1,0:T(4,128)S(1)} all-to-all(f32[32,4,196]{2,1,0:T(4,128)S(1)} %decode.1), channel_id=1, replica_groups=mesh['groups'=2,'pairs'=8,'mp'=2] {'pairs','mp'}, dimensions={0} | all-to-all | bytes 200704 | tf_op jit(solution)/shard_map/all_to_all | solution.py:472
  68.5 0.6 reduce_sum.9
  (7 shorter events, 0.0 us)
Async XLA Ops:
  0.0 20.3 %copy-start.2 = (s32[96,1]{0,1:T(1,128)S(1)}, s32[96,1]{0,1:T(1,128)}, u32[]{:S(2)}) copy-start(s32[96,1]{0,1:T(1,128)} %param.27) | copy-start | bytes 1156
  0.0 20.3 %copy-start.3 = (s32[96]{0:T(128)S(1)}, s32[96]{0:T(128)}, u32[]{:S(2)}) copy-start(s32[96]{0:T(128)} %locals_.1) | copy-start | bytes 1156
  0.0 20.3 %copy-start.4 = (s32[8]{0:T(128)S(1)}, s32[8]{0:T(128)}, u32[]{:S(2)}) copy-start(s32[8]{0:T(128)} %counts.1) | copy-start | bytes 100
  1.3 16.9 %collective-permute-start.4 = (bf16[4,200,384]{2,1,0:T(8,128)(2,1)S(1)}, bf16[4,200,384]{2,1,0:T(8,128)(2,1)S(1)}, u32[]{:S(2)}, u32[]{:S(2)}) collective-permute-start(bf16[4,200,384]{2,1,0:T(8,128)(2,1)S(1)} %pad.4), channel_id=1, source_target_pairs={{4,0},{8,4},{12,8},{14,12},{10,14},{6,10},{2,6},{0,2},{5,1},{9,5},... | collective-permute-start | bytes 1843208 | tf_op jit(solution)/shard_map/ppermute | solution.py:49
  4.3 15.6 %collective-permute-start.6 = (bf16[4,200,384]{2,1,0:T(8,128)(2,1)S(1)}, bf16[4,200,384]{2,1,0:T(8,128)(2,1)S(1)}, u32[]{:S(2)}, u32[]{:S(2)}) collective-permute-start(bf16[4,200,384]{2,1,0:T(8,128)(2,1)S(1)} %pad.4), channel_id=1, source_target_pairs={{0,4},{4,8},{8,12},{12,14},{14,10},{10,6},{6,2},{2,0},{1,5},{5,9},... | collective-permute-start | bytes 1843208 | tf_op jit(solution)/shard_map/ppermute | solution.py:48
  18.2 15.0 %collective-permute-start.5 = (bf16[4,200,384]{2,1,0:T(8,128)(2,1)S(1)}, bf16[4,200,384]{2,1,0:T(8,128)(2,1)S(1)}, u32[]{:S(2)}, u32[]{:S(2)}) collective-permute-start(bf16[4,200,384]{2,1,0:T(8,128)(2,1)S(1)} %collective-permute-done.4), channel_id=1, source_target_pairs={{4,0},{8,4},{12,8},{14,12},{10,14},{6,10},{2,6},{0,2},{5,1},{9,5},... | collective-permute-start | bytes 1843208 | tf_op jit(solution)/shard_map/ppermute | solution.py:49
  19.9 14.4 %collective-permute-start.7 = (bf16[4,200,384]{2,1,0:T(8,128)(2,1)S(1)}, bf16[4,200,384]{2,1,0:T(8,128)(2,1)S(1)}, u32[]{:S(2)}, u32[]{:S(2)}) collective-permute-start(bf16[4,200,384]{2,1,0:T(8,128)(2,1)S(1)} %collective-permute-done.6), channel_id=1, source_target_pairs={{0,4},{4,8},{8,12},{12,14},{14,10},{10,6},{6,2},{2,0},{1,5},{5,9},... | collective-permute-start | bytes 1843208 | tf_op jit(solution)/shard_map/ppermute | solution.py:48
  34.3 3.6 %copy-start.5 = (f32[768]{0:T(1024)S(1)}, f32[768]{0:T(1024)}, u32[]{:S(2)}) copy-start(f32[768]{0:T(1024)} %param.17) | copy-start | bytes 9220
  34.3 3.7 %copy-start.6 = (f32[768]{0:T(1024)S(1)}, f32[768]{0:T(1024)}, u32[]{:S(2)}) copy-start(f32[768]{0:T(1024)} %param.18) | copy-start | bytes 9220
  34.3 3.7 %copy-start.7 = (f32[768]{0:T(1024)S(1)}, f32[768]{0:T(1024)}, u32[]{:S(2)}) copy-start(f32[768]{0:T(1024)} %param.23) | copy-start | bytes 9220
  34.3 5.9 %copy-start = (bf16[4,1024]{1,0:T(4,128)(2,1)S(1)}, bf16[4,1024]{1,0:T(4,128)(2,1)}, u32[]{:S(2)}) copy-start(bf16[4,1024]{1,0:T(4,128)(2,1)} %refs_6_.1) | copy-start | bytes 24580
  34.3 5.9 %copy-start.1 = (f32[1024]{0:T(1024)S(1)}, f32[1024]{0:T(1024)}, u32[]{:S(2)}) copy-start(f32[1024]{0:T(1024)} %param.25) | copy-start | bytes 12292
  37.9 2.3 %collective-permute-start.8 = (bf16[4,200,384]{2,1,0:T(8,128)(2,1)}, bf16[4,200,384]{2,1,0:T(8,128)(2,1)S(1)}, u32[]{:S(2)}, u32[]{:S(2)}) collective-permute-start(bf16[4,200,384]{2,1,0:T(8,128)(2,1)} %get-tuple-element.44), channel_id=1, source_target_pairs={{0,1},{1,0},{2,3},{3,2},{4,5},{5,4},{6,7},{7,6},{8,9},{9,8},{10,11... | collective-permute-start | bytes 1843208 | tf_op jit(solution)/shard_map/ppermute | solution.py:442

commit v3 on v2

--- a/solution.py
+++ b/solution.py
@@ -245,31 +245,61 @@
             pltpu.make_async_copy(source.at[row], target, sem).start()
 
 
-def pick_kernel(keys, table, *refs):
-    parts, (keep, send, sems) = refs[: len(keys)], refs[len(keys) :]
+def pick_kernel(keys, first_column, table, *refs):
+    parts, (out, sems) = refs[: len(keys)], refs[-2:]
     for wait in (False, True):
         for j in range(4):
-            fetch(table, 4 + j, keys, parts, send.at[j], sems.at[4 + j], wait)
-            fetch(table, j, keys, parts, keep.at[j], sems.at[j], wait)
-
-
-def pick(table, parts):
+            fetch(table, first_column + j, keys, parts, out.at[j], sems.at[j], wait)
+
+
+def pick(table, parts, first_column, held):
     keys = sorted(parts)
     hold = in_vmem if len(keys) < 10 else in_hbm
     space = pltpu.VMEM if len(keys) < 10 else pltpu.HBM
     _, rows, half = parts[0].shape
-    picked = jax.ShapeDtypeStruct((4, rows, half), BF16)
-    vector = pl.BlockSpec(memory_space=pltpu.VMEM)
     return pl.pallas_call(
-        functools.partial(pick_kernel, keys),
-        out_shape=(picked, picked),
+        functools.partial(pick_kernel, keys, first_column),
+        out_shape=jax.ShapeDtypeStruct((4, rows, half), BF16),
         in_specs=[pl.BlockSpec(memory_space=pltpu.SMEM)]
-        + [pl.BlockSpec(memory_space=space)] * len(keys),
-        out_specs=(vector, vector),
-        scratch_shapes=[pltpu.SemaphoreType.DMA((8,))],
+        + [pl.BlockSpec(memory_space=space)] * len(keys)
+        + [pl.BlockSpec(memory_space=pltpu.VMEM)] * len(held),
+        out_specs=pl.BlockSpec(memory_space=pltpu.VMEM),
+        scratch_shapes=[pltpu.SemaphoreType.DMA((4,))],
         compiler_params=pltpu.CompilerParams(vmem_limit_bytes=8 * 1024 * 1024),
+        cost_estimate=pl.CostEstimate(
+            flops=0, bytes_accessed=16 * rows * half, transcendentals=0
+        ),
         name="pick",
-    )(table, *[hold(parts[key]) for key in keys])
+    )(table, *[hold(parts[key]) for key in keys], *[in_vmem(array) for array in held])
+
+
+def stage_kernel(count, *refs):
+    sources, targets, sems = refs[:count], refs[count : 2 * count], refs[2 * count]
+    copies = [pltpu.make_async_copy(sources[i], targets[i], sems.at[i]) for i in range(count)]
+    for copy in copies:
+        copy.start()
+    for copy in copies:
+        copy.wait()
+
+
+def stage(arrays):
+    count = len(arrays)
+    size = sum(array.size * array.dtype.itemsize for array in arrays)
+    return pl.pallas_call(
+        functools.partial(stage_kernel, count),
+        out_shape=tuple(jax.ShapeDtypeStruct(array.shape, array.dtype) for array in arrays),
+        in_specs=[pl.BlockSpec(memory_space=pltpu.HBM)] * count,
+        out_specs=(pl.BlockSpec(memory_space=pltpu.VMEM),) * count,
+        scratch_shapes=[pltpu.SemaphoreType.DMA((count,))],
+        compiler_params=pltpu.CompilerParams(vmem_limit_bytes=16 * 1024 * 1024),
+        cost_estimate=pl.CostEstimate(flops=0, bytes_accessed=2 * size, transcendentals=0),
+        name="stage",
+    )(*[in_hbm(array) for array in arrays])
+
+
+def gather_images(table, parts, held):
+    other = lax.ppermute(pick(table, parts, 4, held), "mp", [(0, 1), (1, 0)])
+    return pick(table, parts, 0, held), other
 
 
 def norm_last(rows, gain):
@@ -281,19 +311,12 @@
 
 def decode_kernel(tokens, table, *refs):
     (mine, theirs, gain_q, gain_c, gain_h, bias_h, wp) = refs[:7]
-    weights, out = refs[7:12], refs[12]
-    (xq, xc, res, q, k, v, att, hid) = refs[13:21]
-    held, wsems = refs[21:26], refs[26]
-    wq, wk, wv, wo, wh = held
+    wq, wk, wv, wo, wh = refs[7:12]
+    out = refs[12]
+    (xq, xc, res, q, k, v, att, hid) = refs[13:]
     rows, half = mine.shape[1], mine.shape[2]
     views, padded, width = q.shape
     core = table[3, 0]
-
-    copies = [
-        pltpu.make_async_copy(weights[i], held[i], wsems.at[i]) for i in range(len(weights))
-    ]
-    for copy in copies:
-        copy.start()
 
     out[...] = jnp.zeros_like(out)
     tail = jnp.zeros((views, padded - rows, width), BF16)
@@ -329,13 +352,10 @@
     head_size = width // HEADS
     queries = xq[...].reshape(total, width)
     contexts = xc[...].reshape(total, width)
-    copies[0].wait()
     proj = jnp.dot(queries, wq[...], preferred_element_type=F32)
     q[...] = (proj.astype(BF16) * BF16(head_size**-0.5)).reshape(views, padded, width)
-    copies[1].wait()
     proj = jnp.dot(contexts, wk[...], preferred_element_type=F32)
     k[...] = proj.astype(BF16).reshape(views, padded, width)
-    copies[2].wait()
     proj = jnp.dot(contexts, wv[...], preferred_element_type=F32)
     v[...] = proj.astype(BF16).reshape(views, padded, width)
 
@@ -365,11 +385,9 @@
 
     lax.fori_loop(0, views, attend, 0)
 
-    copies[3].wait()
     updated = jnp.dot(att[...].reshape(total, width), wo[...], preferred_element_type=F32)
     updated = updated + res[...].reshape(total, width).astype(F32)
     head_in = norm_last(updated, gain_h[...]).astype(BF16)
-    copies[4].wait()
     hidden = jnp.dot(head_in, wh[...], preferred_element_type=F32) + bias_h[...]
     hid[...] = jax.nn.gelu(hidden).astype(BF16).reshape(views, padded, hid.shape[2])
     for i in range(views):
@@ -410,10 +428,31 @@
     views = 3
 
     shard = jnp.pad(tokens, ((0, 0), (0, rows - token_count), (0, 0)))
-    anywhere = pl.BlockSpec(memory_space=pltpu.HBM)
     scalars = pl.BlockSpec(memory_space=pltpu.SMEM)
     vector = pl.BlockSpec(memory_space=pltpu.VMEM)
     owners = view_owner[:, 0]
+    weights = stage((query_weight, key_weight, value_weight, out_weight, hidden_weight))
+    vectors = (
+        gain_query.reshape(1, width),
+        gain_context.reshape(1, width),
+        gain_head.reshape(1, width),
+        hidden_bias.reshape(1, hidden_width),
+        point_weight,
+    )
+    wide = pltpu.VMEM((views, padded, width), BF16)
+
+    def decode(table, parts, vectors, weights):
+        keep, other = gather_images(table, parts, weights)
+        return pl.pallas_call(
+            functools.partial(decode_kernel, token_count),
+            out_shape=jax.ShapeDtypeStruct((worker_count * image_count, 4, token_count), F32),
+            in_specs=[scalars] + [vector] * 12,
+            out_specs=vector,
+            scratch_shapes=[wide] * 7 + [pltpu.VMEM((views, padded, hidden_width), BF16)],
+            compiler_params=pltpu.CompilerParams(vmem_limit_bytes=32 * 1024 * 1024),
+            name="decode",
+        )(table, in_vmem(keep), in_vmem(other), *vectors, *[in_vmem(w) for w in weights])
+
     if worker_count == 8:
         reach = 2
         pairs = worker_count * views
@@ -426,49 +465,25 @@
             + [pltpu.SMEM((worker_count,), jnp.int32), pltpu.SMEM((pairs,), jnp.int32)]
             + [pltpu.SMEM((worker_count,), jnp.int32)],
             compiler_params=pltpu.CompilerParams(vmem_limit_bytes=2 * 1024 * 1024),
+            cost_estimate=pl.CostEstimate(flops=0, bytes_accessed=20 * 10**6, transcendentals=0),
             name="deal",
         )(owners, view_local, pair_count, jnp.stack([worker, core]))
         parts = ring_near(shard, worker_count, reach)
-        keep, send = lax.cond(
+        flat = lax.cond(
             table[4, 0] == 1,
-            lambda near: pick(table, near),
-            lambda near: pick(table, ring_far(near, worker_count, reach)),
+            decode,
+            lambda table, near, *rest: decode(
+                table, ring_far(near, worker_count, reach), *rest
+            ),
+            table,
             parts,
+            vectors,
+            weights,
         )
     else:
         table = plan(owners, view_local, pair_count, worker, core, image_count, worker_count)
         parts = ring_far({0: shard, worker_count: shard}, worker_count, 0)
-        keep, send = pick(table, parts)
-    other = lax.ppermute(send, "mp", [(0, 1), (1, 0)])
-
-    wide = pltpu.VMEM((views, padded, width), BF16)
-    square = pltpu.VMEM((width, width), BF16)
-    flat = pl.pallas_call(
-        functools.partial(decode_kernel, token_count),
-        out_shape=jax.ShapeDtypeStruct((worker_count * image_count, 4, token_count), F32),
-        in_specs=[scalars] + [vector] * 7 + [anywhere] * 5,
-        out_specs=vector,
-        scratch_shapes=[wide] * 7
-        + [pltpu.VMEM((views, padded, hidden_width), BF16)]
-        + [square] * 4
-        + [pltpu.VMEM((width, hidden_width), BF16), pltpu.SemaphoreType.DMA((5,))],
-        compiler_params=pltpu.CompilerParams(vmem_limit_bytes=32 * 1024 * 1024),
-        name="decode",
-    )(
-        table,
-        keep,
-        other,
-        gain_query.reshape(1, width),
-        gain_context.reshape(1, width),
-        gain_head.reshape(1, width),
-        hidden_bias.reshape(1, hidden_width),
-        point_weight,
-        in_hbm(query_weight),
-        in_hbm(key_weight),
-        in_hbm(value_weight),
-        in_hbm(out_weight),
-        in_hbm(hidden_weight),
-    )
+        flat = decode(table, parts, vectors, weights)
     arrived = lax.all_to_all(flat, ("pairs", "mp"), 0, 0, tiled=True)
     mine = image_count // core_count
     return jnp.sum(arrived.reshape(worker_count * core_count, mine, 4, token_count), axis=0)

time: 69.4 us -> 66.9 us (0.964)
  waiting for transfers between devices: 22.7 us -> 17.1 us
  Pallas kernels: 25.2 us -> 28.1 us
    ppermute x2, waiting for transfers between devices: 19.5 us -> 1.2 us  [ring_near(): coming = lax.ppermute(coming, 'pairs', back)]
    ppermute x2, waiting for transfers between devices: 1.09 us -> 15.9 us  [ring_near(): going = lax.ppermute(going, 'pairs', ahead)]
    ppermute x2, starting transfers between devices: 4.7 us -> 0.24 us  [ring_near(): coming = lax.ppermute(coming, 'pairs', back)]
    ppermute x2, starting transfers between devices: 0.47 us -> 4.87 us  [ring_near(): going = lax.ppermute(going, 'pairs', ahead)]
    ppermute x1, waiting for transfers between devices: 2.17 us -> 0.01 us  [gather_images(): other = lax.ppermute(pick(table, parts, 4, held), 'mp', [(0, 1), (1, 0)])]
    pallas_call x2 -> x4, Pallas kernels: 19.1 us -> 20.9 us  [the longest x1 12.7 us: decode(): pl.pallas_call(functools.partial(decode_kernel, token_count), out_shape=j...]
    pallas_call x1, Pallas kernels: 6.07 us -> 7.12 us  [per_device(): pl.pallas_call(functools.partial(deal_kernel, worker_count, image_count,...]
  transfers between devices with their start and end apart: 5 -> 5, of which waited for: 4 -> 3; matrix products, arithmetic and copies ran while one was open for 1% -> 1% of each run, Pallas kernels for 9% -> 19%
where the time goes in v3:
time: 66.9 us; the launch traced here: 66.7 us
  Pallas kernels  28.1 us (42%)
  waiting for transfers between devices  17.1 us (26%)
  blocking collectives  12.8 us (19%)
  starting transfers between devices  5.18 us (8%)
  local copies, waits for them, and re-layouts  1.84 us (3%)
  between operations  0.76 us (1%)
  other arithmetic  0.72 us (1%)
    ppermute x2, waiting for transfers between devices, ring_near(): going = lax.ppermute(going, 'pairs', ahead)  15.9 us
    all_to_all x1, blocking collectives, per_device(): arrived = lax.all_to_all(flat, ('pairs', 'mp'), 0, 0, tiled=True)  12.8 us
    pallas_call x1, Pallas kernels, decode(): pl.pallas_call(functools.partial(decode_kernel, token_count), out_shape=j...  12.7 us
    pallas_call x1, Pallas kernels, per_device(): pl.pallas_call(functools.partial(deal_kernel, worker_count, image_count,...  7.12 us
    pallas_call x2, Pallas kernels, pick(): pl.pallas_call(functools.partial(pick_kernel, keys, first_column), out_sh...  5.32 us
    ppermute x2, starting transfers between devices, ring_near(): going = lax.ppermute(going, 'pairs', ahead)  4.87 us
    pallas_call x1, Pallas kernels, stage(): pl.pallas_call(functools.partial(stage_kernel, count), out_shape=tuple((j...  2.89 us
  transfers between devices with their start and end apart: 5, of which 3 were waited for; matrix products, arithmetic and copies ran while one was open for 1% of the time, Pallas kernels for 19%

profile of v3, /device:TPU:0, one launch (start us, length us, event | category | flops | bytes accessed | tf_op | source)
XLA Modules:
  0.0 66.7 jit_solution(6799791905107824490)
XLA Ops:
  0.0 0.0 copy-start
  0.0 1.2 %copy.15 = bf16[4,196,384]{2,1,0:T(8,128)(2,1)S(1)} copy(bf16[4,196,384]{2,0,1:T(4,128)(2,1)} %param.16) | data formatting | bytes 1204224 | tf_op args[0]
  1.2 0.1 pad.4
  1.3 3.1 %collective-permute-start.8 = (bf16[4,200,384]{2,1,0:T(8,128)(2,1)S(1)}, bf16[4,200,384]{2,1,0:T(8,128)(2,1)}, u32[]{:S(2)}, u32[]{:S(2)}) collective-permute-start(bf16[4,200,384]{2,1,0:T(8,128)(2,1)S(1)} %pad.4), channel_id=1, source_target_pairs={{0,4},{4,8},{8,12},{12,14},{14,10},{10,6},{6,2},{2,0},{1,5},{5,9},... | collective-permute-start | bytes 1843208 | tf_op jit(solution)/shard_map/ppermute | solution.py:48
  4.4 0.0 collective-permute-start.6
  4.4 13.9 %collective-permute-done.8 = bf16[4,200,384]{2,1,0:T(8,128)(2,1)} collective-permute-done((bf16[4,200,384]{2,1,0:T(8,128)(2,1)S(1)}, bf16[4,200,384]{2,1,0:T(8,128)(2,1)}, u32[]{:S(2)}, u32[]{:S(2)}) %collective-permute-start.8) | collective-permute-done | bytes 614432 | tf_op jit(solution)/shard_map/ppermute | solution.py:48
  18.3 1.8 %collective-permute-start.9 = (bf16[4,200,384]{2,1,0:T(8,128)(2,1)}, bf16[4,200,384]{2,1,0:T(8,128)(2,1)}, u32[]{:S(2)}, u32[]{:S(2)}) collective-permute-start(bf16[4,200,384]{2,1,0:T(8,128)(2,1)} %collective-permute-done.8), channel_id=1, source_target_pairs={{0,4},{4,8},{8,12},{12,14},{14,10},{10,6},{6,2},{2,0},{1,5},{5,9},... | collective-permute-start | bytes 1843208 | tf_op jit(solution)/shard_map/ppermute | solution.py:48
  20.1 0.0 collective-permute-done.6
  20.1 0.2 collective-permute-start.7
  20.3 0.0 copy-done.5
  20.3 0.0 copy-done.6
  20.4 0.0 copy-done.7
  20.4 0.1 pad_add_fusion.me
  20.5 0.0 copy-done.2
  20.5 0.0 copy-done.1
  20.5 0.0 copy-done
  20.5 7.1 %deal.1 = s32[5,8]{1,0:T(8,128)S(1)} custom-call(s32[96]{0:T(128)S(1)} %bitcast.6, s32[96]{0:T(128)S(1)} %copy-done.1, s32[8]{0:T(128)S(1)} %copy-done.2, s32[2]{0:T(128)S(1)} %pad_add_fusion.me), custom_call_target="tpu_custom_call" | custom-call | bytes 20000000 | tf_op jit(solution)/shard_map/deal/pallas_call | solution.py:459
  27.6 0.5 slice.9
  28.8 0.0 copy-start.3
  28.8 0.0 copy-start.4
  28.8 2.9 %stage.1 = (bf16[768,768]{1,0:T(8,128)(2,1)S(1)}, bf16[768,768]{1,0:T(8,128)(2,1)S(1)}, bf16[768,768]{1,0:T(8,128)(2,1)S(1)}, bf16[768,768]{1,0:T(8,128)(2,1)S(1)}, bf16[768,1024]{1,0:T(8,128)(2,1)S(1)}) custom-call(bf16[768,768]{1,0:T(8,128)(2,1)} %refs_0_.1, bf16[768,768]{1,0:T(8,128)(2,1)} %refs_1_.1, bf16[768,768]{1,0:T(8,128)(2,1)} %refs_2_.1, ...), custom_call_target="tpu_custom_call" | custom-call | bytes 12582912 | tf_op jit(solution)/shard_map/stage/pallas_call | solution.py:288
  31.7 2.0 %collective-permute-done.9 = bf16[4,200,384]{2,1,0:T(8,128)(2,1)} collective-permute-done((bf16[4,200,384]{2,1,0:T(8,128)(2,1)}, bf16[4,200,384]{2,1,0:T(8,128)(2,1)}, u32[]{:S(2)}, u32[]{:S(2)}) %collective-permute-start.9) | collective-permute-done | bytes 614432 | tf_op jit(solution)/shard_map/ppermute | solution.py:48
  33.7 1.2 %collective-permute-done.7 = bf16[4,200,384]{2,1,0:T(8,128)(2,1)} collective-permute-done((bf16[4,200,384]{2,1,0:T(8,128)(2,1)}, bf16[4,200,384]{2,1,0:T(8,128)(2,1)}, u32[]{:S(2)}, u32[]{:S(2)}) %collective-permute-start.7) | collective-permute-done | bytes 614432 | tf_op jit(solution)/shard_map/ppermute | solution.py:49
  34.9 0.0 copy-done.3
  34.9 18.4 %conditional.1 = (f32[32,4,196]{2,1,0:T(4,128)S(1)}) conditional(s32[]{:T(128)} %bitcast.3, (bf16[4,200,384]{2,1,0:T(8,128)(2,1)}, bf16[4,200,384]{2,1,0:T(8,128)(2,1)}, s32[5,8]{1,0:T(8,128)S(1)}, bf16[4,200,384]{2,1,0:T(8,128)(2,1)S(1)}, bf16[4,200,384]{2,1,0:T(8,128)(2,1)}, /*index=5*/bf16[4,200,384]{2,1,0:T(8,128)(2,1)}, ...), branch_computations={%region_0.1_spmd, %region_1.2_spmd} | conditional | bytes 13517008 | solution.py:472
  34.9 2.6 %pick.7 = bf16[4,200,384]{2,1,0:T(8,128)(2,1)S(1)} custom-call(s32[5,8]{1,0:T(8,128)S(1)} %get-tuple-element.88.table, bf16[4,200,384]{2,1,0:T(8,128)(2,1)S(1)} %get-tuple-element.89.refs_0_, bf16[4,200,384]{2,1,0:T(8,128)(2,1)} %get-tuple-element.90.refs_1_, bf16[4,200,384]{2,1,0:T(8,128)(2,1)} %get-tuple-element.91.refs_2_, ...), custom_call_target="tpu_custom_call" | custom-call | bytes 1228800 | tf_op jit(solution)/shard_map/cond/branch_1_fun/pick/pallas_call | solution.py:260
  37.4 0.1 collective-permute-start.5
  37.5 2.8 %pick.6.refs_0_ = bf16[4,200,384]{2,1,0:T(8,128)(2,1)S(1)} custom-call(s32[5,8]{1,0:T(8,128)S(1)} %get-tuple-element.88.table, bf16[4,200,384]{2,1,0:T(8,128)(2,1)S(1)} %get-tuple-element.89.refs_0_, bf16[4,200,384]{2,1,0:T(8,128)(2,1)} %get-tuple-element.90.refs_1_, bf16[4,200,384]{2,1,0:T(8,128)(2,1)} %get-tuple-element.91.refs_2_, ...), custom_call_target="tpu_custom_call" | custom-call | bytes 1228800 | tf_op jit(solution)/shard_map/cond/branch_1_fun/pick/pallas_call | solution.py:260
  40.3 0.0 collective-permute-done.5.refs_1_
  40.3 12.7 %decode.3 = f32[32,4,196]{2,1,0:T(4,128)S(1)} custom-call(s32[5,8]{1,0:T(8,128)S(1)} %get-tuple-element.88.table, bf16[4,200,384]{2,1,0:T(8,128)(2,1)S(1)} %pick.6.refs_0_, bf16[4,200,384]{2,1,0:T(8,128)(2,1)S(1)} %collective-permute-done.5.refs_1_, f32[1,768]{1,0:T(1,128)S(1)} %get-tuple-element.99.refs_2_, f32[1,768]{1,0:T(1,128)S(1)} %get-tuple-element.100.refs_3_, ...), custom_call_target="tpu_custom_call" | custom-call | tf_op jit(solution)/shard_map/cond/branch_1_fun/decode/pallas_call | solution.py:446
  53.2 12.8 %all_to_all.5 = f32[32,4,196]{2,1,0:T(4,128)S(1)} all-to-all(f32[32,4,196]{2,1,0:T(4,128)S(1)} %get-tuple-element.114), channel_id=1, replica_groups=mesh['groups'=2,'pairs'=8,'mp'=2] {'pairs','mp'}, dimensions={0} | all-to-all | bytes 200704 | tf_op jit(solution)/shard_map/all_to_all | solution.py:487
  66.0 0.6 reduce_sum.9
  (9 shorter events, 0.0 us)
Async XLA Ops:
  0.0 20.3 %copy-start.5 = (f32[768]{0:T(1024)S(1)}, f32[768]{0:T(1024)}, u32[]{:S(2)}) copy-start(f32[768]{0:T(1024)} %param.17) | copy-start | bytes 9220
  0.0 20.3 %copy-start.6 = (f32[768]{0:T(1024)S(1)}, f32[768]{0:T(1024)}, u32[]{:S(2)}) copy-start(f32[768]{0:T(1024)} %param.18) | copy-start | bytes 9220
  0.0 20.3 %copy-start.7 = (f32[768]{0:T(1024)S(1)}, f32[768]{0:T(1024)}, u32[]{:S(2)}) copy-start(f32[768]{0:T(1024)} %param.23) | copy-start | bytes 9220
  0.0 20.4 %copy-start.2 = (s32[8]{0:T(128)S(1)}, s32[8]{0:T(128)}, u32[]{:S(2)}) copy-start(s32[8]{0:T(128)} %counts.1) | copy-start | bytes 100
  0.0 20.4 %copy-start.1 = (s32[96]{0:T(128)S(1)}, s32[96]{0:T(128)}, u32[]{:S(2)}) copy-start(s32[96]{0:T(128)} %locals_.1) | copy-start | bytes 1156
  0.0 20.4 %copy-start = (s32[96,1]{0,1:T(1,128)S(1)}, s32[96,1]{0,1:T(1,128)}, u32[]{:S(2)}) copy-start(s32[96,1]{0,1:T(1,128)} %param.27) | copy-start | bytes 1156
  1.3 17.0 %collective-permute-start.8 = (bf16[4,200,384]{2,1,0:T(8,128)(2,1)S(1)}, bf16[4,200,384]{2,1,0:T(8,128)(2,1)}, u32[]{:S(2)}, u32[]{:S(2)}) collective-permute-start(bf16[4,200,384]{2,1,0:T(8,128)(2,1)S(1)} %pad.4), channel_id=1, source_target_pairs={{0,4},{4,8},{8,12},{12,14},{14,10},{10,6},{6,2},{2,0},{1,5},{5,9},... | collective-permute-start | bytes 1843208 | tf_op jit(solution)/shard_map/ppermute | solution.py:48
  4.4 15.7 %collective-permute-start.6 = (bf16[4,200,384]{2,1,0:T(8,128)(2,1)S(1)}, bf16[4,200,384]{2,1,0:T(8,128)(2,1)}, u32[]{:S(2)}, u32[]{:S(2)}) collective-permute-start(bf16[4,200,384]{2,1,0:T(8,128)(2,1)S(1)} %pad.4), channel_id=1, source_target_pairs={{4,0},{8,4},{12,8},{14,12},{10,14},{6,10},{2,6},{0,2},{5,1},{9,5},... | collective-permute-start | bytes 1843208 | tf_op jit(solution)/shard_map/ppermute | solution.py:49
  18.3 15.4 %collective-permute-start.9 = (bf16[4,200,384]{2,1,0:T(8,128)(2,1)}, bf16[4,200,384]{2,1,0:T(8,128)(2,1)}, u32[]{:S(2)}, u32[]{:S(2)}) collective-permute-start(bf16[4,200,384]{2,1,0:T(8,128)(2,1)} %collective-permute-done.8), channel_id=1, source_target_pairs={{0,4},{4,8},{8,12},{12,14},{14,10},{10,6},{6,2},{2,0},{1,5},{5,9},... | collective-permute-start | bytes 1843208 | tf_op jit(solution)/shard_map/ppermute | solution.py:48
  20.1 14.8 %collective-permute-start.7 = (bf16[4,200,384]{2,1,0:T(8,128)(2,1)}, bf16[4,200,384]{2,1,0:T(8,128)(2,1)}, u32[]{:S(2)}, u32[]{:S(2)}) collective-permute-start(bf16[4,200,384]{2,1,0:T(8,128)(2,1)} %collective-permute-done.6), channel_id=1, source_target_pairs={{4,0},{8,4},{12,8},{14,12},{10,14},{6,10},{2,6},{0,2},{5,1},{9,5},... | collective-permute-start | bytes 1843208 | tf_op jit(solution)/shard_map/ppermute | solution.py:49
  28.8 6.1 %copy-start.3 = (bf16[4,1024]{1,0:T(4,128)(2,1)S(1)}, bf16[4,1024]{1,0:T(4,128)(2,1)}, u32[]{:S(2)}) copy-start(bf16[4,1024]{1,0:T(4,128)(2,1)} %param.26) | copy-start | bytes 24580
  28.8 6.1 %copy-start.4 = (f32[1024]{0:T(1024)S(1)}, f32[1024]{0:T(1024)}, u32[]{:S(2)}) copy-start(f32[1024]{0:T(1024)} %param.25) | copy-start | bytes 12292
  37.4 2.8 %collective-permute-start.5 = (bf16[4,200,384]{2,1,0:T(8,128)(2,1)S(1)}, bf16[4,200,384]{2,1,0:T(8,128)(2,1)S(1)}, u32[]{:S(2)}, u32[]{:S(2)}) collective-permute-start(bf16[4,200,384]{2,1,0:T(8,128)(2,1)S(1)} %pick.7), channel_id=1, source_target_pairs={{0,1},{1,0},{2,3},{3,2},{4,5},{5,4},{6,7},{7,6},{8,9},{9,8},{10,11... | collective-permute-start | bytes 1843208 | tf_op jit(solution)/shard_map/cond/branch_1_fun/ppermute | solution.py:301

commit v4 on v3

--- a/solution.py
+++ b/solution.py
@@ -70,6 +70,9 @@
 
 FIRST = (0, 1, 2, 3, 4, 5, 3, 2)
 SECOND = (4, 5, 3, 2, 0, 1, 2, 3)
+SHARE = 3
+MOST = 4
+LEVEL = 5
 
 
 def deal_kernel(
@@ -89,9 +92,8 @@
     members,
     parent,
 ):
-    share = 3
     requests = owners.shape[0] // worker_count
-    pairs = worker_count * share
+    pairs = worker_count * SHARE
     everyone = 2**worker_count - 1
 
     def list_worker(w, r):
@@ -117,13 +119,15 @@
     lax.fori_loop(0, pairs, set_pair, 0)
     for w in range(worker_count):
         load[w] = 0
+        for x in range(MOST):
+            members[w * MOST + x] = 0
 
     def put(pair, w, slot):
-        members[w * share + slot] = pair
+        members[w * MOST + slot] = pair
         holder[pair] = w
         spot[pair] = slot
 
-    def match(r, missed):
+    def match(most, r):
         for w in range(worker_count):
             parent[w] = r
 
@@ -137,10 +141,10 @@
             w = jnp.int32(0)
             for x in range(worker_count - 1, -1, -1):
                 w = jnp.where(((todo >> x) & 1) == 1, jnp.int32(x), w)
-            room = load[w] < share
+            room = load[w] < most
             fresh_all = jnp.int32(0)
-            for i in range(share):
-                q = jnp.where(room, r, members[w * share + i])
+            for i in range(most):
+                q = jnp.where(room, r, members[w * MOST + i])
                 fresh = jnp.where(room, 0, fits[q] & ~(seen | fresh_all))
                 for x in range(worker_count):
 
@@ -170,41 +174,61 @@
             load[found] = slot + 1
             lax.while_loop(moving, move, (found, slot))
 
-        return missed + jnp.where(found < 0, 1, 0)
-
-    for w in range(pairs):
-        members[w] = 0
-    missed = lax.fori_loop(0, pairs, match, jnp.int32(0))
+        return jnp.where(found < 0, 1, 0)
+
+    missed = lax.fori_loop(0, pairs, lambda r, m: m + match(SHARE, r), jnp.int32(0))
+    table[LEVEL, 0] = jnp.where(missed > 0, 1, 0)
 
     @pl.when(missed > 0)
     def _():
-        def place_pair(r, carry):
-            def try_worker(w, carry):
-                @pl.when(jnp.logical_and(holder[r] < 0, load[w] < share))
-                def _():
-                    put(r, w, load[w])
-                    load[w] = load[w] + 1
-
-                return carry
-
-            return lax.fori_loop(0, worker_count, try_worker, carry)
-
-        lax.fori_loop(0, pairs, place_pair, 0)
+        def again(r, left):
+            lost = jnp.where(holder[r] < 0, 1, 0)
+
+            @pl.when(lost == 1)
+            def _():
+                match(MOST, r)
+
+            return left + jnp.where(holder[r] < 0, 1, 0)
+
+        left = lax.fori_loop(0, pairs, again, jnp.int32(0))
+
+        @pl.when(left > 0)
+        def _():
+            table[LEVEL, 0] = 2
+
+            def place_pair(r, carry):
+                def try_worker(w, carry):
+                    @pl.when(jnp.logical_and(holder[r] < 0, load[w] < MOST))
+                    def _():
+                        put(r, w, load[w])
+                        load[w] = load[w] + 1
+
+                    return carry
+
+                return lax.fori_loop(0, worker_count, try_worker, carry)
+
+            lax.fori_loop(0, pairs, place_pair, 0)
 
     core = me[1]
     here = ring_place(me[0], worker_count)
     middle, half = worker_count // 2, image_count // 2
+    narrow = table[LEVEL, 0] == 0
     for column in range(8):
         place = jnp.where(core == 0, FIRST[column], SECOND[column])
-        view = first[members[here * share + place // 2]] + lax.rem(place, 2)
+        wide_place = jnp.where(core == 0, column, (column + 4) % 8)
+        place = jnp.where(narrow, place, wide_place)
+        slot = place // 2
+        used = slot < load[here]
+        view = first[members[here * MOST + slot]] + lax.rem(place, 2)
         owner, row = owners[view], locals_[view]
         gap = lax.rem(ring_place(owner, worker_count) - here + worker_count, worker_count)
         late = jnp.logical_and(gap == middle, row >= half)
-        table[0, column] = jnp.where(late, worker_count, gap)
-        table[1, column] = jnp.where(late, row - half, row)
+        part = jnp.where(late, worker_count, gap)
+        table[0, column] = jnp.where(used, part, 0)
+        table[1, column] = jnp.where(used, jnp.where(late, row - half, row), 0)
         table[2, column] = owner * image_count + row
         table[3, column] = core
-        table[4, column] = jnp.where(missed == 0, 1, 0)
+        table[4, column] = jnp.where(used, 1, 0)
 
 
 def plan(owners, locals_, counts, worker, core, image_count, worker_count):
@@ -230,7 +254,7 @@
     part = jnp.where(late, worker_count, gap)
     row = jnp.where(late, row - half, row)
     head = jnp.broadcast_to(jnp.asarray(core, jnp.int32), (8,))
-    return jnp.stack([part, row, image, head])
+    return jnp.stack([part, row, image, head, jnp.ones_like(image)])
 
 
 def fetch(table, column, keys, parts, target, sem, wait):
@@ -326,7 +350,7 @@
 
     here = pl.ds(pl.multiple_of(core * half, half), half)
     there = pl.ds(pl.multiple_of((1 - core) * half, half), half)
-    context_of = (1, 0, None, 2)
+    context_of = (1, 0, None, 2) if views == 3 else (1, 0, 3, 2)
     for j in range(4):
         raw_a, raw_b = mine[j], theirs[j]
         a, b = raw_a.astype(F32), raw_b.astype(F32)
@@ -398,7 +422,10 @@
         last = lax.broadcasted_iota(jnp.int32, raw.shape, 0) == 3
         contrib = jnp.where(last, conf, raw * conf)
         image = table[2, i]
-        out[image] = out[image] + contrib[:, :tokens]
+
+        @pl.when(table[4, i] == 1)
+        def _():
+            out[image] = out[image] + contrib[:, :tokens]
 
 
 def per_device(
@@ -425,7 +452,6 @@
     width, hidden_width = hidden_weight.shape
     rows = -(-token_count // 8) * 8
     padded = -(-token_count // 16) * 16
-    views = 3
 
     shard = jnp.pad(tokens, ((0, 0), (0, rows - token_count), (0, 0)))
     scalars = pl.BlockSpec(memory_space=pltpu.SMEM)
@@ -439,9 +465,9 @@
         hidden_bias.reshape(1, hidden_width),
         point_weight,
     )
-    wide = pltpu.VMEM((views, padded, width), BF16)
-
-    def decode(table, parts, vectors, weights):
+
+    def decode(views, table, parts, vectors, weights):
+        wide = pltpu.VMEM((views, padded, width), BF16)
         keep, other = gather_images(table, parts, weights)
         return pl.pallas_call(
             functools.partial(decode_kernel, token_count),
@@ -455,26 +481,28 @@
 
     if worker_count == 8:
         reach = 2
-        pairs = worker_count * views
+        pairs = worker_count * SHARE
         table = pl.pallas_call(
             functools.partial(deal_kernel, worker_count, image_count, reach),
-            out_shape=jax.ShapeDtypeStruct((5, 8), jnp.int32),
+            out_shape=jax.ShapeDtypeStruct((LEVEL + 1, 8), jnp.int32),
             in_specs=[scalars] * 4,
             out_specs=scalars,
             scratch_shapes=[pltpu.SMEM((pairs,), jnp.int32)] * 4
-            + [pltpu.SMEM((worker_count,), jnp.int32), pltpu.SMEM((pairs,), jnp.int32)]
+            + [pltpu.SMEM((worker_count,), jnp.int32)]
+            + [pltpu.SMEM((worker_count * MOST,), jnp.int32)]
             + [pltpu.SMEM((worker_count,), jnp.int32)],
             compiler_params=pltpu.CompilerParams(vmem_limit_bytes=2 * 1024 * 1024),
             cost_estimate=pl.CostEstimate(flops=0, bytes_accessed=20 * 10**6, transcendentals=0),
             name="deal",
         )(owners, view_local, pair_count, jnp.stack([worker, core]))
         parts = ring_near(shard, worker_count, reach)
-        flat = lax.cond(
-            table[4, 0] == 1,
-            decode,
-            lambda table, near, *rest: decode(
-                table, ring_far(near, worker_count, reach), *rest
-            ),
+
+        def decode_far(table, near, *rest):
+            return decode(MOST, table, ring_far(near, worker_count, reach), *rest)
+
+        flat = lax.switch(
+            table[LEVEL, 0],
+            (functools.partial(decode, SHARE), functools.partial(decode, MOST), decode_far),
             table,
             parts,
             vectors,
@@ -483,7 +511,7 @@
     else:
         table = plan(owners, view_local, pair_count, worker, core, image_count, worker_count)
         parts = ring_far({0: shard, worker_count: shard}, worker_count, 0)
-        flat = decode(table, parts, vectors, weights)
+        flat = decode(SHARE, table, parts, vectors, weights)
     arrived = lax.all_to_all(flat, ("pairs", "mp"), 0, 0, tiled=True)
     mine = image_count // core_count
     return jnp.sum(arrived.reshape(worker_count * core_count, mine, 4, token_count), axis=0)

time: 66.9 us -> 67.2 us (level)
  no operation moved by 1% of the time
where the time goes in v4:
time: 67.2 us; the launch traced here: 66.9 us
  Pallas kernels  28.5 us (42%)
  waiting for transfers between devices  16.9 us (25%)
  blocking collectives  12.8 us (19%)
  starting transfers between devices  5.18 us (8%)
  local copies, waits for them, and re-layouts  1.84 us (3%)
  between operations  0.76 us (1%)
  other arithmetic  0.72 us (1%)
    ppermute x2, waiting for transfers between devices, ring_near(): going = lax.ppermute(going, 'pairs', ahead)  15.7 us
    pallas_call x1, Pallas kernels, decode(): pl.pallas_call(functools.partial(decode_kernel, token_count), out_shape=j...  13.2 us
    all_to_all x1, blocking collectives, per_device(): arrived = lax.all_to_all(flat, ('pairs', 'mp'), 0, 0, tiled=True)  12.8 us
    pallas_call x1, Pallas kernels, per_device(): pl.pallas_call(functools.partial(deal_kernel, worker_count, image_count,...  7.31 us
    pallas_call x2, Pallas kernels, pick(): pl.pallas_call(functools.partial(pick_kernel, keys, first_column), out_sh...  5.14 us
    ppermute x2, starting transfers between devices, ring_near(): going = lax.ppermute(going, 'pairs', ahead)  4.87 us
    pallas_call x1, Pallas kernels, stage(): pl.pallas_call(functools.partial(stage_kernel, count), out_shape=tuple((j...  2.89 us
  transfers between devices with their start and end apart: 5, of which 3 were waited for; matrix products, arithmetic and copies ran while one was open for 1% of the time, Pallas kernels for 19%

profile of v4, /device:TPU:0, one launch (start us, length us, event | category | flops | bytes accessed | tf_op | source)
XLA Modules:
  0.0 66.9 jit_solution(5616764677778327110)
XLA Ops:
  0.0 0.0 copy-start
  0.0 1.2 %copy.15 = bf16[4,196,384]{2,1,0:T(8,128)(2,1)S(1)} copy(bf16[4,196,384]{2,0,1:T(4,128)(2,1)} %param.17) | data formatting | bytes 1204224 | tf_op args[0]
  1.2 0.1 pad.4
  1.3 3.1 %collective-permute-start.9 = (bf16[4,200,384]{2,1,0:T(8,128)(2,1)S(1)}, bf16[4,200,384]{2,1,0:T(8,128)(2,1)}, u32[]{:S(2)}, u32[]{:S(2)}) collective-permute-start(bf16[4,200,384]{2,1,0:T(8,128)(2,1)S(1)} %pad.4), channel_id=1, source_target_pairs={{0,4},{4,8},{8,12},{12,14},{14,10},{10,6},{6,2},{2,0},{1,5},{5,9},... | collective-permute-start | bytes 1843208 | tf_op jit(solution)/shard_map/ppermute | solution.py:48
  4.4 0.0 collective-permute-start.7
  4.4 13.9 %collective-permute-done.9 = bf16[4,200,384]{2,1,0:T(8,128)(2,1)} collective-permute-done((bf16[4,200,384]{2,1,0:T(8,128)(2,1)S(1)}, bf16[4,200,384]{2,1,0:T(8,128)(2,1)}, u32[]{:S(2)}, u32[]{:S(2)}) %collective-permute-start.9) | collective-permute-done | bytes 614432 | tf_op jit(solution)/shard_map/ppermute | solution.py:48
  18.3 1.8 %collective-permute-start.10 = (bf16[4,200,384]{2,1,0:T(8,128)(2,1)}, bf16[4,200,384]{2,1,0:T(8,128)(2,1)}, u32[]{:S(2)}, u32[]{:S(2)}) collective-permute-start(bf16[4,200,384]{2,1,0:T(8,128)(2,1)} %collective-permute-done.9), channel_id=1, source_target_pairs={{0,4},{4,8},{8,12},{12,14},{14,10},{10,6},{6,2},{2,0},{1,5},{5,9},... | collective-permute-start | bytes 1843208 | tf_op jit(solution)/shard_map/ppermute | solution.py:48
  20.1 0.0 collective-permute-done.7
  20.1 0.2 collective-permute-start.8
  20.3 0.0 copy-done.5
  20.3 0.0 copy-done.6
  20.4 0.0 copy-done.7
  20.4 0.1 pad_add_fusion.me
  20.5 0.0 copy-done.2
  20.5 0.0 copy-done.1
  20.5 0.0 copy-done
  20.5 7.3 %deal.1 = s32[6,8]{1,0:T(8,128)S(1)} custom-call(s32[96]{0:T(128)S(1)} %bitcast.6, s32[96]{0:T(128)S(1)} %copy-done.1, s32[8]{0:T(128)S(1)} %copy-done.2, s32[2]{0:T(128)S(1)} %pad_add_fusion.me), custom_call_target="tpu_custom_call" | custom-call | bytes 20000000 | tf_op jit(solution)/shard_map/deal/pallas_call | solution.py:485
  27.8 0.5 slice.9
  28.9 0.0 copy-start.3
  29.0 0.0 copy-start.4
  29.0 2.9 %stage.1 = (bf16[768,768]{1,0:T(8,128)(2,1)S(1)}, bf16[768,768]{1,0:T(8,128)(2,1)S(1)}, bf16[768,768]{1,0:T(8,128)(2,1)S(1)}, bf16[768,768]{1,0:T(8,128)(2,1)S(1)}, bf16[768,1024]{1,0:T(8,128)(2,1)S(1)}) custom-call(bf16[768,768]{1,0:T(8,128)(2,1)} %refs_0_.1, bf16[768,768]{1,0:T(8,128)(2,1)} %refs_1_.1, bf16[768,768]{1,0:T(8,128)(2,1)} %refs_2_.1, ...), custom_call_target="tpu_custom_call" | custom-call | bytes 12582912 | tf_op jit(solution)/shard_map/stage/pallas_call | solution.py:312
  31.9 1.8 %collective-permute-done.10 = bf16[4,200,384]{2,1,0:T(8,128)(2,1)} collective-permute-done((bf16[4,200,384]{2,1,0:T(8,128)(2,1)}, bf16[4,200,384]{2,1,0:T(8,128)(2,1)}, u32[]{:S(2)}, u32[]{:S(2)}) %collective-permute-start.10) | collective-permute-done | bytes 614432 | tf_op jit(solution)/shard_map/ppermute | solution.py:48
  33.7 1.2 %collective-permute-done.8 = bf16[4,200,384]{2,1,0:T(8,128)(2,1)} collective-permute-done((bf16[4,200,384]{2,1,0:T(8,128)(2,1)}, bf16[4,200,384]{2,1,0:T(8,128)(2,1)}, u32[]{:S(2)}, u32[]{:S(2)}) %collective-permute-start.8) | collective-permute-done | bytes 614432 | tf_op jit(solution)/shard_map/ppermute | solution.py:49
  34.9 0.0 copy-done.4
  34.9 18.7 %conditional.1 = (f32[32,4,196]{2,1,0:T(4,128)S(1)}) conditional(s32[]{:T(128)} %bitcast.3, (s32[6,8]{1,0:T(8,128)S(1)}, bf16[4,200,384]{2,1,0:T(8,128)(2,1)S(1)}, bf16[4,200,384]{2,1,0:T(8,128)(2,1)}, bf16[4,200,384]{2,1,0:T(8,128)(2,1)}, bf16[4,200,384]{2,1,0:T(8,128)(2,1)}, /*index=5*/bf16[4,200,384]{2,1,0:T(8,128)(2,1)}, ...), branch_computations={%region_0.1_spmd, %region_1.2_spmd, %region_2.3_spmd} | conditional | bytes 13517008 | solution.py:503
  34.9 2.6 %pick.7 = bf16[4,200,384]{2,1,0:T(8,128)(2,1)S(1)} custom-call(s32[6,8]{1,0:T(8,128)S(1)} %get-tuple-element.104.table, bf16[4,200,384]{2,1,0:T(8,128)(2,1)S(1)} %get-tuple-element.106.refs_0_, bf16[4,200,384]{2,1,0:T(8,128)(2,1)} %get-tuple-element.107.refs_1_, bf16[4,200,384]{2,1,0:T(8,128)(2,1)} %get-tuple-element.108.refs_2_, ...), custom_call_target="tpu_custom_call" | custom-call | bytes 1228800 | tf_op jit(solution)/shard_map/cond/branch_0_fun/pick/pallas_call | solution.py:284
  37.4 0.1 collective-permute-start
  37.5 2.6 %pick.6.refs_0_ = bf16[4,200,384]{2,1,0:T(8,128)(2,1)S(1)} custom-call(s32[6,8]{1,0:T(8,128)S(1)} %get-tuple-element.104.table, bf16[4,200,384]{2,1,0:T(8,128)(2,1)S(1)} %get-tuple-element.106.refs_0_, bf16[4,200,384]{2,1,0:T(8,128)(2,1)} %get-tuple-element.107.refs_1_, bf16[4,200,384]{2,1,0:T(8,128)(2,1)} %get-tuple-element.108.refs_2_, ...), custom_call_target="tpu_custom_call" | custom-call | bytes 1228800 | tf_op jit(solution)/shard_map/cond/branch_0_fun/pick/pallas_call | solution.py:284
  40.1 0.0 collective-permute-done.refs_1_
  40.1 13.2 %decode.3 = f32[32,4,196]{2,1,0:T(4,128)S(1)} custom-call(s32[6,8]{1,0:T(8,128)S(1)} %get-tuple-element.104.table, bf16[4,200,384]{2,1,0:T(8,128)(2,1)S(1)} %pick.6.refs_0_, bf16[4,200,384]{2,1,0:T(8,128)(2,1)S(1)} %collective-permute-done.refs_1_, f32[1,768]{1,0:T(1,128)S(1)} %get-tuple-element.116.refs_2_, f32[1,768]{1,0:T(1,128)S(1)} %get-tuple-element.117.refs_3_, ...), custom_call_target="tpu_custom_call" | custom-call | tf_op jit(solution)/shard_map/cond/branch_0_fun/decode/pallas_call | solution.py:472
  53.5 12.8 %all_to_all.5 = f32[32,4,196]{2,1,0:T(4,128)S(1)} all-to-all(f32[32,4,196]{2,1,0:T(4,128)S(1)} %get-tuple-element.163), channel_id=1, replica_groups=mesh['groups'=2,'pairs'=8,'mp'=2] {'pairs','mp'}, dimensions={0} | all-to-all | bytes 200704 | tf_op jit(solution)/shard_map/all_to_all | solution.py:515
  66.3 0.6 reduce_sum.9
  (9 shorter events, 0.0 us)
Async XLA Ops:
  0.0 20.3 %copy-start.5 = (f32[768]{0:T(1024)S(1)}, f32[768]{0:T(1024)}, u32[]{:S(2)}) copy-start(f32[768]{0:T(1024)} %param.18) | copy-start | bytes 9220
  0.0 20.3 %copy-start.6 = (f32[768]{0:T(1024)S(1)}, f32[768]{0:T(1024)}, u32[]{:S(2)}) copy-start(f32[768]{0:T(1024)} %param.19) | copy-start | bytes 9220
  0.0 20.3 %copy-start.7 = (f32[768]{0:T(1024)S(1)}, f32[768]{0:T(1024)}, u32[]{:S(2)}) copy-start(f32[768]{0:T(1024)} %param.24) | copy-start | bytes 9220
  0.0 20.4 %copy-start.2 = (s32[8]{0:T(128)S(1)}, s32[8]{0:T(128)}, u32[]{:S(2)}) copy-start(s32[8]{0:T(128)} %counts.1) | copy-start | bytes 100
  0.0 20.4 %copy-start.1 = (s32[96]{0:T(128)S(1)}, s32[96]{0:T(128)}, u32[]{:S(2)}) copy-start(s32[96]{0:T(128)} %locals_.1) | copy-start | bytes 1156
  0.0 20.4 %copy-start = (s32[96,1]{0,1:T(1,128)S(1)}, s32[96,1]{0,1:T(1,128)}, u32[]{:S(2)}) copy-start(s32[96,1]{0,1:T(1,128)} %param.28) | copy-start | bytes 1156
  1.3 17.0 %collective-permute-start.9 = (bf16[4,200,384]{2,1,0:T(8,128)(2,1)S(1)}, bf16[4,200,384]{2,1,0:T(8,128)(2,1)}, u32[]{:S(2)}, u32[]{:S(2)}) collective-permute-start(bf16[4,200,384]{2,1,0:T(8,128)(2,1)S(1)} %pad.4), channel_id=1, source_target_pairs={{0,4},{4,8},{8,12},{12,14},{14,10},{10,6},{6,2},{2,0},{1,5},{5,9},... | collective-permute-start | bytes 1843208 | tf_op jit(solution)/shard_map/ppermute | solution.py:48
  4.4 15.7 %collective-permute-start.7 = (bf16[4,200,384]{2,1,0:T(8,128)(2,1)S(1)}, bf16[4,200,384]{2,1,0:T(8,128)(2,1)}, u32[]{:S(2)}, u32[]{:S(2)}) collective-permute-start(bf16[4,200,384]{2,1,0:T(8,128)(2,1)S(1)} %pad.4), channel_id=1, source_target_pairs={{4,0},{8,4},{12,8},{14,12},{10,14},{6,10},{2,6},{0,2},{5,1},{9,5},... | collective-permute-start | bytes 1843208 | tf_op jit(solution)/shard_map/ppermute | solution.py:49
  18.3 15.4 %collective-permute-start.10 = (bf16[4,200,384]{2,1,0:T(8,128)(2,1)}, bf16[4,200,384]{2,1,0:T(8,128)(2,1)}, u32[]{:S(2)}, u32[]{:S(2)}) collective-permute-start(bf16[4,200,384]{2,1,0:T(8,128)(2,1)} %collective-permute-done.9), channel_id=1, source_target_pairs={{0,4},{4,8},{8,12},{12,14},{14,10},{10,6},{6,2},{2,0},{1,5},{5,9},... | collective-permute-start | bytes 1843208 | tf_op jit(solution)/shard_map/ppermute | solution.py:48
  20.1 14.8 %collective-permute-start.8 = (bf16[4,200,384]{2,1,0:T(8,128)(2,1)}, bf16[4,200,384]{2,1,0:T(8,128)(2,1)}, u32[]{:S(2)}, u32[]{:S(2)}) collective-permute-start(bf16[4,200,384]{2,1,0:T(8,128)(2,1)} %collective-permute-done.7), channel_id=1, source_target_pairs={{4,0},{8,4},{12,8},{14,12},{10,14},{6,10},{2,6},{0,2},{5,1},{9,5},... | collective-permute-start | bytes 1843208 | tf_op jit(solution)/shard_map/ppermute | solution.py:49
  28.9 5.9 %copy-start.3 = (bf16[4,1024]{1,0:T(4,128)(2,1)S(1)}, bf16[4,1024]{1,0:T(4,128)(2,1)}, u32[]{:S(2)}) copy-start(bf16[4,1024]{1,0:T(4,128)(2,1)} %param.27) | copy-start | bytes 24580
  29.0 5.9 %copy-start.4 = (f32[1024]{0:T(1024)S(1)}, f32[1024]{0:T(1024)}, u32[]{:S(2)}) copy-start(f32[1024]{0:T(1024)} %param.26) | copy-start | bytes 12292
  37.4 2.7 %collective-permute-start = (bf16[4,200,384]{2,1,0:T(8,128)(2,1)S(1)}, bf16[4,200,384]{2,1,0:T(8,128)(2,1)S(1)}, u32[]{:S(2)}, u32[]{:S(2)}) collective-permute-start(bf16[4,200,384]{2,1,0:T(8,128)(2,1)S(1)} %pick.7), channel_id=1, source_target_pairs={{0,1},{1,0},{2,3},{3,2},{4,5},{5,4},{6,7},{7,6},{8,9},{9,8},{10,11... | collective-permute-start | bytes 1843208 | tf_op jit(solution)/shard_map/cond/branch_0_fun/ppermute | solution.py:325

commit v5 on v4

--- a/solution.py
+++ b/solution.py
@@ -392,22 +392,25 @@
         for b in range(width // block):
             cols = slice(b * block, (b + 1) * block)
             qb, kb, vb = q[i, :, cols], k[i, :, cols], v[i, :, cols]
-            blended = []
-            for keep in (0, 1):
-                qh = jnp.where(low, qb, nothing) if keep == 0 else jnp.where(low, nothing, qb)
-                scores = lax.dot_general(
-                    qh, kb, (((1,), (1,)), ((), ())), preferred_element_type=F32
-                )
-                scores = scores + hide
-                peak = jnp.max(scores, axis=-1, keepdims=True)
-                expo = jnp.exp(scores - peak)
-                inverse = 1.0 / jnp.sum(expo, axis=-1, keepdims=True)
-                probs = (expo * inverse).astype(BF16)
-                blended.append(jnp.dot(probs, vb, preferred_element_type=F32))
+            qh = jnp.concatenate([jnp.where(low, qb, nothing), jnp.where(low, nothing, qb)], axis=0)
+            scores = lax.dot_general(
+                qh, kb, (((1,), (1,)), ((), ())), preferred_element_type=F32
+            )
+            scores = scores + hide
+            peak = jnp.max(scores, axis=-1, keepdims=True)
+            expo = jnp.exp(scores - peak)
+            inverse = 1.0 / jnp.sum(expo, axis=-1, keepdims=True)
+            probs = (expo * inverse).astype(BF16)
+            both = jnp.dot(probs, vb, preferred_element_type=F32)
+            blended = (both[:padded], both[padded:])
             att[i, :, cols] = jnp.where(low, blended[0], blended[1]).astype(BF16)
         return carry
 
-    lax.fori_loop(0, views, attend, 0)
+    if views == SHARE:
+        for i in range(views):
+            attend(i, 0)
+    else:
+        lax.fori_loop(0, views, attend, 0)
 
     updated = jnp.dot(att[...].reshape(total, width), wo[...], preferred_element_type=F32)
     updated = updated + res[...].reshape(total, width).astype(F32)

time: 67.2 us -> 65.5 us (0.975)
  Pallas kernels: 28.5 us -> 26.8 us
    pallas_call x1, Pallas kernels: 13.2 us -> 11.5 us  [decode(): pl.pallas_call(functools.partial(decode_kernel, token_count), out_shape=j...]
where the time goes in v5:
time: 65.5 us; the launch traced here: 65.3 us
  Pallas kernels  26.8 us (41%)
  waiting for transfers between devices  17 us (26%)
  blocking collectives  12.8 us (20%)
  starting transfers between devices  5.18 us (8%)
  local copies, waits for them, and re-layouts  1.84 us (3%)
  between operations  0.76 us (1%)
  other arithmetic  0.72 us (1%)
    ppermute x2, waiting for transfers between devices, ring_near(): going = lax.ppermute(going, 'pairs', ahead)  15.8 us
    all_to_all x1, blocking collectives, per_device(): arrived = lax.all_to_all(flat, ('pairs', 'mp'), 0, 0, tiled=True)  12.8 us
    pallas_call x1, Pallas kernels, decode(): pl.pallas_call(functools.partial(decode_kernel, token_count), out_shape=j...  11.5 us
    pallas_call x1, Pallas kernels, per_device(): pl.pallas_call(functools.partial(deal_kernel, worker_count, image_count,...  7.23 us
    pallas_call x2, Pallas kernels, pick(): pl.pallas_call(functools.partial(pick_kernel, keys, first_column), out_sh...  5.14 us
    ppermute x2, starting transfers between devices, ring_near(): going = lax.ppermute(going, 'pairs', ahead)  4.87 us
    pallas_call x1, Pallas kernels, stage(): pl.pallas_call(functools.partial(stage_kernel, count), out_shape=tuple((j...  2.89 us
  transfers between devices with their start and end apart: 5, of which 3 were waited for; matrix products, arithmetic and copies ran while one was open for 1% of the time, Pallas kernels for 19%

profile of v5, /device:TPU:0, one launch (start us, length us, event | category | flops | bytes accessed | tf_op | source)
XLA Modules:
  0.0 65.3 jit_solution(5939420129685663351)
XLA Ops:
  0.0 0.0 copy-start
  0.0 1.2 %copy.15 = bf16[4,196,384]{2,1,0:T(8,128)(2,1)S(1)} copy(bf16[4,196,384]{2,0,1:T(4,128)(2,1)} %param.17) | data formatting | bytes 1204224 | tf_op args[0]
  1.2 0.1 pad.4
  1.3 3.1 %collective-permute-start.9 = (bf16[4,200,384]{2,1,0:T(8,128)(2,1)S(1)}, bf16[4,200,384]{2,1,0:T(8,128)(2,1)}, u32[]{:S(2)}, u32[]{:S(2)}) collective-permute-start(bf16[4,200,384]{2,1,0:T(8,128)(2,1)S(1)} %pad.4), channel_id=1, source_target_pairs={{0,4},{4,8},{8,12},{12,14},{14,10},{10,6},{6,2},{2,0},{1,5},{5,9},... | collective-permute-start | bytes 1843208 | tf_op jit(solution)/shard_map/ppermute | solution.py:48
  4.4 0.0 collective-permute-start.7
  4.4 13.9 %collective-permute-done.9 = bf16[4,200,384]{2,1,0:T(8,128)(2,1)} collective-permute-done((bf16[4,200,384]{2,1,0:T(8,128)(2,1)S(1)}, bf16[4,200,384]{2,1,0:T(8,128)(2,1)}, u32[]{:S(2)}, u32[]{:S(2)}) %collective-permute-start.9) | collective-permute-done | bytes 614432 | tf_op jit(solution)/shard_map/ppermute | solution.py:48
  18.3 1.8 %collective-permute-start.10 = (bf16[4,200,384]{2,1,0:T(8,128)(2,1)}, bf16[4,200,384]{2,1,0:T(8,128)(2,1)}, u32[]{:S(2)}, u32[]{:S(2)}) collective-permute-start(bf16[4,200,384]{2,1,0:T(8,128)(2,1)} %collective-permute-done.9), channel_id=1, source_target_pairs={{0,4},{4,8},{8,12},{12,14},{14,10},{10,6},{6,2},{2,0},{1,5},{5,9},... | collective-permute-start | bytes 1843208 | tf_op jit(solution)/shard_map/ppermute | solution.py:48
  20.1 0.0 collective-permute-done.7
  20.1 0.2 collective-permute-start.8
  20.3 0.0 copy-done.5
  20.3 0.0 copy-done.6
  20.4 0.0 copy-done.7
  20.4 0.1 pad_add_fusion.me
  20.5 0.0 copy-done.2
  20.5 0.0 copy-done.1
  20.5 0.0 copy-done
  20.5 7.2 %deal.1 = s32[6,8]{1,0:T(8,128)S(1)} custom-call(s32[96]{0:T(128)S(1)} %bitcast.6, s32[96]{0:T(128)S(1)} %copy-done.1, s32[8]{0:T(128)S(1)} %copy-done.2, s32[2]{0:T(128)S(1)} %pad_add_fusion.me), custom_call_target="tpu_custom_call" | custom-call | bytes 20000000 | tf_op jit(solution)/shard_map/deal/pallas_call | solution.py:488
  27.7 0.5 slice.9
  28.9 0.0 copy-start.3
  28.9 0.0 copy-start.4
  28.9 2.9 %stage.1 = (bf16[768,768]{1,0:T(8,128)(2,1)S(1)}, bf16[768,768]{1,0:T(8,128)(2,1)S(1)}, bf16[768,768]{1,0:T(8,128)(2,1)S(1)}, bf16[768,768]{1,0:T(8,128)(2,1)S(1)}, bf16[768,1024]{1,0:T(8,128)(2,1)S(1)}) custom-call(bf16[768,768]{1,0:T(8,128)(2,1)} %refs_0_.1, bf16[768,768]{1,0:T(8,128)(2,1)} %refs_1_.1, bf16[768,768]{1,0:T(8,128)(2,1)} %refs_2_.1, ...), custom_call_target="tpu_custom_call" | custom-call | bytes 12582912 | tf_op jit(solution)/shard_map/stage/pallas_call | solution.py:312
  31.8 1.9 %collective-permute-done.10 = bf16[4,200,384]{2,1,0:T(8,128)(2,1)} collective-permute-done((bf16[4,200,384]{2,1,0:T(8,128)(2,1)}, bf16[4,200,384]{2,1,0:T(8,128)(2,1)}, u32[]{:S(2)}, u32[]{:S(2)}) %collective-permute-start.10) | collective-permute-done | bytes 614432 | tf_op jit(solution)/shard_map/ppermute | solution.py:48
  33.7 1.2 %collective-permute-done.8 = bf16[4,200,384]{2,1,0:T(8,128)(2,1)} collective-permute-done((bf16[4,200,384]{2,1,0:T(8,128)(2,1)}, bf16[4,200,384]{2,1,0:T(8,128)(2,1)}, u32[]{:S(2)}, u32[]{:S(2)}) %collective-permute-start.8) | collective-permute-done | bytes 614432 | tf_op jit(solution)/shard_map/ppermute | solution.py:49
  34.9 0.0 copy-done.4
  34.9 17.0 %conditional.1 = (f32[32,4,196]{2,1,0:T(4,128)S(1)}) conditional(s32[]{:T(128)} %bitcast.3, (s32[6,8]{1,0:T(8,128)S(1)}, bf16[4,200,384]{2,1,0:T(8,128)(2,1)S(1)}, bf16[4,200,384]{2,1,0:T(8,128)(2,1)}, bf16[4,200,384]{2,1,0:T(8,128)(2,1)}, bf16[4,200,384]{2,1,0:T(8,128)(2,1)}, /*index=5*/bf16[4,200,384]{2,1,0:T(8,128)(2,1)}, ...), branch_computations={%region_0.1_spmd, %region_1.2_spmd, %region_2.3_spmd} | conditional | bytes 13517008 | solution.py:506
  34.9 2.6 %pick.7 = bf16[4,200,384]{2,1,0:T(8,128)(2,1)S(1)} custom-call(s32[6,8]{1,0:T(8,128)S(1)} %get-tuple-element.104.table, bf16[4,200,384]{2,1,0:T(8,128)(2,1)S(1)} %get-tuple-element.106.refs_0_, bf16[4,200,384]{2,1,0:T(8,128)(2,1)} %get-tuple-element.107.refs_1_, bf16[4,200,384]{2,1,0:T(8,128)(2,1)} %get-tuple-element.108.refs_2_, ...), custom_call_target="tpu_custom_call" | custom-call | bytes 1228800 | tf_op jit(solution)/shard_map/cond/branch_0_fun/pick/pallas_call | solution.py:284
  37.4 0.1 collective-permute-start
  37.5 2.6 %pick.6.refs_0_ = bf16[4,200,384]{2,1,0:T(8,128)(2,1)S(1)} custom-call(s32[6,8]{1,0:T(8,128)S(1)} %get-tuple-element.104.table, bf16[4,200,384]{2,1,0:T(8,128)(2,1)S(1)} %get-tuple-element.106.refs_0_, bf16[4,200,384]{2,1,0:T(8,128)(2,1)} %get-tuple-element.107.refs_1_, bf16[4,200,384]{2,1,0:T(8,128)(2,1)} %get-tuple-element.108.refs_2_, ...), custom_call_target="tpu_custom_call" | custom-call | bytes 1228800 | tf_op jit(solution)/shard_map/cond/branch_0_fun/pick/pallas_call | solution.py:284
  40.1 0.0 collective-permute-done.refs_1_
  40.1 11.5 %decode.3 = f32[32,4,196]{2,1,0:T(4,128)S(1)} custom-call(s32[6,8]{1,0:T(8,128)S(1)} %get-tuple-element.104.table, bf16[4,200,384]{2,1,0:T(8,128)(2,1)S(1)} %pick.6.refs_0_, bf16[4,200,384]{2,1,0:T(8,128)(2,1)S(1)} %collective-permute-done.refs_1_, f32[1,768]{1,0:T(1,128)S(1)} %get-tuple-element.116.refs_2_, f32[1,768]{1,0:T(1,128)S(1)} %get-tuple-element.117.refs_3_, ...), custom_call_target="tpu_custom_call" | custom-call | tf_op jit(solution)/shard_map/cond/branch_0_fun/decode/pallas_call | solution.py:475
  51.9 12.8 %all_to_all.5 = f32[32,4,196]{2,1,0:T(4,128)S(1)} all-to-all(f32[32,4,196]{2,1,0:T(4,128)S(1)} %get-tuple-element.163), channel_id=1, replica_groups=mesh['groups'=2,'pairs'=8,'mp'=2] {'pairs','mp'}, dimensions={0} | all-to-all | bytes 200704 | tf_op jit(solution)/shard_map/all_to_all | solution.py:518
  64.6 0.6 reduce_sum.9
  (9 shorter events, 0.0 us)
Async XLA Ops:
  0.0 20.3 %copy-start.5 = (f32[768]{0:T(1024)S(1)}, f32[768]{0:T(1024)}, u32[]{:S(2)}) copy-start(f32[768]{0:T(1024)} %param.18) | copy-start | bytes 9220
  0.0 20.3 %copy-start.6 = (f32[768]{0:T(1024)S(1)}, f32[768]{0:T(1024)}, u32[]{:S(2)}) copy-start(f32[768]{0:T(1024)} %param.19) | copy-start | bytes 9220
  0.0 20.3 %copy-start.7 = (f32[768]{0:T(1024)S(1)}, f32[768]{0:T(1024)}, u32[]{:S(2)}) copy-start(f32[768]{0:T(1024)} %param.24) | copy-start | bytes 9220
  0.0 20.4 %copy-start.2 = (s32[8]{0:T(128)S(1)}, s32[8]{0:T(128)}, u32[]{:S(2)}) copy-start(s32[8]{0:T(128)} %counts.1) | copy-start | bytes 100
  0.0 20.4 %copy-start.1 = (s32[96]{0:T(128)S(1)}, s32[96]{0:T(128)}, u32[]{:S(2)}) copy-start(s32[96]{0:T(128)} %locals_.1) | copy-start | bytes 1156
  0.0 20.4 %copy-start = (s32[96,1]{0,1:T(1,128)S(1)}, s32[96,1]{0,1:T(1,128)}, u32[]{:S(2)}) copy-start(s32[96,1]{0,1:T(1,128)} %param.28) | copy-start | bytes 1156
  1.3 17.0 %collective-permute-start.9 = (bf16[4,200,384]{2,1,0:T(8,128)(2,1)S(1)}, bf16[4,200,384]{2,1,0:T(8,128)(2,1)}, u32[]{:S(2)}, u32[]{:S(2)}) collective-permute-start(bf16[4,200,384]{2,1,0:T(8,128)(2,1)S(1)} %pad.4), channel_id=1, source_target_pairs={{0,4},{4,8},{8,12},{12,14},{14,10},{10,6},{6,2},{2,0},{1,5},{5,9},... | collective-permute-start | bytes 1843208 | tf_op jit(solution)/shard_map/ppermute | solution.py:48
  4.4 15.7 %collective-permute-start.7 = (bf16[4,200,384]{2,1,0:T(8,128)(2,1)S(1)}, bf16[4,200,384]{2,1,0:T(8,128)(2,1)}, u32[]{:S(2)}, u32[]{:S(2)}) collective-permute-start(bf16[4,200,384]{2,1,0:T(8,128)(2,1)S(1)} %pad.4), channel_id=1, source_target_pairs={{4,0},{8,4},{12,8},{14,12},{10,14},{6,10},{2,6},{0,2},{5,1},{9,5},... | collective-permute-start | bytes 1843208 | tf_op jit(solution)/shard_map/ppermute | solution.py:49
  18.3 15.4 %collective-permute-start.10 = (bf16[4,200,384]{2,1,0:T(8,128)(2,1)}, bf16[4,200,384]{2,1,0:T(8,128)(2,1)}, u32[]{:S(2)}, u32[]{:S(2)}) collective-permute-start(bf16[4,200,384]{2,1,0:T(8,128)(2,1)} %collective-permute-done.9), channel_id=1, source_target_pairs={{0,4},{4,8},{8,12},{12,14},{14,10},{10,6},{6,2},{2,0},{1,5},{5,9},... | collective-permute-start | bytes 1843208 | tf_op jit(solution)/shard_map/ppermute | solution.py:48
  20.1 14.8 %collective-permute-start.8 = (bf16[4,200,384]{2,1,0:T(8,128)(2,1)}, bf16[4,200,384]{2,1,0:T(8,128)(2,1)}, u32[]{:S(2)}, u32[]{:S(2)}) collective-permute-start(bf16[4,200,384]{2,1,0:T(8,128)(2,1)} %collective-permute-done.7), channel_id=1, source_target_pairs={{4,0},{8,4},{12,8},{14,12},{10,14},{6,10},{2,6},{0,2},{5,1},{9,5},... | collective-permute-start | bytes 1843208 | tf_op jit(solution)/shard_map/ppermute | solution.py:49
  28.9 6.0 %copy-start.3 = (bf16[4,1024]{1,0:T(4,128)(2,1)S(1)}, bf16[4,1024]{1,0:T(4,128)(2,1)}, u32[]{:S(2)}) copy-start(bf16[4,1024]{1,0:T(4,128)(2,1)} %param.27) | copy-start | bytes 24580
  28.9 6.0 %copy-start.4 = (f32[1024]{0:T(1024)S(1)}, f32[1024]{0:T(1024)}, u32[]{:S(2)}) copy-start(f32[1024]{0:T(1024)} %param.26) | copy-start | bytes 12292
  37.4 2.7 %collective-permute-start = (bf16[4,200,384]{2,1,0:T(8,128)(2,1)S(1)}, bf16[4,200,384]{2,1,0:T(8,128)(2,1)S(1)}, u32[]{:S(2)}, u32[]{:S(2)}) collective-permute-start(bf16[4,200,384]{2,1,0:T(8,128)(2,1)S(1)} %pick.7), channel_id=1, source_target_pairs={{0,1},{1,0},{2,3},{3,2},{4,5},{5,4},{6,7},{7,6},{8,9},{9,8},{10,11... | collective-permute-start | bytes 1843208 | tf_op jit(solution)/shard_map/cond/branch_0_fun/ppermute | solution.py:325

commit v6 on v5

--- a/solution.py
+++ b/solution.py
@@ -73,6 +73,7 @@
 SHARE = 3
 MOST = 4
 LEVEL = 5
+SPOT = 6
 
 
 def deal_kernel(
@@ -229,6 +230,11 @@
         table[2, column] = owner * image_count + row
         table[3, column] = core
         table[4, column] = jnp.where(used, 1, 0)
+        ahead = jnp.logical_or(gap == 1, gap == 2)
+        nearest = jnp.logical_or(gap == 1, gap == worker_count - 1)
+        ours = nearest == (core == 0)
+        spot_there = jnp.where(ours, 0, 12) + jnp.where(ahead, 0, image_count) + row
+        table[SPOT, column] = jnp.where(gap == 0, 2 * image_count + row, spot_there)
 
 
 def plan(owners, locals_, counts, worker, core, image_count, worker_count):
@@ -336,13 +342,14 @@
 def decode_kernel(tokens, table, *refs):
     (mine, theirs, gain_q, gain_c, gain_h, bias_h, wp) = refs[:7]
     wq, wk, wv, wo, wh = refs[7:12]
-    out = refs[12]
-    (xq, xc, res, q, k, v, att, hid) = refs[13:]
+    outs = refs[12:-8]
+    (xq, xc, res, q, k, v, att, hid) = refs[-8:]
     rows, half = mine.shape[1], mine.shape[2]
     views, padded, width = q.shape
     core = table[3, 0]
 
-    out[...] = jnp.zeros_like(out)
+    for out in outs:
+        out[...] = jnp.zeros_like(out)
     tail = jnp.zeros((views, padded - rows, width), BF16)
     xq[:, rows:, :] = tail
     xc[:, rows:, :] = tail
@@ -424,11 +431,26 @@
         conf = 1.0 + jnp.exp(raw[3:4])
         last = lax.broadcasted_iota(jnp.int32, raw.shape, 0) == 3
         contrib = jnp.where(last, conf, raw * conf)
-        image = table[2, i]
-
-        @pl.when(table[4, i] == 1)
+        contrib = contrib[:, :tokens]
+        used = table[4, i] == 1
+        if len(outs) == 1:
+            image = table[2, i]
+
+            @pl.when(used)
+            def _():
+                outs[0][image] = outs[0][image] + contrib
+
+            continue
+        spot = table[SPOT, i]
+        kept = outs[0].shape[0]
+
+        @pl.when(jnp.logical_and(used, spot < kept))
         def _():
-            out[image] = out[image] + contrib[:, :tokens]
+            outs[0][spot] = outs[0][spot] + contrib
+
+        @pl.when(jnp.logical_and(used, spot >= kept))
+        def _():
+            outs[1][spot - kept] = outs[1][spot - kept] + contrib
 
 
 def per_device(
@@ -469,25 +491,54 @@
         point_weight,
     )
 
-    def decode(views, table, parts, vectors, weights):
+    def decode(views, spots, table, parts, vectors, weights):
         wide = pltpu.VMEM((views, padded, width), BF16)
         keep, other = gather_images(table, parts, weights)
         return pl.pallas_call(
             functools.partial(decode_kernel, token_count),
-            out_shape=jax.ShapeDtypeStruct((worker_count * image_count, 4, token_count), F32),
+            out_shape=tuple(
+                jax.ShapeDtypeStruct((count, 4, token_count), F32) for count in spots
+            ),
             in_specs=[scalars] + [vector] * 12,
-            out_specs=vector,
+            out_specs=(vector,) * len(spots),
             scratch_shapes=[wide] * 7 + [pltpu.VMEM((views, padded, hidden_width), BF16)],
             compiler_params=pltpu.CompilerParams(vmem_limit_bytes=32 * 1024 * 1024),
             name="decode",
         )(table, in_vmem(keep), in_vmem(other), *vectors, *[in_vmem(w) for w in weights])
+
+    swap = [(0, 1), (1, 0)]
+    mine = image_count // core_count
+
+    def decode_any(views, table, parts, vectors, weights):
+        spots = (worker_count * image_count,)
+        (flat,) = decode(views, spots, table, parts, vectors, weights)
+        arrived = lax.all_to_all(flat, ("pairs", "mp"), 0, 0, tiled=True)
+        return jnp.sum(arrived.reshape(worker_count * core_count, mine, 4, token_count), axis=0)
+
+    def decode_near(views, table, parts, vectors, weights):
+        spots = (3 * image_count, 2 * image_count)
+        keep, send = decode(views, spots, table, parts, vectors, weights)
+        leaving = keep[: 2 * image_count] + lax.ppermute(send, "mp", swap)
+        order = ring_order(worker_count)
+        ahead = [
+            (order[i] * core_count + c, order[(i + 1 + c) % worker_count] * core_count + c)
+            for i in range(worker_count)
+            for c in range(core_count)
+        ]
+        back = [(b, a) for a, b in ahead]
+        axes = ("pairs", "mp")
+        total = keep[2 * image_count :] + lax.ppermute(leaving[:image_count], axes, ahead)
+        total = total + lax.ppermute(leaving[image_count:], axes, back)
+        theirs = lax.dynamic_slice_in_dim(total, (1 - core) * mine, mine, 0)
+        ours = lax.dynamic_slice_in_dim(total, core * mine, mine, 0)
+        return ours + lax.ppermute(theirs, "mp", swap)
 
     if worker_count == 8:
         reach = 2
         pairs = worker_count * SHARE
         table = pl.pallas_call(
             functools.partial(deal_kernel, worker_count, image_count, reach),
-            out_shape=jax.ShapeDtypeStruct((LEVEL + 1, 8), jnp.int32),
+            out_shape=jax.ShapeDtypeStruct((SPOT + 1, 8), jnp.int32),
             in_specs=[scalars] * 4,
             out_specs=scalars,
             scratch_shapes=[pltpu.SMEM((pairs,), jnp.int32)] * 4
@@ -501,23 +552,23 @@
         parts = ring_near(shard, worker_count, reach)
 
         def decode_far(table, near, *rest):
-            return decode(MOST, table, ring_far(near, worker_count, reach), *rest)
-
-        flat = lax.switch(
+            return decode_any(MOST, table, ring_far(near, worker_count, reach), *rest)
+
+        return lax.switch(
             table[LEVEL, 0],
-            (functools.partial(decode, SHARE), functools.partial(decode, MOST), decode_far),
+            (
+                functools.partial(decode_near, SHARE),
+                functools.partial(decode_near, MOST),
+                decode_far,
+            ),
             table,
             parts,
             vectors,
             weights,
         )
-    else:
-        table = plan(owners, view_local, pair_count, worker, core, image_count, worker_count)
-        parts = ring_far({0: shard, worker_count: shard}, worker_count, 0)
-        flat = decode(SHARE, table, parts, vectors, weights)
-    arrived = lax.all_to_all(flat, ("pairs", "mp"), 0, 0, tiled=True)
-    mine = image_count // core_count
-    return jnp.sum(arrived.reshape(worker_count * core_count, mine, 4, token_count), axis=0)
+    table = plan(owners, view_local, pair_count, worker, core, image_count, worker_count)
+    parts = ring_far({0: shard, worker_count: shard}, worker_count, 0)
+    return decode_any(SHARE, table, parts, vectors, weights)
 
 
 def solution(mesh):

time: 65.5 us -> 61.2 us (0.934)
  blocking collectives: 12.8 us -> 0 us
  waiting for transfers between devices: 17 us -> 23 us
  starting transfers between devices: 5.18 us -> 8.69 us
  Pallas kernels: 26.8 us -> 25.8 us
  local copies, waits for them, and re-layouts: 1.84 us -> 2.53 us
    all_to_all x1 -> x0, blocking collectives: 12.8 us -> none  [per_device(): arrived = lax.all_to_all(flat, ('pairs', 'mp'), 0, 0, tiled=True)]
    ppermute x0 -> x4, waiting for transfers between devices: none -> 5.15 us  [the longest x1 1.75 us: decode_near(): total = total + lax.ppermute(leaving[image_count:], axes, back)]
    ppermute x0 -> x4, starting transfers between devices: none -> 3.51 us  [the longest x1 1.63 us: decode_near(): lax.ppermute(leaving[:image_count], axes, ahead)]
    pallas_call x1, Pallas kernels: 7.23 us -> 6.18 us  [per_device(): pl.pallas_call(functools.partial(deal_kernel, worker_count, image_count,...]
    ppermute x2, waiting for transfers between devices: 15.8 us -> 16.7 us  [ring_near(): going = lax.ppermute(going, 'pairs', ahead)]
    unnamed x17 -> x19, local copies, waits for them, and re-layouts: 1.25 us -> 1.85 us
  transfers between devices with their start and end apart: 5 -> 9, of which waited for: 3 -> 7; matrix products, arithmetic and copies ran while one was open for 1% -> 1% of each run, Pallas kernels for 19% -> 19%
where the time goes in v6:
time: 61.2 us; the launch traced here: 61 us
  Pallas kernels  25.8 us (42%)
  waiting for transfers between devices  23 us (38%)
  starting transfers between devices  8.69 us (14%)
  local copies, waits for them, and re-layouts  2.53 us (4%)
  between operations  0.79 us (1%)
    ppermute x2, waiting for transfers between devices, ring_near(): going = lax.ppermute(going, 'pairs', ahead)  16.7 us
    pallas_call x1, Pallas kernels, decode(): pl.pallas_call(functools.partial(decode_kernel, token_count), out_shape=t...  11.6 us
    pallas_call x1, Pallas kernels, per_device(): pl.pallas_call(functools.partial(deal_kernel, worker_count, image_count,...  6.18 us
    pallas_call x2, Pallas kernels, pick(): pl.pallas_call(functools.partial(pick_kernel, keys, first_column), out_sh...  5.14 us
    ppermute x2, starting transfers between devices, ring_near(): going = lax.ppermute(going, 'pairs', ahead)  4.87 us
    pallas_call x1, Pallas kernels, stage(): pl.pallas_call(functools.partial(stage_kernel, count), out_shape=tuple((j...  2.89 us
    unnamed x19, local copies, waits for them, and re-layouts  1.85 us
    ppermute x1, waiting for transfers between devices, decode_near(): total = total + lax.ppermute(leaving[image_count:], axes, back)  1.75 us
  transfers between devices with their start and end apart: 9, of which 7 were waited for; matrix products, arithmetic and copies ran while one was open for 1% of the time, Pallas kernels for 19%

profile of v6, /device:TPU:0, one launch (start us, length us, event | category | flops | bytes accessed | tf_op | source)
XLA Modules:
  0.0 61.0 jit_solution(16504238315464240288)
XLA Ops:
  0.0 0.0 copy-start
  0.0 1.2 %copy.18 = bf16[4,196,384]{2,1,0:T(8,128)(2,1)S(1)} copy(bf16[4,196,384]{2,0,1:T(4,128)(2,1)} %param.17) | data formatting | bytes 1204224 | tf_op args[0]
  1.2 0.1 pad.4
  1.3 3.1 %collective-permute-start.17 = (bf16[4,200,384]{2,1,0:T(8,128)(2,1)S(1)}, bf16[4,200,384]{2,1,0:T(8,128)(2,1)}, u32[]{:S(2)}, u32[]{:S(2)}) collective-permute-start(bf16[4,200,384]{2,1,0:T(8,128)(2,1)S(1)} %pad.4), channel_id=1, source_target_pairs={{0,4},{4,8},{8,12},{12,14},{14,10},{10,6},{6,2},{2,0},{1,5},{5,9},... | collective-permute-start | bytes 1843208 | tf_op jit(solution)/shard_map/ppermute | solution.py:48
  4.4 0.0 collective-permute-start.15
  4.4 13.9 %collective-permute-done.17 = bf16[4,200,384]{2,1,0:T(8,128)(2,1)} collective-permute-done((bf16[4,200,384]{2,1,0:T(8,128)(2,1)S(1)}, bf16[4,200,384]{2,1,0:T(8,128)(2,1)}, u32[]{:S(2)}, u32[]{:S(2)}) %collective-permute-start.17) | collective-permute-done | bytes 614432 | tf_op jit(solution)/shard_map/ppermute | solution.py:48
  18.3 1.8 %collective-permute-start.18 = (bf16[4,200,384]{2,1,0:T(8,128)(2,1)}, bf16[4,200,384]{2,1,0:T(8,128)(2,1)}, u32[]{:S(2)}, u32[]{:S(2)}) collective-permute-start(bf16[4,200,384]{2,1,0:T(8,128)(2,1)} %collective-permute-done.17), channel_id=1, source_target_pairs={{0,4},{4,8},{8,12},{12,14},{14,10},{10,6},{6,2},{2,0},{1,5},{5,9},... | collective-permute-start | bytes 1843208 | tf_op jit(solution)/shard_map/ppermute | solution.py:48
  20.1 0.0 collective-permute-done.15
  20.1 0.2 collective-permute-start.16
  20.4 0.1 pad_add_fusion.me
  20.5 6.2 %deal.1 = s32[7,8]{1,0:T(8,128)S(1)} custom-call(s32[96]{0:T(128)S(1)} %bitcast.6, s32[96]{0:T(128)S(1)} %copy-done.1, s32[8]{0:T(128)S(1)} %copy-done.2, s32[2]{0:T(128)S(1)} %pad_add_fusion.me), custom_call_target="tpu_custom_call" | custom-call | bytes 20000000 | tf_op jit(solution)/shard_map/deal/pallas_call | solution.py:539
  26.6 0.6 slice.33
  27.9 0.0 copy-start.3
  28.0 0.0 copy-start.4
  28.0 2.9 %stage.1 = (bf16[768,768]{1,0:T(8,128)(2,1)S(1)}, bf16[768,768]{1,0:T(8,128)(2,1)S(1)}, bf16[768,768]{1,0:T(8,128)(2,1)S(1)}, bf16[768,768]{1,0:T(8,128)(2,1)S(1)}, bf16[768,1024]{1,0:T(8,128)(2,1)S(1)}) custom-call(bf16[768,768]{1,0:T(8,128)(2,1)} %refs_0_.1, bf16[768,768]{1,0:T(8,128)(2,1)} %refs_1_.1, bf16[768,768]{1,0:T(8,128)(2,1)} %refs_2_.1, ...), custom_call_target="tpu_custom_call" | custom-call | bytes 12582912 | tf_op jit(solution)/shard_map/stage/pallas_call | solution.py:318
  30.9 2.8 %collective-permute-done.18 = bf16[4,200,384]{2,1,0:T(8,128)(2,1)} collective-permute-done((bf16[4,200,384]{2,1,0:T(8,128)(2,1)}, bf16[4,200,384]{2,1,0:T(8,128)(2,1)}, u32[]{:S(2)}, u32[]{:S(2)}) %collective-permute-start.18) | collective-permute-done | bytes 614432 | tf_op jit(solution)/shard_map/ppermute | solution.py:48
  33.7 1.2 %collective-permute-done.16 = bf16[4,200,384]{2,1,0:T(8,128)(2,1)} collective-permute-done((bf16[4,200,384]{2,1,0:T(8,128)(2,1)}, bf16[4,200,384]{2,1,0:T(8,128)(2,1)}, u32[]{:S(2)}, u32[]{:S(2)}) %collective-permute-start.16) | collective-permute-done | bytes 614432 | tf_op jit(solution)/shard_map/ppermute | solution.py:49
  34.9 25.6 %conditional.1 = (f32[2,4,196]{2,1,0:T(4,128)S(1)}) conditional(s32[]{:T(128)} %bitcast.4, (s32[7,8]{1,0:T(8,128)S(1)}, bf16[4,200,384]{2,1,0:T(8,128)(2,1)S(1)}, bf16[4,200,384]{2,1,0:T(8,128)(2,1)}, bf16[4,200,384]{2,1,0:T(8,128)(2,1)}, bf16[4,200,384]{2,1,0:T(8,128)(2,1)}, /*index=5*/bf16[4,200,384]{2,1,0:T(8,128)(2,1)}, ...), branch_computations={%region_0.1_spmd, %region_1.2_spmd, %region_2.4_spmd} | conditional | flops 23520 | bytes 13824340 | solution.py:557
  34.9 2.6 %pick.7 = bf16[4,200,384]{2,1,0:T(8,128)(2,1)S(1)} custom-call(s32[7,8]{1,0:T(8,128)S(1)} %get-tuple-element.108.table, bf16[4,200,384]{2,1,0:T(8,128)(2,1)S(1)} %get-tuple-element.110.refs_0_, bf16[4,200,384]{2,1,0:T(8,128)(2,1)} %get-tuple-element.111.refs_1_, bf16[4,200,384]{2,1,0:T(8,128)(2,1)} %get-tuple-element.112.refs_2_, ...), custom_call_target="tpu_custom_call" | custom-call | bytes 1228800 | tf_op jit(solution)/shard_map/cond/branch_0_fun/pick/pallas_call | solution.py:290
  37.4 0.1 collective-permute-start.5
  37.5 2.6 %pick.6.refs_0_ = bf16[4,200,384]{2,1,0:T(8,128)(2,1)S(1)} custom-call(s32[7,8]{1,0:T(8,128)S(1)} %get-tuple-element.108.table, bf16[4,200,384]{2,1,0:T(8,128)(2,1)S(1)} %get-tuple-element.110.refs_0_, bf16[4,200,384]{2,1,0:T(8,128)(2,1)} %get-tuple-element.111.refs_1_, bf16[4,200,384]{2,1,0:T(8,128)(2,1)} %get-tuple-element.112.refs_2_, ...), custom_call_target="tpu_custom_call" | custom-call | bytes 1228800 | tf_op jit(solution)/shard_map/cond/branch_0_fun/pick/pallas_call | solution.py:290
  40.1 0.0 collective-permute-done.5.refs_1_
  40.1 11.6 %decode.3 = (f32[12,4,196]{2,1,0:T(4,128)S(1)}, f32[8,4,196]{2,1,0:T(4,128)S(1)}) custom-call(s32[7,8]{1,0:T(8,128)S(1)} %get-tuple-element.108.table, bf16[4,200,384]{2,1,0:T(8,128)(2,1)S(1)} %pick.6.refs_0_, bf16[4,200,384]{2,1,0:T(8,128)(2,1)S(1)} %collective-permute-done.5.refs_1_, f32[1,768]{1,0:T(1,128)S(1)} %get-tuple-element.120.refs_2_, ...), custom_call_target="tpu_custom_call" | custom-call | tf_op jit(solution)/shard_map/cond/branch_0_fun/decode/pallas_call | solution.py:497
  51.7 0.5 collective-permute-start.6
  52.2 0.9 %collective-permute-done.6 = f32[8,4,196]{2,1,0:T(4,128)S(1)} collective-permute-done((f32[8,4,196]{2,1,0:T(4,128)S(1)}, f32[8,4,196]{2,1,0:T(4,128)S(1)}, u32[]{:S(2)}, u32[]{:S(2)}) %collective-permute-start.6) | collective-permute-done | bytes 25120 | tf_op jit(solution)/shard_map/cond/branch_0_fun/ppermute | solution.py:521
  53.1 1.6 %collective-permute-start.7 = (f32[4,4,196]{2,1,0:T(4,128)S(1)}, f32[4,4,196]{2,1,0:T(4,128)S(1)}, u32[]{:S(2)}, u32[]{:S(2)}) collective-permute-start(f32[4,4,196]{2,1,0:T(4,128)S(1)} %get-tuple-element.174), channel_id=1, source_target_pairs={{0,4},{1,9},{4,8},{5,13},{8,12},{9,15},{12,14},{13,11},{14,10},{15... | collective-permute-start | bytes 37640 | tf_op jit(solution)/shard_map/cond/branch_0_fun/ppermute | solution.py:530
  54.8 0.4 collective-permute-start.8
  55.2 1.7 %collective-permute-done.7 = f32[4,4,196]{2,1,0:T(4,128)S(1)} collective-permute-done((f32[4,4,196]{2,1,0:T(4,128)S(1)}, f32[4,4,196]{2,1,0:T(4,128)S(1)}, u32[]{:S(2)}, u32[]{:S(2)}) %collective-permute-start.7) | collective-permute-done | bytes 12576 | tf_op jit(solution)/shard_map/cond/branch_0_fun/ppermute | solution.py:530
  56.9 1.8 %collective-permute-done.8 = f32[4,4,196]{2,1,0:T(4,128)S(1)} collective-permute-done((f32[4,4,196]{2,1,0:T(4,128)S(1)}, f32[4,4,196]{2,1,0:T(4,128)S(1)}, u32[]{:S(2)}, u32[]{:S(2)}) %collective-permute-start.8) | collective-permute-done | bytes 12576 | tf_op jit(solution)/shard_map/cond/branch_0_fun/ppermute | solution.py:531
  58.7 0.9 %collective-permute-start.9 = (f32[2,4,196]{2,1,0:T(4,128)S(1)}, f32[2,4,196]{2,1,0:T(4,128)S(1)}, u32[]{:S(2)}, u32[]{:S(2)}) collective-permute-start(f32[2,4,196]{2,1,0:T(4,128)S(1)} %constant_dynamic-slice_fusion), channel_id=1, source_target_pairs={{0,1},{1,0},{2,3},{3,2},{4,5},{5,4},{6,7},{7,6},{8,9},{9,8},{10,11... | collective-permute-start | bytes 18824 | tf_op jit(solution)/shard_map/cond/branch_0_fun/ppermute | solution.py:534
  59.6 0.8 %collective-permute-done.9 = f32[2,4,196]{2,1,0:T(4,128)S(1)} collective-permute-done((f32[2,4,196]{2,1,0:T(4,128)S(1)}, f32[2,4,196]{2,1,0:T(4,128)S(1)}, u32[]{:S(2)}, u32[]{:S(2)}) %collective-permute-start.9) | collective-permute-done | bytes 6304 | tf_op jit(solution)/shard_map/cond/branch_0_fun/ppermute | solution.py:534
  60.4 0.6 copy-done.5
  (22 shorter events, 0.1 us)
Async XLA Ops:
  0.0 20.3 %copy-start.6 = (f32[768]{0:T(1024)S(1)}, f32[768]{0:T(1024)}, u32[]{:S(2)}) copy-start(f32[768]{0:T(1024)} %param.18) | copy-start | bytes 9220
  0.0 20.3 %copy-start.7 = (f32[768]{0:T(1024)S(1)}, f32[768]{0:T(1024)}, u32[]{:S(2)}) copy-start(f32[768]{0:T(1024)} %param.19) | copy-start | bytes 9220
  0.0 20.3 %copy-start.8 = (f32[768]{0:T(1024)S(1)}, f32[768]{0:T(1024)}, u32[]{:S(2)}) copy-start(f32[768]{0:T(1024)} %param.24) | copy-start | bytes 9220
  0.0 20.4 %copy-start.2 = (s32[8]{0:T(128)S(1)}, s32[8]{0:T(128)}, u32[]{:S(2)}) copy-start(s32[8]{0:T(128)} %counts.1) | copy-start | bytes 100
  0.0 20.4 %copy-start.1 = (s32[96]{0:T(128)S(1)}, s32[96]{0:T(128)}, u32[]{:S(2)}) copy-start(s32[96]{0:T(128)} %locals_.1) | copy-start | bytes 1156
  0.0 20.4 %copy-start = (s32[96,1]{0,1:T(1,128)S(1)}, s32[96,1]{0,1:T(1,128)}, u32[]{:S(2)}) copy-start(s32[96,1]{0,1:T(1,128)} %param.28) | copy-start | bytes 1156
  1.3 17.0 %collective-permute-start.17 = (bf16[4,200,384]{2,1,0:T(8,128)(2,1)S(1)}, bf16[4,200,384]{2,1,0:T(8,128)(2,1)}, u32[]{:S(2)}, u32[]{:S(2)}) collective-permute-start(bf16[4,200,384]{2,1,0:T(8,128)(2,1)S(1)} %pad.4), channel_id=1, source_target_pairs={{0,4},{4,8},{8,12},{12,14},{14,10},{10,6},{6,2},{2,0},{1,5},{5,9},... | collective-permute-start | bytes 1843208 | tf_op jit(solution)/shard_map/ppermute | solution.py:48
  4.4 15.7 %collective-permute-start.15 = (bf16[4,200,384]{2,1,0:T(8,128)(2,1)S(1)}, bf16[4,200,384]{2,1,0:T(8,128)(2,1)}, u32[]{:S(2)}, u32[]{:S(2)}) collective-permute-start(bf16[4,200,384]{2,1,0:T(8,128)(2,1)S(1)} %pad.4), channel_id=1, source_target_pairs={{4,0},{8,4},{12,8},{14,12},{10,14},{6,10},{2,6},{0,2},{5,1},{9,5},... | collective-permute-start | bytes 1843208 | tf_op jit(solution)/shard_map/ppermute | solution.py:49
  18.3 15.4 %collective-permute-start.18 = (bf16[4,200,384]{2,1,0:T(8,128)(2,1)}, bf16[4,200,384]{2,1,0:T(8,128)(2,1)}, u32[]{:S(2)}, u32[]{:S(2)}) collective-permute-start(bf16[4,200,384]{2,1,0:T(8,128)(2,1)} %collective-permute-done.17), channel_id=1, source_target_pairs={{0,4},{4,8},{8,12},{12,14},{14,10},{10,6},{6,2},{2,0},{1,5},{5,9},... | collective-permute-start | bytes 1843208 | tf_op jit(solution)/shard_map/ppermute | solution.py:48
  20.1 14.8 %collective-permute-start.16 = (bf16[4,200,384]{2,1,0:T(8,128)(2,1)}, bf16[4,200,384]{2,1,0:T(8,128)(2,1)}, u32[]{:S(2)}, u32[]{:S(2)}) collective-permute-start(bf16[4,200,384]{2,1,0:T(8,128)(2,1)} %collective-permute-done.15), channel_id=1, source_target_pairs={{4,0},{8,4},{12,8},{14,12},{10,14},{6,10},{2,6},{0,2},{5,1},{9,5},... | collective-permute-start | bytes 1843208 | tf_op jit(solution)/shard_map/ppermute | solution.py:49
  27.9 6.9 %copy-start.3 = (bf16[4,1024]{1,0:T(4,128)(2,1)S(1)}, bf16[4,1024]{1,0:T(4,128)(2,1)}, u32[]{:S(2)}) copy-start(bf16[4,1024]{1,0:T(4,128)(2,1)} %param.27) | copy-start | bytes 24580
  28.0 6.9 %copy-start.4 = (f32[1024]{0:T(1024)S(1)}, f32[1024]{0:T(1024)}, u32[]{:S(2)}) copy-start(f32[1024]{0:T(1024)} %param.26) | copy-start | bytes 12292
  37.4 2.7 %collective-permute-start.5 = (bf16[4,200,384]{2,1,0:T(8,128)(2,1)S(1)}, bf16[4,200,384]{2,1,0:T(8,128)(2,1)S(1)}, u32[]{:S(2)}, u32[]{:S(2)}) collective-permute-start(bf16[4,200,384]{2,1,0:T(8,128)(2,1)S(1)} %pick.7), channel_id=1, source_target_pairs={{0,1},{1,0},{2,3},{3,2},{4,5},{5,4},{6,7},{7,6},{8,9},{9,8},{10,11... | collective-permute-start | bytes 1843208 | tf_op jit(solution)/shard_map/cond/branch_0_fun/ppermute | solution.py:331
  51.7 1.4 %collective-permute-start.6 = (f32[8,4,196]{2,1,0:T(4,128)S(1)}, f32[8,4,196]{2,1,0:T(4,128)S(1)}, u32[]{:S(2)}, u32[]{:S(2)}) collective-permute-start(f32[8,4,196]{2,1,0:T(4,128)S(1)} %get-tuple-element.126), channel_id=1, source_target_pairs={{0,1},{1,0},{2,3},{3,2},{4,5},{5,4},{6,7},{7,6},{8,9},{9,8},{10,11... | collective-permute-start | bytes 75272 | tf_op jit(solution)/shard_map/cond/branch_0_fun/ppermute | solution.py:521
  53.1 3.8 %collective-permute-start.7 = (f32[4,4,196]{2,1,0:T(4,128)S(1)}, f32[4,4,196]{2,1,0:T(4,128)S(1)}, u32[]{:S(2)}, u32[]{:S(2)}) collective-permute-start(f32[4,4,196]{2,1,0:T(4,128)S(1)} %get-tuple-element.174), channel_id=1, source_target_pairs={{0,4},{1,9},{4,8},{5,13},{8,12},{9,15},{12,14},{13,11},{14,10},{15... | collective-permute-start | bytes 37640 | tf_op jit(solution)/shard_map/cond/branch_0_fun/ppermute | solution.py:530
  54.8 3.9 %collective-permute-start.8 = (f32[4,4,196]{2,1,0:T(4,128)S(1)}, f32[4,4,196]{2,1,0:T(4,128)S(1)}, u32[]{:S(2)}, u32[]{:S(2)}) collective-permute-start(f32[4,4,196]{2,1,0:T(4,128)S(1)} %get-tuple-element.175), channel_id=1, source_target_pairs={{4,0},{9,1},{8,4},{13,5},{12,8},{15,9},{14,12},{11,13},{10,14},{7,... | collective-permute-start | bytes 37640 | tf_op jit(solution)/shard_map/cond/branch_0_fun/ppermute | solution.py:531
  58.7 1.7 %collective-permute-start.9 = (f32[2,4,196]{2,1,0:T(4,128)S(1)}, f32[2,4,196]{2,1,0:T(4,128)S(1)}, u32[]{:S(2)}, u32[]{:S(2)}) collective-permute-start(f32[2,4,196]{2,1,0:T(4,128)S(1)} %constant_dynamic-slice_fusion), channel_id=1, source_target_pairs={{0,1},{1,0},{2,3},{3,2},{4,5},{5,4},{6,7},{7,6},{8,9},{9,8},{10,11... | collective-permute-start | bytes 18824 | tf_op jit(solution)/shard_map/cond/branch_0_fun/ppermute | solution.py:534
  60.4 0.6 copy-start.5

commit v7 on v6

--- a/solution.py
+++ b/solution.py
@@ -293,7 +293,7 @@
         in_specs=[pl.BlockSpec(memory_space=pltpu.SMEM)]
         + [pl.BlockSpec(memory_space=space)] * len(keys)
         + [pl.BlockSpec(memory_space=pltpu.VMEM)] * len(held),
-        out_specs=pl.BlockSpec(memory_space=pltpu.VMEM),
+        out_specs=pl.BlockSpec(memory_space=pl.ANY),
         scratch_shapes=[pltpu.SemaphoreType.DMA((4,))],
         compiler_params=pltpu.CompilerParams(vmem_limit_bytes=8 * 1024 * 1024),
         cost_estimate=pl.CostEstimate(

time: 61.2 us -> 61.2 us (level)
  Pallas kernels: 25.8 us -> 27.2 us
  waiting for transfers between devices: 23 us -> 21.6 us
    pallas_call x1, Pallas kernels: 6.18 us -> 7.62 us  [per_device(): pl.pallas_call(functools.partial(deal_kernel, worker_count, image_count,...]
    ppermute x2, waiting for transfers between devices: 16.7 us -> 15.2 us  [ring_near(): going = lax.ppermute(going, 'pairs', ahead)]
  transfers between devices with their start and end apart: 9 -> 9, of which waited for: 7 -> 7; matrix products, arithmetic and copies ran while one was open for 1% -> 1% of each run, Pallas kernels for 19% -> 21%
where the time goes in v7:
time: 61.2 us; the launch traced here: 61 us
  Pallas kernels  27.2 us (44%)
  waiting for transfers between devices  21.6 us (35%)
  starting transfers between devices  8.7 us (14%)
  local copies, waits for them, and re-layouts  2.53 us (4%)
  between operations  0.79 us (1%)
    ppermute x2, waiting for transfers between devices, ring_near(): going = lax.ppermute(going, 'pairs', ahead)  15.2 us
    pallas_call x1, Pallas kernels, decode(): pl.pallas_call(functools.partial(decode_kernel, token_count), out_shape=t...  11.6 us
    pallas_call x1, Pallas kernels, per_device(): pl.pallas_call(functools.partial(deal_kernel, worker_count, image_count,...  7.62 us
    pallas_call x2, Pallas kernels, pick(): pl.pallas_call(functools.partial(pick_kernel, keys, first_column), out_sh...  5.14 us
    ppermute x2, starting transfers between devices, ring_near(): going = lax.ppermute(going, 'pairs', ahead)  4.87 us
    pallas_call x1, Pallas kernels, stage(): pl.pallas_call(functools.partial(stage_kernel, count), out_shape=tuple((j...  2.89 us
    unnamed x19, local copies, waits for them, and re-layouts  1.85 us
    ppermute x1, waiting for transfers between devices, decode_near(): total = total + lax.ppermute(leaving[image_count:], axes, back)  1.74 us
  transfers between devices with their start and end apart: 9, of which 7 were waited for; matrix products, arithmetic and copies ran while one was open for 1% of the time, Pallas kernels for 21%

profile of v7, /device:TPU:0, one launch (start us, length us, event | category | flops | bytes accessed | tf_op | source)
XLA Modules:
  0.0 61.0 jit_solution(16504238315464240288)
XLA Ops:
  0.0 0.0 copy-start
  0.0 1.2 %copy.18 = bf16[4,196,384]{2,1,0:T(8,128)(2,1)S(1)} copy(bf16[4,196,384]{2,0,1:T(4,128)(2,1)} %param.17) | data formatting | bytes 1204224 | tf_op args[0]
  1.2 0.1 pad.4
  1.3 3.1 %collective-permute-start.17 = (bf16[4,200,384]{2,1,0:T(8,128)(2,1)S(1)}, bf16[4,200,384]{2,1,0:T(8,128)(2,1)}, u32[]{:S(2)}, u32[]{:S(2)}) collective-permute-start(bf16[4,200,384]{2,1,0:T(8,128)(2,1)S(1)} %pad.4), channel_id=1, source_target_pairs={{0,4},{4,8},{8,12},{12,14},{14,10},{10,6},{6,2},{2,0},{1,5},{5,9},... | collective-permute-start | bytes 1843208 | tf_op jit(solution)/shard_map/ppermute | solution.py:48
  4.4 0.0 collective-permute-start.15
  4.4 13.9 %collective-permute-done.17 = bf16[4,200,384]{2,1,0:T(8,128)(2,1)} collective-permute-done((bf16[4,200,384]{2,1,0:T(8,128)(2,1)S(1)}, bf16[4,200,384]{2,1,0:T(8,128)(2,1)}, u32[]{:S(2)}, u32[]{:S(2)}) %collective-permute-start.17) | collective-permute-done | bytes 614432 | tf_op jit(solution)/shard_map/ppermute | solution.py:48
  18.3 1.8 %collective-permute-start.18 = (bf16[4,200,384]{2,1,0:T(8,128)(2,1)}, bf16[4,200,384]{2,1,0:T(8,128)(2,1)}, u32[]{:S(2)}, u32[]{:S(2)}) collective-permute-start(bf16[4,200,384]{2,1,0:T(8,128)(2,1)} %collective-permute-done.17), channel_id=1, source_target_pairs={{0,4},{4,8},{8,12},{12,14},{14,10},{10,6},{6,2},{2,0},{1,5},{5,9},... | collective-permute-start | bytes 1843208 | tf_op jit(solution)/shard_map/ppermute | solution.py:48
  20.1 0.0 collective-permute-done.15
  20.1 0.2 collective-permute-start.16
  20.4 0.1 pad_add_fusion.me
  20.5 7.6 %deal.1 = s32[7,8]{1,0:T(8,128)S(1)} custom-call(s32[96]{0:T(128)S(1)} %bitcast.6, s32[96]{0:T(128)S(1)} %copy-done.1, s32[8]{0:T(128)S(1)} %copy-done.2, s32[2]{0:T(128)S(1)} %pad_add_fusion.me), custom_call_target="tpu_custom_call" | custom-call | bytes 20000000 | tf_op jit(solution)/shard_map/deal/pallas_call | solution.py:539
  28.1 0.6 slice.33
  29.4 0.0 copy-start.3
  29.4 0.0 copy-start.4
  29.4 2.9 %stage.1 = (bf16[768,768]{1,0:T(8,128)(2,1)S(1)}, bf16[768,768]{1,0:T(8,128)(2,1)S(1)}, bf16[768,768]{1,0:T(8,128)(2,1)S(1)}, bf16[768,768]{1,0:T(8,128)(2,1)S(1)}, bf16[768,1024]{1,0:T(8,128)(2,1)S(1)}) custom-call(bf16[768,768]{1,0:T(8,128)(2,1)} %refs_0_.1, bf16[768,768]{1,0:T(8,128)(2,1)} %refs_1_.1, bf16[768,768]{1,0:T(8,128)(2,1)} %refs_2_.1, ...), custom_call_target="tpu_custom_call" | custom-call | bytes 12582912 | tf_op jit(solution)/shard_map/stage/pallas_call | solution.py:318
  32.3 1.3 %collective-permute-done.18 = bf16[4,200,384]{2,1,0:T(8,128)(2,1)} collective-permute-done((bf16[4,200,384]{2,1,0:T(8,128)(2,1)}, bf16[4,200,384]{2,1,0:T(8,128)(2,1)}, u32[]{:S(2)}, u32[]{:S(2)}) %collective-permute-start.18) | collective-permute-done | bytes 614432 | tf_op jit(solution)/shard_map/ppermute | solution.py:48
  33.7 1.2 %collective-permute-done.16 = bf16[4,200,384]{2,1,0:T(8,128)(2,1)} collective-permute-done((bf16[4,200,384]{2,1,0:T(8,128)(2,1)}, bf16[4,200,384]{2,1,0:T(8,128)(2,1)}, u32[]{:S(2)}, u32[]{:S(2)}) %collective-permute-start.16) | collective-permute-done | bytes 614432 | tf_op jit(solution)/shard_map/ppermute | solution.py:49
  34.9 25.6 %conditional.1 = (f32[2,4,196]{2,1,0:T(4,128)S(1)}) conditional(s32[]{:T(128)} %bitcast.4, (s32[7,8]{1,0:T(8,128)S(1)}, bf16[4,200,384]{2,1,0:T(8,128)(2,1)S(1)}, bf16[4,200,384]{2,1,0:T(8,128)(2,1)}, bf16[4,200,384]{2,1,0:T(8,128)(2,1)}, bf16[4,200,384]{2,1,0:T(8,128)(2,1)}, /*index=5*/bf16[4,200,384]{2,1,0:T(8,128)(2,1)}, ...), branch_computations={%region_0.1_spmd, %region_1.2_spmd, %region_2.4_spmd} | conditional | flops 23520 | bytes 13824340 | solution.py:557
  34.9 2.6 %pick.7 = bf16[4,200,384]{2,1,0:T(8,128)(2,1)S(1)} custom-call(s32[7,8]{1,0:T(8,128)S(1)} %get-tuple-element.108.table, bf16[4,200,384]{2,1,0:T(8,128)(2,1)S(1)} %get-tuple-element.110.refs_0_, bf16[4,200,384]{2,1,0:T(8,128)(2,1)} %get-tuple-element.111.refs_1_, bf16[4,200,384]{2,1,0:T(8,128)(2,1)} %get-tuple-element.112.refs_2_, ...), custom_call_target="tpu_custom_call" | custom-call | bytes 1228800 | tf_op jit(solution)/shard_map/cond/branch_0_fun/pick/pallas_call | solution.py:290
  37.4 0.1 collective-permute-start.5
  37.5 2.6 %pick.6.refs_0_ = bf16[4,200,384]{2,1,0:T(8,128)(2,1)S(1)} custom-call(s32[7,8]{1,0:T(8,128)S(1)} %get-tuple-element.108.table, bf16[4,200,384]{2,1,0:T(8,128)(2,1)S(1)} %get-tuple-element.110.refs_0_, bf16[4,200,384]{2,1,0:T(8,128)(2,1)} %get-tuple-element.111.refs_1_, bf16[4,200,384]{2,1,0:T(8,128)(2,1)} %get-tuple-element.112.refs_2_, ...), custom_call_target="tpu_custom_call" | custom-call | bytes 1228800 | tf_op jit(solution)/shard_map/cond/branch_0_fun/pick/pallas_call | solution.py:290
  40.1 0.0 collective-permute-done.5.refs_1_
  40.1 11.6 %decode.3 = (f32[12,4,196]{2,1,0:T(4,128)S(1)}, f32[8,4,196]{2,1,0:T(4,128)S(1)}) custom-call(s32[7,8]{1,0:T(8,128)S(1)} %get-tuple-element.108.table, bf16[4,200,384]{2,1,0:T(8,128)(2,1)S(1)} %pick.6.refs_0_, bf16[4,200,384]{2,1,0:T(8,128)(2,1)S(1)} %collective-permute-done.5.refs_1_, f32[1,768]{1,0:T(1,128)S(1)} %get-tuple-element.120.refs_2_, ...), custom_call_target="tpu_custom_call" | custom-call | tf_op jit(solution)/shard_map/cond/branch_0_fun/decode/pallas_call | solution.py:497
  51.7 0.5 collective-permute-start.6
  52.2 0.9 %collective-permute-done.6 = f32[8,4,196]{2,1,0:T(4,128)S(1)} collective-permute-done((f32[8,4,196]{2,1,0:T(4,128)S(1)}, f32[8,4,196]{2,1,0:T(4,128)S(1)}, u32[]{:S(2)}, u32[]{:S(2)}) %collective-permute-start.6) | collective-permute-done | bytes 25120 | tf_op jit(solution)/shard_map/cond/branch_0_fun/ppermute | solution.py:521
  53.1 1.6 %collective-permute-start.7 = (f32[4,4,196]{2,1,0:T(4,128)S(1)}, f32[4,4,196]{2,1,0:T(4,128)S(1)}, u32[]{:S(2)}, u32[]{:S(2)}) collective-permute-start(f32[4,4,196]{2,1,0:T(4,128)S(1)} %get-tuple-element.174), channel_id=1, source_target_pairs={{0,4},{1,9},{4,8},{5,13},{8,12},{9,15},{12,14},{13,11},{14,10},{15... | collective-permute-start | bytes 37640 | tf_op jit(solution)/shard_map/cond/branch_0_fun/ppermute | solution.py:530
  54.8 0.5 collective-permute-start.8
  55.2 1.7 %collective-permute-done.7 = f32[4,4,196]{2,1,0:T(4,128)S(1)} collective-permute-done((f32[4,4,196]{2,1,0:T(4,128)S(1)}, f32[4,4,196]{2,1,0:T(4,128)S(1)}, u32[]{:S(2)}, u32[]{:S(2)}) %collective-permute-start.7) | collective-permute-done | bytes 12576 | tf_op jit(solution)/shard_map/cond/branch_0_fun/ppermute | solution.py:530
  56.9 1.7 %collective-permute-done.8 = f32[4,4,196]{2,1,0:T(4,128)S(1)} collective-permute-done((f32[4,4,196]{2,1,0:T(4,128)S(1)}, f32[4,4,196]{2,1,0:T(4,128)S(1)}, u32[]{:S(2)}, u32[]{:S(2)}) %collective-permute-start.8) | collective-permute-done | bytes 12576 | tf_op jit(solution)/shard_map/cond/branch_0_fun/ppermute | solution.py:531
  58.7 0.9 %collective-permute-start.9 = (f32[2,4,196]{2,1,0:T(4,128)S(1)}, f32[2,4,196]{2,1,0:T(4,128)S(1)}, u32[]{:S(2)}, u32[]{:S(2)}) collective-permute-start(f32[2,4,196]{2,1,0:T(4,128)S(1)} %constant_dynamic-slice_fusion), channel_id=1, source_target_pairs={{0,1},{1,0},{2,3},{3,2},{4,5},{5,4},{6,7},{7,6},{8,9},{9,8},{10,11... | collective-permute-start | bytes 18824 | tf_op jit(solution)/shard_map/cond/branch_0_fun/ppermute | solution.py:534
  59.6 0.8 %collective-permute-done.9 = f32[2,4,196]{2,1,0:T(4,128)S(1)} collective-permute-done((f32[2,4,196]{2,1,0:T(4,128)S(1)}, f32[2,4,196]{2,1,0:T(4,128)S(1)}, u32[]{:S(2)}, u32[]{:S(2)}) %collective-permute-start.9) | collective-permute-done | bytes 6304 | tf_op jit(solution)/shard_map/cond/branch_0_fun/ppermute | solution.py:534
  60.4 0.6 copy-done.5
  (22 shorter events, 0.1 us)
Async XLA Ops:
  0.0 20.3 %copy-start.6 = (f32[768]{0:T(1024)S(1)}, f32[768]{0:T(1024)}, u32[]{:S(2)}) copy-start(f32[768]{0:T(1024)} %param.18) | copy-start | bytes 9220
  0.0 20.3 %copy-start.7 = (f32[768]{0:T(1024)S(1)}, f32[768]{0:T(1024)}, u32[]{:S(2)}) copy-start(f32[768]{0:T(1024)} %param.19) | copy-start | bytes 9220
  0.0 20.3 %copy-start.8 = (f32[768]{0:T(1024)S(1)}, f32[768]{0:T(1024)}, u32[]{:S(2)}) copy-start(f32[768]{0:T(1024)} %param.24) | copy-start | bytes 9220
  0.0 20.4 %copy-start.2 = (s32[8]{0:T(128)S(1)}, s32[8]{0:T(128)}, u32[]{:S(2)}) copy-start(s32[8]{0:T(128)} %counts.1) | copy-start | bytes 100
  0.0 20.4 %copy-start.1 = (s32[96]{0:T(128)S(1)}, s32[96]{0:T(128)}, u32[]{:S(2)}) copy-start(s32[96]{0:T(128)} %locals_.1) | copy-start | bytes 1156
  0.0 20.4 %copy-start = (s32[96,1]{0,1:T(1,128)S(1)}, s32[96,1]{0,1:T(1,128)}, u32[]{:S(2)}) copy-start(s32[96,1]{0,1:T(1,128)} %param.28) | copy-start | bytes 1156
  1.3 17.0 %collective-permute-start.17 = (bf16[4,200,384]{2,1,0:T(8,128)(2,1)S(1)}, bf16[4,200,384]{2,1,0:T(8,128)(2,1)}, u32[]{:S(2)}, u32[]{:S(2)}) collective-permute-start(bf16[4,200,384]{2,1,0:T(8,128)(2,1)S(1)} %pad.4), channel_id=1, source_target_pairs={{0,4},{4,8},{8,12},{12,14},{14,10},{10,6},{6,2},{2,0},{1,5},{5,9},... | collective-permute-start | bytes 1843208 | tf_op jit(solution)/shard_map/ppermute | solution.py:48
  4.4 15.7 %collective-permute-start.15 = (bf16[4,200,384]{2,1,0:T(8,128)(2,1)S(1)}, bf16[4,200,384]{2,1,0:T(8,128)(2,1)}, u32[]{:S(2)}, u32[]{:S(2)}) collective-permute-start(bf16[4,200,384]{2,1,0:T(8,128)(2,1)S(1)} %pad.4), channel_id=1, source_target_pairs={{4,0},{8,4},{12,8},{14,12},{10,14},{6,10},{2,6},{0,2},{5,1},{9,5},... | collective-permute-start | bytes 1843208 | tf_op jit(solution)/shard_map/ppermute | solution.py:49
  18.3 15.4 %collective-permute-start.18 = (bf16[4,200,384]{2,1,0:T(8,128)(2,1)}, bf16[4,200,384]{2,1,0:T(8,128)(2,1)}, u32[]{:S(2)}, u32[]{:S(2)}) collective-permute-start(bf16[4,200,384]{2,1,0:T(8,128)(2,1)} %collective-permute-done.17), channel_id=1, source_target_pairs={{0,4},{4,8},{8,12},{12,14},{14,10},{10,6},{6,2},{2,0},{1,5},{5,9},... | collective-permute-start | bytes 1843208 | tf_op jit(solution)/shard_map/ppermute | solution.py:48
  20.1 14.8 %collective-permute-start.16 = (bf16[4,200,384]{2,1,0:T(8,128)(2,1)}, bf16[4,200,384]{2,1,0:T(8,128)(2,1)}, u32[]{:S(2)}, u32[]{:S(2)}) collective-permute-start(bf16[4,200,384]{2,1,0:T(8,128)(2,1)} %collective-permute-done.15), channel_id=1, source_target_pairs={{4,0},{8,4},{12,8},{14,12},{10,14},{6,10},{2,6},{0,2},{5,1},{9,5},... | collective-permute-start | bytes 1843208 | tf_op jit(solution)/shard_map/ppermute | solution.py:49
  29.4 5.5 %copy-start.3 = (bf16[4,1024]{1,0:T(4,128)(2,1)S(1)}, bf16[4,1024]{1,0:T(4,128)(2,1)}, u32[]{:S(2)}) copy-start(bf16[4,1024]{1,0:T(4,128)(2,1)} %param.27) | copy-start | bytes 24580
  29.4 5.5 %copy-start.4 = (f32[1024]{0:T(1024)S(1)}, f32[1024]{0:T(1024)}, u32[]{:S(2)}) copy-start(f32[1024]{0:T(1024)} %param.26) | copy-start | bytes 12292
  37.4 2.7 %collective-permute-start.5 = (bf16[4,200,384]{2,1,0:T(8,128)(2,1)S(1)}, bf16[4,200,384]{2,1,0:T(8,128)(2,1)S(1)}, u32[]{:S(2)}, u32[]{:S(2)}) collective-permute-start(bf16[4,200,384]{2,1,0:T(8,128)(2,1)S(1)} %pick.7), channel_id=1, source_target_pairs={{0,1},{1,0},{2,3},{3,2},{4,5},{5,4},{6,7},{7,6},{8,9},{9,8},{10,11... | collective-permute-start | bytes 1843208 | tf_op jit(solution)/shard_map/cond/branch_0_fun/ppermute | solution.py:331
  51.7 1.4 %collective-permute-start.6 = (f32[8,4,196]{2,1,0:T(4,128)S(1)}, f32[8,4,196]{2,1,0:T(4,128)S(1)}, u32[]{:S(2)}, u32[]{:S(2)}) collective-permute-start(f32[8,4,196]{2,1,0:T(4,128)S(1)} %get-tuple-element.126), channel_id=1, source_target_pairs={{0,1},{1,0},{2,3},{3,2},{4,5},{5,4},{6,7},{7,6},{8,9},{9,8},{10,11... | collective-permute-start | bytes 75272 | tf_op jit(solution)/shard_map/cond/branch_0_fun/ppermute | solution.py:521
  53.1 3.8 %collective-permute-start.7 = (f32[4,4,196]{2,1,0:T(4,128)S(1)}, f32[4,4,196]{2,1,0:T(4,128)S(1)}, u32[]{:S(2)}, u32[]{:S(2)}) collective-permute-start(f32[4,4,196]{2,1,0:T(4,128)S(1)} %get-tuple-element.174), channel_id=1, source_target_pairs={{0,4},{1,9},{4,8},{5,13},{8,12},{9,15},{12,14},{13,11},{14,10},{15... | collective-permute-start | bytes 37640 | tf_op jit(solution)/shard_map/cond/branch_0_fun/ppermute | solution.py:530
  54.8 3.9 %collective-permute-start.8 = (f32[4,4,196]{2,1,0:T(4,128)S(1)}, f32[4,4,196]{2,1,0:T(4,128)S(1)}, u32[]{:S(2)}, u32[]{:S(2)}) collective-permute-start(f32[4,4,196]{2,1,0:T(4,128)S(1)} %get-tuple-element.175), channel_id=1, source_target_pairs={{4,0},{9,1},{8,4},{13,5},{12,8},{15,9},{14,12},{11,13},{10,14},{7,... | collective-permute-start | bytes 37640 | tf_op jit(solution)/shard_map/cond/branch_0_fun/ppermute | solution.py:531
  58.7 1.7 %collective-permute-start.9 = (f32[2,4,196]{2,1,0:T(4,128)S(1)}, f32[2,4,196]{2,1,0:T(4,128)S(1)}, u32[]{:S(2)}, u32[]{:S(2)}) collective-permute-start(f32[2,4,196]{2,1,0:T(4,128)S(1)} %constant_dynamic-slice_fusion), channel_id=1, source_target_pairs={{0,1},{1,0},{2,3},{3,2},{4,5},{5,4},{6,7},{7,6},{8,9},{9,8},{10,11... | collective-permute-start | bytes 18824 | tf_op jit(solution)/shard_map/cond/branch_0_fun/ppermute | solution.py:534
  60.4 0.6 copy-start.5

commit v8 on v7

--- a/solution.py
+++ b/solution.py
@@ -351,33 +351,25 @@
     for out in outs:
         out[...] = jnp.zeros_like(out)
     tail = jnp.zeros((views, padded - rows, width), BF16)
-    xq[:, rows:, :] = tail
-    xc[:, rows:, :] = tail
+    att[:, rows:, :] = tail
     res[:, rows:, :] = tail
 
     here = pl.ds(pl.multiple_of(core * half, half), half)
     there = pl.ds(pl.multiple_of((1 - core) * half, half), half)
     context_of = (1, 0, None, 2) if views == 3 else (1, 0, 3, 2)
     for j in range(4):
-        raw_a, raw_b = mine[j], theirs[j]
-        a, b = raw_a.astype(F32), raw_b.astype(F32)
-        average = (
-            jnp.sum(a, axis=-1, keepdims=True) + jnp.sum(b, axis=-1, keepdims=True)
-        ) / width
-        a, b = a - average, b - average
-        variance = (
-            jnp.sum(a * a, axis=-1, keepdims=True) + jnp.sum(b * b, axis=-1, keepdims=True)
-        ) / width
-        scale = lax.rsqrt(variance + EPS)
-        a, b = a * scale, b * scale
+        whole, spot = (res, j) if j < views else (att, 0)
+        whole[spot, :rows, here] = mine[j]
+        whole[spot, :rows, there] = theirs[j]
+        full = whole[spot].astype(F32)
+        average = jnp.mean(full, axis=-1, keepdims=True)
+        full = full - average
+        variance = jnp.mean(full * full, axis=-1, keepdims=True)
+        full = full * lax.rsqrt(variance + EPS)
         if j < views:
-            xq[j, :rows, here] = (a * gain_q[:, here]).astype(BF16)
-            xq[j, :rows, there] = (b * gain_q[:, there]).astype(BF16)
-            res[j, :rows, here] = raw_a
-            res[j, :rows, there] = raw_b
+            xq[j] = (full * gain_q[...]).astype(BF16)
         if context_of[j] is not None:
-            xc[context_of[j], :rows, here] = (a * gain_c[:, here]).astype(BF16)
-            xc[context_of[j], :rows, there] = (b * gain_c[:, there]).astype(BF16)
+            xc[context_of[j]] = (full * gain_c[...]).astype(BF16)
 
     total = views * padded
     head_size = width // HEADS
@@ -513,7 +505,8 @@
         spots = (worker_count * image_count,)
         (flat,) = decode(views, spots, table, parts, vectors, weights)
         arrived = lax.all_to_all(flat, ("pairs", "mp"), 0, 0, tiled=True)
-        return jnp.sum(arrived.reshape(worker_count * core_count, mine, 4, token_count), axis=0)
+        arrived = arrived.reshape(worker_count * core_count, mine, 4, token_count)
+        return jnp.sum(arrived, axis=0), jnp.zeros_like(arrived[0])
 
     def decode_near(views, table, parts, vectors, weights):
         spots = (3 * image_count, 2 * image_count)
@@ -531,7 +524,7 @@
         total = total + lax.ppermute(leaving[image_count:], axes, back)
         theirs = lax.dynamic_slice_in_dim(total, (1 - core) * mine, mine, 0)
         ours = lax.dynamic_slice_in_dim(total, core * mine, mine, 0)
-        return ours + lax.ppermute(theirs, "mp", swap)
+        return ours, lax.ppermute(theirs, "mp", swap)
 
     if worker_count == 8:
         reach = 2
@@ -554,7 +547,7 @@
         def decode_far(table, near, *rest):
             return decode_any(MOST, table, ring_far(near, worker_count, reach), *rest)
 
-        return lax.switch(
+        ours, theirs = lax.switch(
             table[LEVEL, 0],
             (
                 functools.partial(decode_near, SHARE),
@@ -566,9 +559,11 @@
             vectors,
             weights,
         )
+        return ours + theirs
     table = plan(owners, view_local, pair_count, worker, core, image_count, worker_count)
     parts = ring_far({0: shard, worker_count: shard}, worker_count, 0)
-    return decode_any(SHARE, table, parts, vectors, weights)
+    ours, theirs = decode_any(SHARE, table, parts, vectors, weights)
+    return ours + theirs
 
 
 def solution(mesh):

time: 61.2 us -> 61.6 us (level)
  other arithmetic: 0.1 us -> 1.39 us
    ppermute x2, waiting for transfers between devices: 15.2 us -> 1.09 us  [ring_near(): going = lax.ppermute(going, 'pairs', ahead)]
    ppermute x2, waiting for transfers between devices: 1.2 us -> 15.3 us  [ring_near(): coming = lax.ppermute(coming, 'pairs', back)]
    ppermute x2, starting transfers between devices: 0.24 us -> 4.7 us  [ring_near(): coming = lax.ppermute(coming, 'pairs', back)]
    ppermute x2, starting transfers between devices: 4.87 us -> 0.47 us  [ring_near(): going = lax.ppermute(going, 'pairs', ahead)]
    add x1, other arithmetic: 0.01 us -> 1.3 us  [per_device(): return ours + theirs]
    ppermute x1, starting transfers between devices: 1.62 us -> 0.44 us  [decode_near(): lax.ppermute(leaving[:image_count], axes, ahead)]
    ppermute x1, starting transfers between devices: 0.46 us -> 1.64 us  [decode_near(): total = total + lax.ppermute(leaving[image_count:], axes, back)]
    unnamed x19 -> x17, local copies, waits for them, and re-layouts: 1.85 us -> 1.25 us
where the time goes in v8:
time: 61.6 us; the launch traced here: 61.4 us
  Pallas kernels  26.8 us (44%)
  waiting for transfers between devices  21.5 us (35%)
  starting transfers between devices  8.93 us (14%)
  local copies, waits for them, and re-layouts  1.93 us (3%)
  other arithmetic  1.39 us (2%)
  between operations  0.77 us (1%)
    ppermute x2, waiting for transfers between devices, ring_near(): coming = lax.ppermute(coming, 'pairs', back)  15.3 us
    pallas_call x1, Pallas kernels, decode(): pl.pallas_call(functools.partial(decode_kernel, token_count), out_shape=t...  11.2 us
    pallas_call x1, Pallas kernels, per_device(): pl.pallas_call(functools.partial(deal_kernel, worker_count, image_count,...  7.6 us
    pallas_call x2, Pallas kernels, pick(): pl.pallas_call(functools.partial(pick_kernel, keys, first_column), out_sh...  5.14 us
    ppermute x2, starting transfers between devices, ring_near(): coming = lax.ppermute(coming, 'pairs', back)  4.7 us
    pallas_call x1, Pallas kernels, stage(): pl.pallas_call(functools.partial(stage_kernel, count), out_shape=tuple((j...  2.89 us
    ppermute x1, waiting for transfers between devices, decode_near(): total = total + lax.ppermute(leaving[image_count:], axes, back)  1.71 us
    ppermute x1, starting transfers between devices, decode_near(): total = total + lax.ppermute(leaving[image_count:], axes, back)  1.64 us
  transfers between devices with their start and end apart: 9, of which 7 were waited for; matrix products, arithmetic and copies ran while one was open for 1% of the time, Pallas kernels for 21%

profile of v8, /device:TPU:0, one launch (start us, length us, event | category | flops | bytes accessed | tf_op | source)
XLA Modules:
  0.0 61.4 jit_solution(11261127922546232048)
XLA Ops:
  0.0 1.2 %copy.15 = bf16[4,196,384]{2,1,0:T(8,128)(2,1)S(1)} copy(bf16[4,196,384]{2,0,1:T(4,128)(2,1)} %param.17) | data formatting | bytes 1204224 | tf_op args[0]
  1.2 0.1 pad.4
  1.3 3.0 %collective-permute-start.15 = (bf16[4,200,384]{2,1,0:T(8,128)(2,1)S(1)}, bf16[4,200,384]{2,1,0:T(8,128)(2,1)}, u32[]{:S(2)}, u32[]{:S(2)}) collective-permute-start(bf16[4,200,384]{2,1,0:T(8,128)(2,1)S(1)} %pad.4), channel_id=1, source_target_pairs={{4,0},{8,4},{12,8},{14,12},{10,14},{6,10},{2,6},{0,2},{5,1},{9,5},... | collective-permute-start | bytes 1843208 | tf_op jit(solution)/shard_map/ppermute | solution.py:49
  4.3 0.1 collective-permute-start.17
  4.5 13.9 %collective-permute-done.15 = bf16[4,200,384]{2,1,0:T(8,128)(2,1)} collective-permute-done((bf16[4,200,384]{2,1,0:T(8,128)(2,1)S(1)}, bf16[4,200,384]{2,1,0:T(8,128)(2,1)}, u32[]{:S(2)}, u32[]{:S(2)}) %collective-permute-start.15) | collective-permute-done | bytes 614432 | tf_op jit(solution)/shard_map/ppermute | solution.py:49
  18.4 1.7 %collective-permute-start.16 = (bf16[4,200,384]{2,1,0:T(8,128)(2,1)}, bf16[4,200,384]{2,1,0:T(8,128)(2,1)}, u32[]{:S(2)}, u32[]{:S(2)}) collective-permute-start(bf16[4,200,384]{2,1,0:T(8,128)(2,1)} %collective-permute-done.15), channel_id=1, source_target_pairs={{4,0},{8,4},{12,8},{14,12},{10,14},{6,10},{2,6},{0,2},{5,1},{9,5},... | collective-permute-start | bytes 1843208 | tf_op jit(solution)/shard_map/ppermute | solution.py:49
  20.0 0.0 collective-permute-done.17
  20.0 0.3 collective-permute-start.18
  20.4 0.1 pad_add_fusion.me
  20.5 0.0 copy-done.2
  20.5 7.6 %deal.1 = s32[7,8]{1,0:T(8,128)S(1)} custom-call(s32[96]{0:T(128)S(1)} %bitcast.6, s32[96]{0:T(128)S(1)} %copy-done.1, s32[8]{0:T(128)S(1)} %copy-done.2, s32[2]{0:T(128)S(1)} %pad_add_fusion.me), custom_call_target="tpu_custom_call" | custom-call | bytes 20000000 | tf_op jit(solution)/shard_map/deal/pallas_call | solution.py:532
  28.1 0.6 slice.33
  29.4 0.0 copy-start.3
  29.4 0.0 copy-start.4
  29.4 2.9 %stage.1 = (bf16[768,768]{1,0:T(8,128)(2,1)S(1)}, bf16[768,768]{1,0:T(8,128)(2,1)S(1)}, bf16[768,768]{1,0:T(8,128)(2,1)S(1)}, bf16[768,768]{1,0:T(8,128)(2,1)S(1)}, bf16[768,1024]{1,0:T(8,128)(2,1)S(1)}) custom-call(bf16[768,768]{1,0:T(8,128)(2,1)} %refs_0_.1, bf16[768,768]{1,0:T(8,128)(2,1)} %refs_1_.1, bf16[768,768]{1,0:T(8,128)(2,1)} %refs_2_.1, ...), custom_call_target="tpu_custom_call" | custom-call | bytes 12582912 | tf_op jit(solution)/shard_map/stage/pallas_call | solution.py:318
  32.3 1.4 %collective-permute-done.16 = bf16[4,200,384]{2,1,0:T(8,128)(2,1)} collective-permute-done((bf16[4,200,384]{2,1,0:T(8,128)(2,1)}, bf16[4,200,384]{2,1,0:T(8,128)(2,1)}, u32[]{:S(2)}, u32[]{:S(2)}) %collective-permute-start.16) | collective-permute-done | bytes 614432 | tf_op jit(solution)/shard_map/ppermute | solution.py:49
  33.7 1.1 %collective-permute-done.18 = bf16[4,200,384]{2,1,0:T(8,128)(2,1)} collective-permute-done((bf16[4,200,384]{2,1,0:T(8,128)(2,1)}, bf16[4,200,384]{2,1,0:T(8,128)(2,1)}, u32[]{:S(2)}, u32[]{:S(2)}) %collective-permute-start.18) | collective-permute-done | bytes 614432 | tf_op jit(solution)/shard_map/ppermute | solution.py:48
  34.8 25.3 %conditional.1 = (f32[2,4,196]{2,1,0:T(4,128)S(1)}, f32[2,4,196]{2,1,0:T(4,128)}) conditional(s32[]{:T(128)} %bitcast.4, (s32[7,8]{1,0:T(8,128)S(1)}, bf16[4,200,384]{2,1,0:T(8,128)(2,1)S(1)}, bf16[4,200,384]{2,1,0:T(8,128)(2,1)}, bf16[4,200,384]{2,1,0:T(8,128)(2,1)}, bf16[4,200,384]{2,1,0:T(8,128)(2,1)}, ...), branch_computations={%region_0.1_spmd, %region_1.2_spmd, %region_2.4_spmd} | conditional | flops 23520 | bytes 13830624 | solution.py:550
  34.8 2.6 %pick.7 = bf16[4,200,384]{2,1,0:T(8,128)(2,1)S(1)} custom-call(s32[7,8]{1,0:T(8,128)S(1)} %get-tuple-element.105.table, bf16[4,200,384]{2,1,0:T(8,128)(2,1)S(1)} %get-tuple-element.106.refs_0_, bf16[4,200,384]{2,1,0:T(8,128)(2,1)} %get-tuple-element.107.refs_1_, bf16[4,200,384]{2,1,0:T(8,128)(2,1)} %get-tuple-element.108.refs_2_, ...), custom_call_target="tpu_custom_call" | custom-call | bytes 1228800 | tf_op jit(solution)/shard_map/cond/branch_0_fun/pick/pallas_call | solution.py:290
  37.4 0.1 collective-permute-start.5
  37.5 2.6 %pick.6.refs_0_ = bf16[4,200,384]{2,1,0:T(8,128)(2,1)S(1)} custom-call(s32[7,8]{1,0:T(8,128)S(1)} %get-tuple-element.105.table, bf16[4,200,384]{2,1,0:T(8,128)(2,1)S(1)} %get-tuple-element.106.refs_0_, bf16[4,200,384]{2,1,0:T(8,128)(2,1)} %get-tuple-element.107.refs_1_, bf16[4,200,384]{2,1,0:T(8,128)(2,1)} %get-tuple-element.108.refs_2_, ...), custom_call_target="tpu_custom_call" | custom-call | bytes 1228800 | tf_op jit(solution)/shard_map/cond/branch_0_fun/pick/pallas_call | solution.py:290
  40.0 0.0 collective-permute-done.5.refs_1_
  40.1 11.2 %decode.3 = (f32[12,4,196]{2,1,0:T(4,128)S(1)}, f32[8,4,196]{2,1,0:T(4,128)S(1)}) custom-call(s32[7,8]{1,0:T(8,128)S(1)} %get-tuple-element.105.table, bf16[4,200,384]{2,1,0:T(8,128)(2,1)S(1)} %pick.6.refs_0_, bf16[4,200,384]{2,1,0:T(8,128)(2,1)S(1)} %collective-permute-done.5.refs_1_, f32[1,768]{1,0:T(1,128)S(1)} %get-tuple-element.116.refs_2_, ...), custom_call_target="tpu_custom_call" | custom-call | tf_op jit(solution)/shard_map/cond/branch_0_fun/decode/pallas_call | solution.py:489
  51.2 0.5 collective-permute-start.6
  51.8 0.9 %collective-permute-done.6 = f32[8,4,196]{2,1,0:T(4,128)S(1)} collective-permute-done((f32[8,4,196]{2,1,0:T(4,128)S(1)}, f32[8,4,196]{2,1,0:T(4,128)S(1)}, u32[]{:S(2)}, u32[]{:S(2)}) %collective-permute-start.6) | collective-permute-done | bytes 25120 | tf_op jit(solution)/shard_map/cond/branch_0_fun/ppermute | solution.py:514
  52.7 1.6 %collective-permute-start.8 = (f32[4,4,196]{2,1,0:T(4,128)S(1)}, f32[4,4,196]{2,1,0:T(4,128)S(1)}, u32[]{:S(2)}, u32[]{:S(2)}) collective-permute-start(f32[4,4,196]{2,1,0:T(4,128)S(1)} %get-tuple-element.174), channel_id=1, source_target_pairs={{4,0},{9,1},{8,4},{13,5},{12,8},{15,9},{14,12},{11,13},{10,14},{7,... | collective-permute-start | bytes 37640 | tf_op jit(solution)/shard_map/cond/branch_0_fun/ppermute | solution.py:524
  54.3 0.4 collective-permute-start.7
  54.7 1.7 %collective-permute-done.8 = f32[4,4,196]{2,1,0:T(4,128)S(1)} collective-permute-done((f32[4,4,196]{2,1,0:T(4,128)S(1)}, f32[4,4,196]{2,1,0:T(4,128)S(1)}, u32[]{:S(2)}, u32[]{:S(2)}) %collective-permute-start.8) | collective-permute-done | bytes 12576 | tf_op jit(solution)/shard_map/cond/branch_0_fun/ppermute | solution.py:524
  56.5 1.6 %collective-permute-done.7 = f32[4,4,196]{2,1,0:T(4,128)S(1)} collective-permute-done((f32[4,4,196]{2,1,0:T(4,128)S(1)}, f32[4,4,196]{2,1,0:T(4,128)S(1)}, u32[]{:S(2)}, u32[]{:S(2)}) %collective-permute-start.7) | collective-permute-done | bytes 12576 | tf_op jit(solution)/shard_map/cond/branch_0_fun/ppermute | solution.py:523
  58.1 1.1 %collective-permute-start.9 = (f32[2,4,196]{2,1,0:T(4,128)S(1)}, f32[2,4,196]{2,1,0:T(4,128)}, u32[]{:S(2)}, u32[]{:S(2)}) collective-permute-start(f32[2,4,196]{2,1,0:T(4,128)S(1)} %get-tuple-element.175), channel_id=1, source_target_pairs={{0,1},{1,0},{2,3},{3,2},{4,5},{5,4},{6,7},{7,6},{8,9},{9,8},{10,11... | collective-permute-start | bytes 18824 | tf_op jit(solution)/shard_map/cond/branch_0_fun/ppermute | solution.py:527
  59.1 1.0 %collective-permute-done.9 = f32[2,4,196]{2,1,0:T(4,128)} collective-permute-done((f32[2,4,196]{2,1,0:T(4,128)S(1)}, f32[2,4,196]{2,1,0:T(4,128)}, u32[]{:S(2)}, u32[]{:S(2)}) %collective-permute-start.9) | collective-permute-done | bytes 6304 | tf_op jit(solution)/shard_map/cond/branch_0_fun/ppermute | solution.py:527
  60.1 1.3 %add.35 = f32[2,4,196]{2,1,0:T(4,128)} add(f32[2,4,196]{2,1,0:T(4,128)S(1)} %get-tuple-element.171, f32[2,4,196]{2,1,0:T(4,128)} %get-tuple-element.172) | non-fusion elementwise | flops 1568 | bytes 18816 | tf_op jit(solution)/shard_map/add | solution.py:562
  (20 shorter events, 0.1 us)
Async XLA Ops:
  0.0 20.5 %copy-start = (s32[96,1]{0,1:T(1,128)S(1)}, s32[96,1]{0,1:T(1,128)}, u32[]{:S(2)}) copy-start(s32[96,1]{0,1:T(1,128)} %param.28) | copy-start | bytes 1156
  0.0 20.5 %copy-start.1 = (s32[96]{0:T(128)S(1)}, s32[96]{0:T(128)}, u32[]{:S(2)}) copy-start(s32[96]{0:T(128)} %locals_.1) | copy-start | bytes 1156
  0.0 20.5 %copy-start.2 = (s32[8]{0:T(128)S(1)}, s32[8]{0:T(128)}, u32[]{:S(2)}) copy-start(s32[8]{0:T(128)} %counts.1) | copy-start | bytes 100
  0.0 28.7 %copy-start.5 = (f32[768]{0:T(1024)S(1)}, f32[768]{0:T(1024)}, u32[]{:S(2)}) copy-start(f32[768]{0:T(1024)} %param.18) | copy-start | bytes 9220
  0.0 28.7 %copy-start.6 = (f32[768]{0:T(1024)S(1)}, f32[768]{0:T(1024)}, u32[]{:S(2)}) copy-start(f32[768]{0:T(1024)} %param.19) | copy-start | bytes 9220
  0.0 28.7 %copy-start.7 = (f32[768]{0:T(1024)S(1)}, f32[768]{0:T(1024)}, u32[]{:S(2)}) copy-start(f32[768]{0:T(1024)} %param.24) | copy-start | bytes 9220
  1.3 17.0 %collective-permute-start.15 = (bf16[4,200,384]{2,1,0:T(8,128)(2,1)S(1)}, bf16[4,200,384]{2,1,0:T(8,128)(2,1)}, u32[]{:S(2)}, u32[]{:S(2)}) collective-permute-start(bf16[4,200,384]{2,1,0:T(8,128)(2,1)S(1)} %pad.4), channel_id=1, source_target_pairs={{4,0},{8,4},{12,8},{14,12},{10,14},{6,10},{2,6},{0,2},{5,1},{9,5},... | collective-permute-start | bytes 1843208 | tf_op jit(solution)/shard_map/ppermute | solution.py:49
  4.3 15.7 %collective-permute-start.17 = (bf16[4,200,384]{2,1,0:T(8,128)(2,1)S(1)}, bf16[4,200,384]{2,1,0:T(8,128)(2,1)}, u32[]{:S(2)}, u32[]{:S(2)}) collective-permute-start(bf16[4,200,384]{2,1,0:T(8,128)(2,1)S(1)} %pad.4), channel_id=1, source_target_pairs={{0,4},{4,8},{8,12},{12,14},{14,10},{10,6},{6,2},{2,0},{1,5},{5,9},... | collective-permute-start | bytes 1843208 | tf_op jit(solution)/shard_map/ppermute | solution.py:48
  18.4 15.4 %collective-permute-start.16 = (bf16[4,200,384]{2,1,0:T(8,128)(2,1)}, bf16[4,200,384]{2,1,0:T(8,128)(2,1)}, u32[]{:S(2)}, u32[]{:S(2)}) collective-permute-start(bf16[4,200,384]{2,1,0:T(8,128)(2,1)} %collective-permute-done.15), channel_id=1, source_target_pairs={{4,0},{8,4},{12,8},{14,12},{10,14},{6,10},{2,6},{0,2},{5,1},{9,5},... | collective-permute-start | bytes 1843208 | tf_op jit(solution)/shard_map/ppermute | solution.py:49
  20.0 14.8 %collective-permute-start.18 = (bf16[4,200,384]{2,1,0:T(8,128)(2,1)}, bf16[4,200,384]{2,1,0:T(8,128)(2,1)}, u32[]{:S(2)}, u32[]{:S(2)}) collective-permute-start(bf16[4,200,384]{2,1,0:T(8,128)(2,1)} %collective-permute-done.17), channel_id=1, source_target_pairs={{0,4},{4,8},{8,12},{12,14},{14,10},{10,6},{6,2},{2,0},{1,5},{5,9},... | collective-permute-start | bytes 1843208 | tf_op jit(solution)/shard_map/ppermute | solution.py:48
  29.4 5.4 %copy-start.3 = (bf16[4,1024]{1,0:T(4,128)(2,1)S(1)}, bf16[4,1024]{1,0:T(4,128)(2,1)}, u32[]{:S(2)}) copy-start(bf16[4,1024]{1,0:T(4,128)(2,1)} %param.27) | copy-start | bytes 24580
  29.4 5.4 %copy-start.4 = (f32[1024]{0:T(1024)S(1)}, f32[1024]{0:T(1024)}, u32[]{:S(2)}) copy-start(f32[1024]{0:T(1024)} %param.26) | copy-start | bytes 12292
  37.4 2.7 %collective-permute-start.5 = (bf16[4,200,384]{2,1,0:T(8,128)(2,1)S(1)}, bf16[4,200,384]{2,1,0:T(8,128)(2,1)S(1)}, u32[]{:S(2)}, u32[]{:S(2)}) collective-permute-start(bf16[4,200,384]{2,1,0:T(8,128)(2,1)S(1)} %pick.7), channel_id=1, source_target_pairs={{0,1},{1,0},{2,3},{3,2},{4,5},{5,4},{6,7},{7,6},{8,9},{9,8},{10,11... | collective-permute-start | bytes 1843208 | tf_op jit(solution)/shard_map/cond/branch_0_fun/ppermute | solution.py:331
  51.2 1.4 %collective-permute-start.6 = (f32[8,4,196]{2,1,0:T(4,128)S(1)}, f32[8,4,196]{2,1,0:T(4,128)S(1)}, u32[]{:S(2)}, u32[]{:S(2)}) collective-permute-start(f32[8,4,196]{2,1,0:T(4,128)S(1)} %get-tuple-element.122), channel_id=1, source_target_pairs={{0,1},{1,0},{2,3},{3,2},{4,5},{5,4},{6,7},{7,6},{8,9},{9,8},{10,11... | collective-permute-start | bytes 75272 | tf_op jit(solution)/shard_map/cond/branch_0_fun/ppermute | solution.py:514
  52.7 3.8 %collective-permute-start.8 = (f32[4,4,196]{2,1,0:T(4,128)S(1)}, f32[4,4,196]{2,1,0:T(4,128)S(1)}, u32[]{:S(2)}, u32[]{:S(2)}) collective-permute-start(f32[4,4,196]{2,1,0:T(4,128)S(1)} %get-tuple-element.174), channel_id=1, source_target_pairs={{4,0},{9,1},{8,4},{13,5},{12,8},{15,9},{14,12},{11,13},{10,14},{7,... | collective-permute-start | bytes 37640 | tf_op jit(solution)/shard_map/cond/branch_0_fun/ppermute | solution.py:524
  54.3 3.7 %collective-permute-start.7 = (f32[4,4,196]{2,1,0:T(4,128)S(1)}, f32[4,4,196]{2,1,0:T(4,128)S(1)}, u32[]{:S(2)}, u32[]{:S(2)}) collective-permute-start(f32[4,4,196]{2,1,0:T(4,128)S(1)} %get-tuple-element.173), channel_id=1, source_target_pairs={{0,4},{1,9},{4,8},{5,13},{8,12},{9,15},{12,14},{13,11},{14,10},{15... | collective-permute-start | bytes 37640 | tf_op jit(solution)/shard_map/cond/branch_0_fun/ppermute | solution.py:523
  58.1 2.0 %collective-permute-start.9 = (f32[2,4,196]{2,1,0:T(4,128)S(1)}, f32[2,4,196]{2,1,0:T(4,128)}, u32[]{:S(2)}, u32[]{:S(2)}) collective-permute-start(f32[2,4,196]{2,1,0:T(4,128)S(1)} %get-tuple-element.175), channel_id=1, source_target_pairs={{0,1},{1,0},{2,3},{3,2},{4,5},{5,4},{6,7},{7,6},{8,9},{9,8},{10,11... | collective-permute-start | bytes 18824 | tf_op jit(solution)/shard_map/cond/branch_0_fun/ppermute | solution.py:527

commit v9 on v8

--- a/solution.py
+++ b/solution.py
@@ -405,7 +405,7 @@
             att[i, :, cols] = jnp.where(low, blended[0], blended[1]).astype(BF16)
         return carry
 
-    if views == SHARE:
+    if len(outs) == 2:
         for i in range(views):
             attend(i, 0)
     else:
@@ -506,7 +506,7 @@
         (flat,) = decode(views, spots, table, parts, vectors, weights)
         arrived = lax.all_to_all(flat, ("pairs", "mp"), 0, 0, tiled=True)
         arrived = arrived.reshape(worker_count * core_count, mine, 4, token_count)
-        return jnp.sum(arrived, axis=0), jnp.zeros_like(arrived[0])
+        return jnp.sum(arrived, axis=0)
 
     def decode_near(views, table, parts, vectors, weights):
         spots = (3 * image_count, 2 * image_count)
@@ -524,7 +524,7 @@
         total = total + lax.ppermute(leaving[image_count:], axes, back)
         theirs = lax.dynamic_slice_in_dim(total, (1 - core) * mine, mine, 0)
         ours = lax.dynamic_slice_in_dim(total, core * mine, mine, 0)
-        return ours, lax.ppermute(theirs, "mp", swap)
+        return ours + lax.ppermute(theirs, "mp", swap)
 
     if worker_count == 8:
         reach = 2
@@ -547,7 +547,7 @@
         def decode_far(table, near, *rest):
             return decode_any(MOST, table, ring_far(near, worker_count, reach), *rest)
 
-        ours, theirs = lax.switch(
+        return lax.switch(
             table[LEVEL, 0],
             (
                 functools.partial(decode_near, SHARE),
@@ -559,11 +559,9 @@
             vectors,
             weights,
         )
-        return ours + theirs
     table = plan(owners, view_local, pair_count, worker, core, image_count, worker_count)
     parts = ring_far({0: shard, worker_count: shard}, worker_count, 0)
-    ours, theirs = decode_any(SHARE, table, parts, vectors, weights)
-    return ours + theirs
+    return decode_any(SHARE, table, parts, vectors, weights)
 
 
 def solution(mesh):

time: 61.6 us -> 60.8 us (0.987)
  other arithmetic: 1.39 us -> 0.1 us
    ppermute x2, waiting for transfers between devices: 15.3 us -> 1.2 us  [ring_near(): coming = lax.ppermute(coming, 'pairs', back)]
    ppermute x2, waiting for transfers between devices: 1.09 us -> 15 us  [ring_near(): going = lax.ppermute(going, 'pairs', ahead)]
    ppermute x2, starting transfers between devices: 4.7 us -> 0.24 us  [ring_near(): coming = lax.ppermute(coming, 'pairs', back)]
    ppermute x2, starting transfers between devices: 0.47 us -> 4.87 us  [ring_near(): going = lax.ppermute(going, 'pairs', ahead)]
    add x1, other arithmetic: 1.3 us -> 0.01 us  [decode_near(): return ours + lax.ppermute(theirs, 'mp', swap)]
    ppermute x1, starting transfers between devices: 0.44 us -> 1.63 us  [decode_near(): lax.ppermute(leaving[:image_count], axes, ahead)]
    ppermute x1, starting transfers between devices: 1.64 us -> 0.45 us  [decode_near(): total = total + lax.ppermute(leaving[image_count:], axes, back)]
    unnamed x17 -> x19, local copies, waits for them, and re-layouts: 1.25 us -> 1.85 us
  transfers between devices with their start and end apart: 9 -> 9, of which waited for: 7 -> 7; matrix products, arithmetic and copies ran while one was open for 1% -> 1% of each run, Pallas kernels for 21% -> 22%
where the time goes in v9:
time: 60.8 us; the launch traced here: 60.6 us
  Pallas kernels  27 us (44%)
  waiting for transfers between devices  21.4 us (35%)
  starting transfers between devices  8.71 us (14%)
  local copies, waits for them, and re-layouts  2.53 us (4%)
  between operations  0.79 us (1%)
    ppermute x2, waiting for transfers between devices, ring_near(): going = lax.ppermute(going, 'pairs', ahead)  15 us
    pallas_call x1, Pallas kernels, decode(): pl.pallas_call(functools.partial(decode_kernel, token_count), out_shape=t...  11.2 us
    pallas_call x1, Pallas kernels, per_device(): pl.pallas_call(functools.partial(deal_kernel, worker_count, image_count,...  7.82 us
    pallas_call x2, Pallas kernels, pick(): pl.pallas_call(functools.partial(pick_kernel, keys, first_column), out_sh...  5.14 us
    ppermute x2, starting transfers between devices, ring_near(): going = lax.ppermute(going, 'pairs', ahead)  4.87 us
    pallas_call x1, Pallas kernels, stage(): pl.pallas_call(functools.partial(stage_kernel, count), out_shape=tuple((j...  2.89 us
    unnamed x19, local copies, waits for them, and re-layouts  1.85 us
    ppermute x1, waiting for transfers between devices, decode_near(): total = total + lax.ppermute(leaving[image_count:], axes, back)  1.75 us
  transfers between devices with their start and end apart: 9, of which 7 were waited for; matrix products, arithmetic and copies ran while one was open for 1% of the time, Pallas kernels for 22%

profile of v9, /device:TPU:0, one launch (start us, length us, event | category | flops | bytes accessed | tf_op | source)
XLA Modules:
  0.0 60.6 jit_solution(5924348754886145687)
XLA Ops:
  0.0 0.0 copy-start
  0.0 1.2 %copy.18 = bf16[4,196,384]{2,1,0:T(8,128)(2,1)S(1)} copy(bf16[4,196,384]{2,0,1:T(4,128)(2,1)} %param.17) | data formatting | bytes 1204224 | tf_op args[0]
  1.2 0.1 pad.4
  1.3 3.1 %collective-permute-start.17 = (bf16[4,200,384]{2,1,0:T(8,128)(2,1)S(1)}, bf16[4,200,384]{2,1,0:T(8,128)(2,1)}, u32[]{:S(2)}, u32[]{:S(2)}) collective-permute-start(bf16[4,200,384]{2,1,0:T(8,128)(2,1)S(1)} %pad.4), channel_id=1, source_target_pairs={{0,4},{4,8},{8,12},{12,14},{14,10},{10,6},{6,2},{2,0},{1,5},{5,9},... | collective-permute-start | bytes 1843208 | tf_op jit(solution)/shard_map/ppermute | solution.py:48
  4.4 0.0 collective-permute-start.15
  4.4 13.9 %collective-permute-done.17 = bf16[4,200,384]{2,1,0:T(8,128)(2,1)} collective-permute-done((bf16[4,200,384]{2,1,0:T(8,128)(2,1)S(1)}, bf16[4,200,384]{2,1,0:T(8,128)(2,1)}, u32[]{:S(2)}, u32[]{:S(2)}) %collective-permute-start.17) | collective-permute-done | bytes 614432 | tf_op jit(solution)/shard_map/ppermute | solution.py:48
  18.3 1.8 %collective-permute-start.18 = (bf16[4,200,384]{2,1,0:T(8,128)(2,1)}, bf16[4,200,384]{2,1,0:T(8,128)(2,1)}, u32[]{:S(2)}, u32[]{:S(2)}) collective-permute-start(bf16[4,200,384]{2,1,0:T(8,128)(2,1)} %collective-permute-done.17), channel_id=1, source_target_pairs={{0,4},{4,8},{8,12},{12,14},{14,10},{10,6},{6,2},{2,0},{1,5},{5,9},... | collective-permute-start | bytes 1843208 | tf_op jit(solution)/shard_map/ppermute | solution.py:48
  20.1 0.0 collective-permute-done.15
  20.1 0.2 collective-permute-start.16
  20.4 0.1 pad_add_fusion.me
  20.5 7.8 %deal.1 = s32[7,8]{1,0:T(8,128)S(1)} custom-call(s32[96]{0:T(128)S(1)} %bitcast.6, s32[96]{0:T(128)S(1)} %copy-done.1, s32[8]{0:T(128)S(1)} %copy-done.2, s32[2]{0:T(128)S(1)} %pad_add_fusion.me), custom_call_target="tpu_custom_call" | custom-call | bytes 20000000 | tf_op jit(solution)/shard_map/deal/pallas_call | solution.py:532
  28.3 0.6 slice.33
  29.6 0.0 copy-start.3
  29.6 0.0 copy-start.4
  29.6 2.9 %stage.1 = (bf16[768,768]{1,0:T(8,128)(2,1)S(1)}, bf16[768,768]{1,0:T(8,128)(2,1)S(1)}, bf16[768,768]{1,0:T(8,128)(2,1)S(1)}, bf16[768,768]{1,0:T(8,128)(2,1)S(1)}, bf16[768,1024]{1,0:T(8,128)(2,1)S(1)}) custom-call(bf16[768,768]{1,0:T(8,128)(2,1)} %refs_0_.1, bf16[768,768]{1,0:T(8,128)(2,1)} %refs_1_.1, bf16[768,768]{1,0:T(8,128)(2,1)} %refs_2_.1, ...), custom_call_target="tpu_custom_call" | custom-call | bytes 12582912 | tf_op jit(solution)/shard_map/stage/pallas_call | solution.py:318
  32.5 1.2 %collective-permute-done.18 = bf16[4,200,384]{2,1,0:T(8,128)(2,1)} collective-permute-done((bf16[4,200,384]{2,1,0:T(8,128)(2,1)}, bf16[4,200,384]{2,1,0:T(8,128)(2,1)}, u32[]{:S(2)}, u32[]{:S(2)}) %collective-permute-start.18) | collective-permute-done | bytes 614432 | tf_op jit(solution)/shard_map/ppermute | solution.py:48
  33.7 1.2 %collective-permute-done.16 = bf16[4,200,384]{2,1,0:T(8,128)(2,1)} collective-permute-done((bf16[4,200,384]{2,1,0:T(8,128)(2,1)}, bf16[4,200,384]{2,1,0:T(8,128)(2,1)}, u32[]{:S(2)}, u32[]{:S(2)}) %collective-permute-start.16) | collective-permute-done | bytes 614432 | tf_op jit(solution)/shard_map/ppermute | solution.py:49
  34.9 25.2 %conditional.1 = (f32[2,4,196]{2,1,0:T(4,128)S(1)}) conditional(s32[]{:T(128)} %bitcast.4, (s32[7,8]{1,0:T(8,128)S(1)}, bf16[4,200,384]{2,1,0:T(8,128)(2,1)S(1)}, bf16[4,200,384]{2,1,0:T(8,128)(2,1)}, bf16[4,200,384]{2,1,0:T(8,128)(2,1)}, bf16[4,200,384]{2,1,0:T(8,128)(2,1)}, /*index=5*/bf16[4,200,384]{2,1,0:T(8,128)(2,1)}, ...), branch_computations={%region_0.1_spmd, %region_1.2_spmd, %region_2.4_spmd} | conditional | flops 23520 | bytes 13824340 | solution.py:550
  34.9 2.6 %pick.7 = bf16[4,200,384]{2,1,0:T(8,128)(2,1)S(1)} custom-call(s32[7,8]{1,0:T(8,128)S(1)} %get-tuple-element.108.table, bf16[4,200,384]{2,1,0:T(8,128)(2,1)S(1)} %get-tuple-element.110.refs_0_, bf16[4,200,384]{2,1,0:T(8,128)(2,1)} %get-tuple-element.111.refs_1_, bf16[4,200,384]{2,1,0:T(8,128)(2,1)} %get-tuple-element.112.refs_2_, ...), custom_call_target="tpu_custom_call" | custom-call | bytes 1228800 | tf_op jit(solution)/shard_map/cond/branch_0_fun/pick/pallas_call | solution.py:290
  37.4 0.1 collective-permute-start.5
  37.5 2.6 %pick.6.refs_0_ = bf16[4,200,384]{2,1,0:T(8,128)(2,1)S(1)} custom-call(s32[7,8]{1,0:T(8,128)S(1)} %get-tuple-element.108.table, bf16[4,200,384]{2,1,0:T(8,128)(2,1)S(1)} %get-tuple-element.110.refs_0_, bf16[4,200,384]{2,1,0:T(8,128)(2,1)} %get-tuple-element.111.refs_1_, bf16[4,200,384]{2,1,0:T(8,128)(2,1)} %get-tuple-element.112.refs_2_, ...), custom_call_target="tpu_custom_call" | custom-call | bytes 1228800 | tf_op jit(solution)/shard_map/cond/branch_0_fun/pick/pallas_call | solution.py:290
  40.1 0.0 collective-permute-done.5.refs_1_
  40.1 11.2 %decode.3 = (f32[12,4,196]{2,1,0:T(4,128)S(1)}, f32[8,4,196]{2,1,0:T(4,128)S(1)}) custom-call(s32[7,8]{1,0:T(8,128)S(1)} %get-tuple-element.108.table, bf16[4,200,384]{2,1,0:T(8,128)(2,1)S(1)} %pick.6.refs_0_, bf16[4,200,384]{2,1,0:T(8,128)(2,1)S(1)} %collective-permute-done.5.refs_1_, f32[1,768]{1,0:T(1,128)S(1)} %get-tuple-element.120.refs_2_, ...), custom_call_target="tpu_custom_call" | custom-call | tf_op jit(solution)/shard_map/cond/branch_0_fun/decode/pallas_call | solution.py:489
  51.3 0.6 collective-permute-start.6
  51.9 0.9 %collective-permute-done.6 = f32[8,4,196]{2,1,0:T(4,128)S(1)} collective-permute-done((f32[8,4,196]{2,1,0:T(4,128)S(1)}, f32[8,4,196]{2,1,0:T(4,128)S(1)}, u32[]{:S(2)}, u32[]{:S(2)}) %collective-permute-start.6) | collective-permute-done | bytes 25120 | tf_op jit(solution)/shard_map/cond/branch_0_fun/ppermute | solution.py:514
  52.7 1.6 %collective-permute-start.7 = (f32[4,4,196]{2,1,0:T(4,128)S(1)}, f32[4,4,196]{2,1,0:T(4,128)S(1)}, u32[]{:S(2)}, u32[]{:S(2)}) collective-permute-start(f32[4,4,196]{2,1,0:T(4,128)S(1)} %get-tuple-element.174), channel_id=1, source_target_pairs={{0,4},{1,9},{4,8},{5,13},{8,12},{9,15},{12,14},{13,11},{14,10},{15... | collective-permute-start | bytes 37640 | tf_op jit(solution)/shard_map/cond/branch_0_fun/ppermute | solution.py:523
  54.4 0.4 collective-permute-start.8
  54.8 1.7 %collective-permute-done.7 = f32[4,4,196]{2,1,0:T(4,128)S(1)} collective-permute-done((f32[4,4,196]{2,1,0:T(4,128)S(1)}, f32[4,4,196]{2,1,0:T(4,128)S(1)}, u32[]{:S(2)}, u32[]{:S(2)}) %collective-permute-start.7) | collective-permute-done | bytes 12576 | tf_op jit(solution)/shard_map/cond/branch_0_fun/ppermute | solution.py:523
  56.5 1.8 %collective-permute-done.8 = f32[4,4,196]{2,1,0:T(4,128)S(1)} collective-permute-done((f32[4,4,196]{2,1,0:T(4,128)S(1)}, f32[4,4,196]{2,1,0:T(4,128)S(1)}, u32[]{:S(2)}, u32[]{:S(2)}) %collective-permute-start.8) | collective-permute-done | bytes 12576 | tf_op jit(solution)/shard_map/cond/branch_0_fun/ppermute | solution.py:524
  58.3 0.9 %collective-permute-start.9 = (f32[2,4,196]{2,1,0:T(4,128)S(1)}, f32[2,4,196]{2,1,0:T(4,128)S(1)}, u32[]{:S(2)}, u32[]{:S(2)}) collective-permute-start(f32[2,4,196]{2,1,0:T(4,128)S(1)} %constant_dynamic-slice_fusion), channel_id=1, source_target_pairs={{0,1},{1,0},{2,3},{3,2},{4,5},{5,4},{6,7},{7,6},{8,9},{9,8},{10,11... | collective-permute-start | bytes 18824 | tf_op jit(solution)/shard_map/cond/branch_0_fun/ppermute | solution.py:527
  59.2 0.8 %collective-permute-done.9 = f32[2,4,196]{2,1,0:T(4,128)S(1)} collective-permute-done((f32[2,4,196]{2,1,0:T(4,128)S(1)}, f32[2,4,196]{2,1,0:T(4,128)S(1)}, u32[]{:S(2)}, u32[]{:S(2)}) %collective-permute-start.9) | collective-permute-done | bytes 6304 | tf_op jit(solution)/shard_map/cond/branch_0_fun/ppermute | solution.py:527
  60.0 0.6 copy-done.5
  (22 shorter events, 0.1 us)
Async XLA Ops:
  0.0 20.3 %copy-start.6 = (f32[768]{0:T(1024)S(1)}, f32[768]{0:T(1024)}, u32[]{:S(2)}) copy-start(f32[768]{0:T(1024)} %param.18) | copy-start | bytes 9220
  0.0 20.3 %copy-start.7 = (f32[768]{0:T(1024)S(1)}, f32[768]{0:T(1024)}, u32[]{:S(2)}) copy-start(f32[768]{0:T(1024)} %param.19) | copy-start | bytes 9220
  0.0 20.3 %copy-start.8 = (f32[768]{0:T(1024)S(1)}, f32[768]{0:T(1024)}, u32[]{:S(2)}) copy-start(f32[768]{0:T(1024)} %param.24) | copy-start | bytes 9220
  0.0 20.4 %copy-start.2 = (s32[8]{0:T(128)S(1)}, s32[8]{0:T(128)}, u32[]{:S(2)}) copy-start(s32[8]{0:T(128)} %counts.1) | copy-start | bytes 100
  0.0 20.4 %copy-start.1 = (s32[96]{0:T(128)S(1)}, s32[96]{0:T(128)}, u32[]{:S(2)}) copy-start(s32[96]{0:T(128)} %locals_.1) | copy-start | bytes 1156
  0.0 20.4 %copy-start = (s32[96,1]{0,1:T(1,128)S(1)}, s32[96,1]{0,1:T(1,128)}, u32[]{:S(2)}) copy-start(s32[96,1]{0,1:T(1,128)} %param.28) | copy-start | bytes 1156
  1.3 17.0 %collective-permute-start.17 = (bf16[4,200,384]{2,1,0:T(8,128)(2,1)S(1)}, bf16[4,200,384]{2,1,0:T(8,128)(2,1)}, u32[]{:S(2)}, u32[]{:S(2)}) collective-permute-start(bf16[4,200,384]{2,1,0:T(8,128)(2,1)S(1)} %pad.4), channel_id=1, source_target_pairs={{0,4},{4,8},{8,12},{12,14},{14,10},{10,6},{6,2},{2,0},{1,5},{5,9},... | collective-permute-start | bytes 1843208 | tf_op jit(solution)/shard_map/ppermute | solution.py:48
  4.4 15.7 %collective-permute-start.15 = (bf16[4,200,384]{2,1,0:T(8,128)(2,1)S(1)}, bf16[4,200,384]{2,1,0:T(8,128)(2,1)}, u32[]{:S(2)}, u32[]{:S(2)}) collective-permute-start(bf16[4,200,384]{2,1,0:T(8,128)(2,1)S(1)} %pad.4), channel_id=1, source_target_pairs={{4,0},{8,4},{12,8},{14,12},{10,14},{6,10},{2,6},{0,2},{5,1},{9,5},... | collective-permute-start | bytes 1843208 | tf_op jit(solution)/shard_map/ppermute | solution.py:49
  18.3 15.4 %collective-permute-start.18 = (bf16[4,200,384]{2,1,0:T(8,128)(2,1)}, bf16[4,200,384]{2,1,0:T(8,128)(2,1)}, u32[]{:S(2)}, u32[]{:S(2)}) collective-permute-start(bf16[4,200,384]{2,1,0:T(8,128)(2,1)} %collective-permute-done.17), channel_id=1, source_target_pairs={{0,4},{4,8},{8,12},{12,14},{14,10},{10,6},{6,2},{2,0},{1,5},{5,9},... | collective-permute-start | bytes 1843208 | tf_op jit(solution)/shard_map/ppermute | solution.py:48
  20.1 14.8 %collective-permute-start.16 = (bf16[4,200,384]{2,1,0:T(8,128)(2,1)}, bf16[4,200,384]{2,1,0:T(8,128)(2,1)}, u32[]{:S(2)}, u32[]{:S(2)}) collective-permute-start(bf16[4,200,384]{2,1,0:T(8,128)(2,1)} %collective-permute-done.15), channel_id=1, source_target_pairs={{4,0},{8,4},{12,8},{14,12},{10,14},{6,10},{2,6},{0,2},{5,1},{9,5},... | collective-permute-start | bytes 1843208 | tf_op jit(solution)/shard_map/ppermute | solution.py:49
  29.6 5.3 %copy-start.3 = (bf16[4,1024]{1,0:T(4,128)(2,1)S(1)}, bf16[4,1024]{1,0:T(4,128)(2,1)}, u32[]{:S(2)}) copy-start(bf16[4,1024]{1,0:T(4,128)(2,1)} %param.27) | copy-start | bytes 24580
  29.6 5.3 %copy-start.4 = (f32[1024]{0:T(1024)S(1)}, f32[1024]{0:T(1024)}, u32[]{:S(2)}) copy-start(f32[1024]{0:T(1024)} %param.26) | copy-start | bytes 12292
  37.4 2.7 %collective-permute-start.5 = (bf16[4,200,384]{2,1,0:T(8,128)(2,1)S(1)}, bf16[4,200,384]{2,1,0:T(8,128)(2,1)S(1)}, u32[]{:S(2)}, u32[]{:S(2)}) collective-permute-start(bf16[4,200,384]{2,1,0:T(8,128)(2,1)S(1)} %pick.7), channel_id=1, source_target_pairs={{0,1},{1,0},{2,3},{3,2},{4,5},{5,4},{6,7},{7,6},{8,9},{9,8},{10,11... | collective-permute-start | bytes 1843208 | tf_op jit(solution)/shard_map/cond/branch_0_fun/ppermute | solution.py:331
  51.3 1.4 %collective-permute-start.6 = (f32[8,4,196]{2,1,0:T(4,128)S(1)}, f32[8,4,196]{2,1,0:T(4,128)S(1)}, u32[]{:S(2)}, u32[]{:S(2)}) collective-permute-start(f32[8,4,196]{2,1,0:T(4,128)S(1)} %get-tuple-element.126), channel_id=1, source_target_pairs={{0,1},{1,0},{2,3},{3,2},{4,5},{5,4},{6,7},{7,6},{8,9},{9,8},{10,11... | collective-permute-start | bytes 75272 | tf_op jit(solution)/shard_map/cond/branch_0_fun/ppermute | solution.py:514
  52.7 3.8 %collective-permute-start.7 = (f32[4,4,196]{2,1,0:T(4,128)S(1)}, f32[4,4,196]{2,1,0:T(4,128)S(1)}, u32[]{:S(2)}, u32[]{:S(2)}) collective-permute-start(f32[4,4,196]{2,1,0:T(4,128)S(1)} %get-tuple-element.174), channel_id=1, source_target_pairs={{0,4},{1,9},{4,8},{5,13},{8,12},{9,15},{12,14},{13,11},{14,10},{15... | collective-permute-start | bytes 37640 | tf_op jit(solution)/shard_map/cond/branch_0_fun/ppermute | solution.py:523
  54.4 3.9 %collective-permute-start.8 = (f32[4,4,196]{2,1,0:T(4,128)S(1)}, f32[4,4,196]{2,1,0:T(4,128)S(1)}, u32[]{:S(2)}, u32[]{:S(2)}) collective-permute-start(f32[4,4,196]{2,1,0:T(4,128)S(1)} %get-tuple-element.175), channel_id=1, source_target_pairs={{4,0},{9,1},{8,4},{13,5},{12,8},{15,9},{14,12},{11,13},{10,14},{7,... | collective-permute-start | bytes 37640 | tf_op jit(solution)/shard_map/cond/branch_0_fun/ppermute | solution.py:524
  58.3 1.7 %collective-permute-start.9 = (f32[2,4,196]{2,1,0:T(4,128)S(1)}, f32[2,4,196]{2,1,0:T(4,128)S(1)}, u32[]{:S(2)}, u32[]{:S(2)}) collective-permute-start(f32[2,4,196]{2,1,0:T(4,128)S(1)} %constant_dynamic-slice_fusion), channel_id=1, source_target_pairs={{0,1},{1,0},{2,3},{3,2},{4,5},{5,4},{6,7},{7,6},{8,9},{9,8},{10,11... | collective-permute-start | bytes 18824 | tf_op jit(solution)/shard_map/cond/branch_0_fun/ppermute | solution.py:527
  60.0 0.6 copy-start.5
